TPU v7x, 128 devices: a whole 4x4x4 slice. The times are simulated.
128 devices in a mesh: sect: 4 (over x), space: 32 (over z, y, core).
Axes of the slice: x: 4, y: 4, z: 4, core: 2. Of those that a mesh axis runs over, the one named last changes fastest.
Arguments:
- dist: bfloat16 [8000, 65536], P('sect', 'space'), may hold values from 0.25 to 4
- velocity: float32 [3, 8000], P(None, 'sect'), may hold values from -1.5 to 1.5
- quad_weight: float32 [8000], P('sect'), may hold values from 0.5 to 2
- collision_rate: float32 [65536], P('space'), may hold values from 0.1 to 0.9
- ghost_source: int32 [8192], P('space'), may hold values from 0 to 2047
- ghost_owner: int32 [8192, 1], P('space'), may hold values from 0 to 31; in each aligned block of 256 rows (0 to 255, 256 to 511, ...) at most 16 rows name the same one
- wall_cell: int32 [32, 32, 16], P('space'), may hold values from 0 to 2047
- plenum_moments: float32 [16384, 20], P('space'), may hold values from -6 to 6
- iface_cell: int32 [16384], P('space'), may hold values from 0 to 65535, as said below
Outputs:
- relaxed: bfloat16 [8000, 65536], P('sect', 'space')
Inputs may be any that keep to these rules, and one draw needn't show every extreme that they name: `ghost_owner`: in the rows of one slab no owner is named more than 16 times, a bound that some block reaches. `iface_cell`: distinct gap cells.
All inputs are finite; a program needn't handle non-finite values.
Results may differ from a plain program's by a relative error of at most 0.0065.
Values may be sent and summed in bfloat16 or wider, within the bound.
A program may use at most 192 MiB of HBM per device.

v0:
```python
import jax
import jax.numpy as jnp
from jax import lax
from jax.sharding import PartitionSpec as P

NV = 8000
MOMENTS = 20


COURANT_SCALE = 0.6
ES_SHIFT = -0.5
WALL_SHARE = 0.5
ORDER_TWO = ((0, 0), (1, 1), (2, 2), (0, 1), (0, 2), (1, 2))
ORDER_THREE = (
    (0, 0, 0),
    (1, 1, 1),
    (2, 2, 2),
    (0, 0, 1),
    (0, 0, 2),
    (1, 1, 0),
    (1, 1, 2),
    (2, 2, 0),
    (2, 2, 1),
    (0, 1, 2),
)
RECON_NORMS = (
    1.0,
    1.0,
    1.0,
    1.0,
    2.0,
    2.0,
    2.0,
    1.0,
    1.0,
    1.0,
    6.0,
    6.0,
    6.0,
    2.0,
    2.0,
    2.0,
    2.0,
    2.0,
    2.0,
    1.0,
)


def with_halo(shard, sides, width):
    for axis, dim in sides:
        count, length = (lax.axis_size(axis), shard.shape[dim])
        up = [(i, (i + 1) % count) for i in range(count - 1)]
        down = [(j, i) for i, j in up]
        last = lax.slice_in_dim(shard, length - width, length, axis=dim)
        first = lax.slice_in_dim(shard, 0, width, axis=dim)
        before = lax.ppermute(last, axis, up)
        after = lax.ppermute(first, axis, down)
        shard = jnp.concatenate([before, shard, after], axis=dim)
    return shard


def hermite(velocity):
    unity_row = jnp.ones_like(velocity[0])
    stacked = [unity_row, velocity[0], velocity[1], velocity[2]]
    for i, j in ORDER_TWO:
        element = velocity[i] * velocity[j]
        if i == j:
            element = element - 1.0
        stacked.append(element)
    for i, j, k in ORDER_THREE:
        element = velocity[i] * velocity[j] * velocity[k]
        if i == j:
            element = element - velocity[k]
        if i == k:
            element = element - velocity[j]
        if j == k:
            element = element - velocity[i]
        stacked.append(element)
    return jnp.stack(stacked)


def moment_basis(velocity, weight):
    return (hermite(velocity) * (weight / NV)[None, :]).astype(jnp.bfloat16)


def recon_basis(velocity):
    norms = jnp.array(RECON_NORMS, dtype=jnp.float32)
    return (hermite(velocity) / norms[:, None]).T.astype(jnp.bfloat16)


def transport(padded, courant):
    left = padded[:, :-2].astype(jnp.float32)
    centre = padded[:, 1:-1].astype(jnp.float32)
    right = padded[:, 2:].astype(jnp.float32)
    ahead = jnp.maximum(courant, 0.0)
    behind = jnp.minimum(courant, 0.0)
    return (centre - ahead * (centre - left) - behind * (right - centre)).astype(jnp.bfloat16)


def es_targets(moments):
    density = moments[0]
    moving = [moments[1], moments[2], moments[3]]
    trace_sum = moments[4] + moments[5] + moments[6]
    second = [[None, None, None], [None, None, None], [None, None, None]]
    for n, (i, j) in enumerate(ORDER_TWO):
        element = (1.0 - ES_SHIFT) * moments[4 + n]
        if i == j:
            element = element + ES_SHIFT * trace_sum / 3.0
        second[i][j] = element
        second[j][i] = element
    stacked = [density] + moving + [second[i][j] for i, j in ORDER_TWO]
    for n, (i, j, k) in enumerate(ORDER_THREE):
        stacked.append(
            0.5 * moments[10 + n]
            + (moving[i] * second[j][k] + moving[j] * second[i][k] + moving[k] * second[i][j])
            / density
        )
    return jnp.stack(stacked)


def slot_places(owner, peers, capacity):
    marks = (owner[:, None] == jnp.arange(peers, dtype=jnp.int32)[None, :]).astype(jnp.int32)
    before = jnp.cumsum(marks, axis=0) - marks
    slot = jnp.sum(marks * before, axis=1)
    return owner * capacity + slot


def add_block(carry, rows, cells, base, width):
    summed, hit = carry
    local = cells - base
    onehot = (local[:, None] == jnp.arange(width, dtype=jnp.int32)[None, :]).astype(jnp.float32)
    summed = summed + jnp.einsum("ka,kc->ac", rows, onehot, precision=lax.Precision.HIGHEST)
    hit = hit + jnp.sum(onehot, axis=0)
    return (summed, hit)


def fold_rows(carry, pieces, base, width):
    rows, cells = pieces
    count = rows.shape[0]
    blocks = (rows.reshape(count // 512, 512, rows.shape[1]), cells.reshape(count // 512, 512))

    def advance(inner, items):
        return (add_block(inner, items[0], items[1], base, width), None)

    carry, unused = lax.scan(advance, carry, blocks)
    return carry


def inject(closure, plenum_moments, iface_cell, base):
    width = closure.shape[1]
    start_state = (jnp.zeros((MOMENTS, width), jnp.float32), jnp.zeros((width,), jnp.float32))
    fluid, hit = fold_rows(
        start_state,
        (
            lax.all_gather(plenum_moments.astype(jnp.bfloat16), "space", axis=0, tiled=True).astype(
                jnp.float32
            ),
            lax.all_gather(iface_cell, "space", axis=0, tiled=True),
        ),
        base,
        width,
    )
    return closure + hit[None, :] * (fluid - closure)


def per_device(
    dist,
    velocity,
    quad_weight,
    collision_rate,
    ghost_source,
    ghost_owner,
    wall_cell,
    plenum_moments,
    iface_cell,
):
    cells = dist.shape[1]
    courant = (COURANT_SCALE * velocity[0])[:, None]
    padded = with_halo(dist, (("space", 1),), 1)
    read = transport(padded, courant)
    partial_moments = jnp.dot(
        moment_basis(velocity, quad_weight), read, preferred_element_type=jnp.float32
    )
    slab_base = lax.axis_index("space") * cells
    moments = lax.psum(partial_moments, "sect")
    targets = inject(es_targets(moments), plenum_moments, iface_cell, slab_base).astype(
        jnp.bfloat16
    )
    recon = recon_basis(velocity)
    equilibrium = jnp.dot(recon, targets, preferred_element_type=jnp.float32)
    peers = lax.axis_size("space")
    capacity = wall_cell.shape[2]
    slots = peers * capacity
    places = slot_places(ghost_owner[:, 0], peers, capacity)
    walls = wall_cell.reshape(slots)
    picked = jnp.take(equilibrium, ghost_source, axis=1)
    outgoing = jnp.zeros((picked.shape[0], slots), jnp.float32).at[:, places].set(picked)
    arrived = lax.all_to_all(outgoing, "space", split_axis=1, concat_axis=1, tiled=True)
    wall_sum = jnp.zeros((picked.shape[0], cells), jnp.float32).at[:, walls].add(arrived)
    rate = collision_rate[None, :]
    current = read.astype(jnp.float32)
    return (current + rate * (equilibrium - current) + WALL_SHARE * wall_sum).astype(jnp.bfloat16)


def solution(mesh):
    in_specs = (
        P("sect", "space"),
        P(None, "sect"),
        P("sect"),
        P("space"),
        P("space"),
        P("space", None),
        P("space", None, None),
        P("space", None),
        P("space"),
    )
    out_specs = P("sect", "space")
    return jax.shard_map(
        per_device, mesh=mesh, in_specs=in_specs, out_specs=out_specs, check_vma=False
    )
```

profile of v0, /device:TPU:1, one launch (start us, length us, event | category | flops | bytes accessed | tf_op | source)
XLA Modules:
  0.0 424.3 jit_solution(15446391911328866115)
XLA Ops:
  8.0 4.6 %collective-permute-start = (bf16[2000,1]{1,0:T(8,128)(2,1)S(1)}, bf16[2000,1]{1,0:T(8,128)(2,1)S(1)}, u32[]{:S(2)}, u32[]{:S(2)}) collective-permute-start(bf16[2000,1]{1,0:T(8,128)(2,1)S(1)} %get-tuple-element.100), channel_id=1, source_target_pairs={{0,1},{1,2},{2,3},{3,4},{4,5},{5,6},{6,7},{7,8},{8,9},{9,10},{10,1... | collective-permute-start | bytes 12008 | tf_op jit(solution)/shard_map/ppermute | solution.py:57
  12.6 1.9 collective-permute-start.1
  23.2 27.7 %all-gather = s32[32,1,512]{2,1,0:T(1,128)S(1)} all-gather(s32[1,1,512]{2,1,0:T(1,128)} %bitcast.62), channel_id=1, replica_groups=mesh['sect'=4,'space'=32] {'space'}, dimensions={0}, use_global_device_ids=true | all-gather | bytes 67584 | tf_op jit(solution)/shard_map/all_gather | solution.py:159
  50.9 22.7 %all_gather.6 = bf16[16384,20]{0,1:T(8,128)(2,1)S(1)} all-gather(bf16[512,20]{0,1:T(8,128)(2,1)S(1)} %convert_element_type.49), channel_id=1, replica_groups=mesh['sect'=4,'space'=32] {'space'}, dimensions={0}, use_global_device_ids=true | all-gather | bytes 675840 | tf_op jit(solution)/shard_map/all_gather | solution.py:156
  74.8 118.8 %while.13 = (s32[]{:T(128)}, f32[20,2048]{1,0:T(8,128)}, f32[2048]{0:T(1024)S(1)}, f32[32,512,20]{1,0,2:T(8,128)S(1)}, s32[32,512]{1,0:T(8,128)S(1)}, /*index=5*/s32[]{:T(128)}, s32[]{:T(128)}, s32[]{:T(128)}) while((s32[]{:T(128)}, f32[20,2048]{1,0:T(8,128)}, f32[2048]{0:T(1024)S(1)}, f32[32,512,20]{1,0,2:T(8,128)S(1)}, ...), condition=%wide.region_3.4_spmd.clone, body=%wide.region_1.3_spmd.clone.sunk | while | flops 255937024 | bytes 491636 | solution.py:146
  75.6 2.2 fusion.49
  78.5 3.1 fusion.49
  82.2 3.1 fusion.49
  85.9 3.1 fusion.49
  89.7 3.1 fusion.49
  93.4 3.1 fusion.49
  97.1 3.1 fusion.49
  100.9 3.1 fusion.49
  104.6 3.1 fusion.49
  108.3 3.1 fusion.49
  112.1 3.1 fusion.49
  115.8 3.1 fusion.49
  119.5 3.1 fusion.49
  123.3 3.1 fusion.49
  127.0 3.1 fusion.49
  130.8 3.1 fusion.49
  134.5 3.1 fusion.49
  138.2 3.1 fusion.49
  142.0 3.1 fusion.49
  145.7 3.1 fusion.49
  149.4 3.1 fusion.49
  153.2 3.1 fusion.49
  156.9 3.1 fusion.49
  160.6 3.1 fusion.49
  164.4 3.1 fusion.49
  168.1 3.1 fusion.49
  171.9 3.1 fusion.49
  175.6 3.1 fusion.49
  179.3 3.1 fusion.49
  183.1 3.1 fusion.49
  186.8 3.1 fusion.49
  190.5 3.1 fusion.49
  194.3 2.4 stack.6
  196.8 17.9 %fusion.17 = f32[20,2048]{1,0:T(8,128)} fusion(f32[20,2000]{1,0:T(8,128)S(1)} %stack.6, f32[2000]{0:T(1024)} %broadcast_multiply_fusion, bf16[2000,2048]{1,0:T(8,128)(2,1)} %param.12, bf16[2000,1]{1,0:T(8,128)(2,1)S(1)} %collective-permute-done.1, bf16[2000,1]{1,0:T(8,128)(2,1)S(1)} %collective-permute-done, f32[2000]{0:T(1024)S(1)} %bitcast.57, ...), kind=kOutput, calls=%fused_computation.37 | convolution fusion | flops 229456000 | bytes 8547840 | tf_op jit(solution)/shard_map/dot_general | solution.py:182
  214.8 38.0 %all-reduce.2.cloned.1.call-done = f32[20,2048]{1,0:T(8,128)} async-done(((f32[20,2048]{1,0:T(8,128)}), f32[20,2048]{1,0:T(8,128)}) %all-reduce.2.cloned.1.call-update) | async-done | bytes 163856 | tf_op jit(solution)/shard_map/psum | solution.py:186
  258.9 8.1 %fusion.18 = f32[2000,2048]{1,0:T(8,128)} fusion(f32[20,2048]{1,0:T(8,128)S(1)} %stack.7, f32[20,2048]{1,0:T(8,128)S(1)} %copy-done.1, f32[20,2000]{1,0:T(8,128)S(1)} %stack.6, f32[20]{0:T(128)S(1)} %copy-done.4, f32[2048]{0:T(1024)S(1)} %get-tuple-element.38), kind=kOutput, calls=%fused_computation.38 | convolution fusion | flops 164083840 | bytes 16879952 | tf_op jit(solution)/shard_map/dot_general | solution.py:191
  266.9 17.6 %copy.30 = f32[2000,2048]{0,1:T(8,128)} copy(f32[2000,2048]{1,0:T(8,128)} %fusion.18) | data formatting | bytes 32768000 | tf_op jit(solution)/shard_map/dot_general | solution.py:191
  284.5 8.0 %scatter_custom_fusion = f32[2000,512]{0,1:T(8,128)} fusion(s32[256]{0:T(256)} %bitcast.64, f32[]{:T(128)} %constant.25.clone.1, f32[]{:T(128)} %constant.73.clone.1, pred[256]{0:T(512)(128)(4,1)S(1)} %compare_and_fusion, f32[2000,2048]{0,1:T(8,128)} %copy.30, s32[1024]{0:T(1024)S(1)} %pad_clamp_fusion), kind=kCustom, calls=%fused_computation.28 | custom fusion | flops 512000 | bytes 20878592 | tf_op jit(solution)/shard_map/scatter | solution.py:198
  292.5 9.9 %all-to-all-start = ((f32[2000,32,16]{0,2,1:T(8,128)}), f32[2000,32,16]{0,2,1:T(8,128)}, u32[]{:S(2)}, u32[]{:S(2)}) async-start(f32[2000,32,16]{0,2,1:T(8,128)} %bitcast.49), calls=%async_computation | async-start | bytes 8388608 | tf_op jit(solution)/shard_map/all_to_all | solution.py:199
  302.5 50.5 %all-to-all-done = f32[2000,32,16]{0,2,1:T(8,128)} async-done(((f32[2000,32,16]{0,2,1:T(8,128)}), f32[2000,32,16]{0,2,1:T(8,128)}, u32[]{:S(2)}, u32[]{:S(2)}) %all-to-all-start) | async-done | bytes 4096032 | tf_op jit(solution)/shard_map/all_to_all | solution.py:199
  353.0 15.2 %scatter_custom_fusion.1 = f32[2000,2048]{0,1:T(8,128)} fusion(s32[512]{0:T(512)S(1)} %bitcast.63, f32[512,2000]{1,0:T(8,128)} %bitcast.11, f32[]{:T(128)} %constant.25.clone.1), kind=kCustom, calls=%fused_computation.24 | custom fusion | flops 1024000 | bytes 16384512 | tf_op jit(solution)/shard_map/scatter-add | solution.py:200
  368.2 17.6 %copy.31 = f32[2000,2048]{1,0:T(8,128)} copy(f32[2000,2048]{0,1:T(8,128)} %scatter_custom_fusion.1) | data formatting | bytes 32768000 | tf_op jit(solution)/shard_map/scatter-add | solution.py:200
  385.8 31.7 %fusion.5 = bf16[2000,2048]{1,0:T(8,128)(2,1)} fusion(f32[2000,2048]{1,0:T(8,128)} %fusion.18, f32[2000,2048]{1,0:T(8,128)} %copy.31, f32[2048]{0:T(1024)S(1)} %copy-done.2, bf16[2000,1]{1,0:T(8,128)(2,1)S(1)} %collective-permute-done.1, bf16[2000,2048]{1,0:T(8,128)(2,1)} %param.12, f32[2000]{0:T(1024)S(1)} %bitcast.58, ...), kind=kLoop, calls=%fused_computation.19 | loop fusion | flops 94208000 | bytes 49184192 | tf_op jit(solution)/shard_map/convert_element_type | solution.py:203
  (175 shorter events, 38.0 us)
Async XLA Ops:
  6.5 187.8 %copy-start = (f32[3,2000]{1,0:T(4,128)S(1)}, f32[3,2000]{1,0:T(4,128)}, u32[]{:S(2)}) copy-start(f32[3,2000]{1,0:T(4,128)} %param.13) | copy-start | bytes 72004
  6.5 246.3 %all-reduce.2.cloned.1.call-start = ((), (), s32[]{:S(2)}) async-start(), calls=%async_computation.1 | async-start | bytes 393216 | tf_op jit(solution)/shard_map/psum | solution.py:186
  8.0 188.7 %collective-permute-start = (bf16[2000,1]{1,0:T(8,128)(2,1)S(1)}, bf16[2000,1]{1,0:T(8,128)(2,1)S(1)}, u32[]{:S(2)}, u32[]{:S(2)}) collective-permute-start(bf16[2000,1]{1,0:T(8,128)(2,1)S(1)} %get-tuple-element.100), channel_id=1, source_target_pairs={{0,1},{1,2},{2,3},{3,4},{4,5},{5,6},{6,7},{7,8},{8,9},{9,10},{10,1... | collective-permute-start | bytes 12008 | tf_op jit(solution)/shard_map/ppermute | solution.py:57
  12.6 184.2 %collective-permute-start.1 = (bf16[2000,1]{1,0:T(8,128)(2,1)S(1)}, bf16[2000,1]{1,0:T(8,128)(2,1)S(1)}, u32[]{:S(2)}, u32[]{:S(2)}) collective-permute-start(bf16[2000,1]{1,0:T(8,128)(2,1)S(1)} %get-tuple-element.101), channel_id=1, source_target_pairs={{1,0},{2,1},{3,2},{4,3},{5,4},{6,5},{7,6},{8,7},{9,8},{10,9},{11,1... | collective-permute-start | bytes 12008 | tf_op jit(solution)/shard_map/ppermute | solution.py:58
  196.7 18.0 %copy-start.5 = (s32[256]{0:T(256)S(1)}, s32[256]{0:T(256)}, u32[]{:S(2)}) copy-start(s32[256]{0:T(256)} %param.16) | copy-start | bytes 3076
  196.7 62.1 %copy-start.1 = (f32[20,2048]{1,0:T(8,128)S(1)}, f32[20,2048]{1,0:T(8,128)}, u32[]{:S(2)}) copy-start(f32[20,2048]{1,0:T(8,128)} %get-tuple-element.39) | copy-start | bytes 491524
  196.8 62.1 %copy-start.4 = (f32[20]{0:T(128)S(1)}, f32[20]{0:T(128)}, u32[]{:S(2)}) copy-start(f32[20]{0:T(128)} %constant.76) | copy-start | bytes 244
  284.5 17.8 %copy-start.3 = (s32[1,32,16]{1,2,0:T(8,128)S(1)}, s32[1,32,16]{1,2,0:T(8,128)}, u32[]{:S(2)}) copy-start(s32[1,32,16]{1,2,0:T(8,128)} %param.18) | copy-start | bytes 6148
  292.5 60.5 %all-to-all-start = ((f32[2000,32,16]{0,2,1:T(8,128)}), f32[2000,32,16]{0,2,1:T(8,128)}, u32[]{:S(2)}, u32[]{:S(2)}) async-start(f32[2000,32,16]{0,2,1:T(8,128)} %bitcast.49), calls=%async_computation | async-start | bytes 8388608 | tf_op jit(solution)/shard_map/all_to_all | solution.py:199
  368.2 17.6 %copy-start.2 = (f32[2048]{0:T(1024)S(1)}, f32[2048]{0:T(1024)}, u32[]{:S(2)}) copy-start(f32[2048]{0:T(1024)} %param.15) | copy-start | bytes 24580
Sparse Core Ops, SparseCore 0:
  214.9 37.8 all-reduce.1
where the time goes:
time: 429 us; the launch traced here: 424 us
  matrix products  124 us (29%)
  waiting for transfers between devices  88.5 us (21%)
  other arithmetic  87.5 us (20%)
  blocking collectives  50.4 us (12%)
  local copies, waits for them, and re-layouts  42.8 us (10%)
  starting transfers between devices  16.4 us (4%)
  between operations  13.6 us (3%)
    dot_general x32, matrix products, add_block(): jnp.einsum('ka,kc->ac', rows, onehot, precision=lax.Precision.HIGHEST)  98 us
    all_to_all x1, waiting for transfers between devices, per_device(): lax.all_to_all(outgoing, 'space', split_axis=1, concat_axis=1, tiled=True)  50.5 us
    psum x1, waiting for transfers between devices, per_device(): moments = lax.psum(partial_moments, 'sect')  38 us
    convert_element_type x1, other arithmetic, per_device(): (current + rate * (equilibrium - current) + WALL_SHARE * wall_sum).astype...  31.7 us
    all_gather x1, blocking collectives, inject(): lax.all_gather(iface_cell, 'space', axis=0, tiled=True)  27.7 us
    all_gather x1, blocking collectives, inject(): lax.all_gather(plenum_moments.astype(jnp.bfloat16), 'space', axis=0, tile...  22.7 us
    reduce_sum x32, other arithmetic, add_block(): hit = hit + jnp.sum(onehot, axis=0)  18.1 us
    dot_general x1, matrix products, per_device(): jnp.dot(moment_basis(velocity, quad_weight), read, preferred_element_type...  17.9 us
  transfers between devices with their start and end apart: 4, of which 2 were waited for; matrix products, arithmetic and copies ran while one was open for 31% of the time, Pallas kernels for 0%

commit v1 on v0

v1 whole, which is shorter than its diff:
```python
import functools

import jax
import jax.numpy as jnp
from jax import lax
from jax.experimental import pallas as pl
from jax.experimental.pallas import tpu as pltpu
from jax.sharding import PartitionSpec as P

NV = 8000
MOMENTS = 20


COURANT_SCALE = 0.6
ES_SHIFT = -0.5
WALL_SHARE = 0.5
ORDER_TWO = ((0, 0), (1, 1), (2, 2), (0, 1), (0, 2), (1, 2))
ORDER_THREE = (
    (0, 0, 0),
    (1, 1, 1),
    (2, 2, 2),
    (0, 0, 1),
    (0, 0, 2),
    (1, 1, 0),
    (1, 1, 2),
    (2, 2, 0),
    (2, 2, 1),
    (0, 1, 2),
)
RECON_NORMS = (
    1.0,
    1.0,
    1.0,
    1.0,
    2.0,
    2.0,
    2.0,
    1.0,
    1.0,
    1.0,
    6.0,
    6.0,
    6.0,
    2.0,
    2.0,
    2.0,
    2.0,
    2.0,
    2.0,
    1.0,
)
ROW_BLOCK = 400
CELL_HI = 8


def halo_columns(shard):
    count = lax.axis_size("space")
    length = shard.shape[1]
    up = [(i, i + 1) for i in range(count - 1)]
    down = [(j, i) for i, j in up]
    before = lax.ppermute(shard[:, length - 1 :], "space", up)
    after = lax.ppermute(shard[:, :1], "space", down)
    return before, after


def hermite(velocity):
    unity_row = jnp.ones_like(velocity[0])
    stacked = [unity_row, velocity[0], velocity[1], velocity[2]]
    for i, j in ORDER_TWO:
        element = velocity[i] * velocity[j]
        if i == j:
            element = element - 1.0
        stacked.append(element)
    for i, j, k in ORDER_THREE:
        element = velocity[i] * velocity[j] * velocity[k]
        if i == j:
            element = element - velocity[k]
        if i == k:
            element = element - velocity[j]
        if j == k:
            element = element - velocity[i]
        stacked.append(element)
    return jnp.stack(stacked)


def moment_basis(velocity, weight):
    return (hermite(velocity) * (weight / NV)[None, :]).astype(jnp.bfloat16)


def recon_basis(velocity):
    norms = jnp.array(RECON_NORMS, dtype=jnp.float32)
    return (hermite(velocity) / norms[:, None]).T.astype(jnp.bfloat16)


def es_targets(moments):
    density = moments[0]
    moving = [moments[1], moments[2], moments[3]]
    trace_sum = moments[4] + moments[5] + moments[6]
    second = [[None, None, None], [None, None, None], [None, None, None]]
    for n, (i, j) in enumerate(ORDER_TWO):
        element = (1.0 - ES_SHIFT) * moments[4 + n]
        if i == j:
            element = element + ES_SHIFT * trace_sum / 3.0
        second[i][j] = element
        second[j][i] = element
    stacked = [density] + moving + [second[i][j] for i, j in ORDER_TWO]
    for n, (i, j, k) in enumerate(ORDER_THREE):
        stacked.append(
            0.5 * moments[10 + n]
            + (moving[i] * second[j][k] + moving[j] * second[i][k] + moving[k] * second[i][j])
            / density
        )
    return jnp.stack(stacked)


def transport_block(dist_ref, left_ref, right_ref, ahead_ref, behind_ref):
    centre = dist_ref[...].astype(jnp.float32)
    width = centre.shape[1]
    column = lax.broadcasted_iota(jnp.int32, centre.shape, 1)
    left = jnp.where(
        column == 0, left_ref[...].astype(jnp.float32), pltpu.roll(centre, 1, 1)
    )
    right = jnp.where(
        column == width - 1,
        right_ref[...].astype(jnp.float32),
        pltpu.roll(centre, width - 1, 1),
    )
    ahead = ahead_ref[...]
    behind = behind_ref[...]
    return (centre - ahead * (centre - left) - behind * (right - centre)).astype(jnp.bfloat16)


def moments_kernel(dist_ref, left_ref, right_ref, ahead_ref, behind_ref, basis_ref, out_ref):
    @pl.when(pl.program_id(0) == 0)
    def _():
        out_ref[...] = jnp.zeros_like(out_ref)

    read = transport_block(dist_ref, left_ref, right_ref, ahead_ref, behind_ref)
    out_ref[...] += jnp.dot(basis_ref[0], read, preferred_element_type=jnp.float32)


def relax_kernel(
    dist_ref, left_ref, right_ref, ahead_ref, behind_ref, recon_ref, recon3_ref, targets_ref,
    walls_ref, rate_ref, out_ref,
):
    read = transport_block(dist_ref, left_ref, right_ref, ahead_ref, behind_ref).astype(jnp.float32)
    equilibrium = jnp.dot(recon_ref[...], targets_ref[...], preferred_element_type=jnp.float32)
    wall_half = jnp.dot(recon3_ref[...], walls_ref[...], preferred_element_type=jnp.float32)
    rate = rate_ref[...]
    out_ref[...] = (read + rate * (equilibrium - read) + wall_half).astype(out_ref.dtype)


def row_spec(width):
    return pl.BlockSpec((ROW_BLOCK, width), lambda i: (i, 0))


def full_spec(shape):
    return pl.BlockSpec(shape, lambda i: (0,) * len(shape))


def moments_call(dist, left, right, ahead, behind, basis):
    rows, cells = dist.shape
    steps = rows // ROW_BLOCK
    blocks = basis.reshape(MOMENTS, steps, ROW_BLOCK).transpose(1, 0, 2)
    return pl.pallas_call(
        moments_kernel,
        grid=(steps,),
        in_specs=[
            row_spec(cells),
            row_spec(1),
            row_spec(1),
            row_spec(1),
            row_spec(1),
            pl.BlockSpec((1, MOMENTS, ROW_BLOCK), lambda i: (i, 0, 0)),
        ],
        out_specs=full_spec((MOMENTS, cells)),
        out_shape=jax.ShapeDtypeStruct((MOMENTS, cells), jnp.float32),
        compiler_params=pltpu.CompilerParams(dimension_semantics=("arbitrary",)),
        cost_estimate=pl.CostEstimate(
            flops=2 * rows * cells * MOMENTS + 8 * rows * cells,
            bytes_accessed=rows * cells * 2 + MOMENTS * cells * 4,
            transcendentals=0,
        ),
    )(dist, left, right, ahead, behind, blocks)


def relax_call(dist, left, right, ahead, behind, recon, recon3, targets, walls, rate):
    rows, cells = dist.shape
    steps = rows // ROW_BLOCK
    return pl.pallas_call(
        relax_kernel,
        grid=(steps,),
        in_specs=[
            row_spec(cells),
            row_spec(1),
            row_spec(1),
            row_spec(1),
            row_spec(1),
            row_spec(recon.shape[1]),
            row_spec(recon3.shape[1]),
            full_spec(targets.shape),
            full_spec(walls.shape),
            full_spec(rate.shape),
        ],
        out_specs=row_spec(cells),
        out_shape=jax.ShapeDtypeStruct((rows, cells), jnp.bfloat16),
        compiler_params=pltpu.CompilerParams(dimension_semantics=("parallel",)),
        cost_estimate=pl.CostEstimate(
            flops=2 * rows * cells * 80 + 12 * rows * cells,
            bytes_accessed=rows * cells * 4,
            transcendentals=0,
        ),
    )(dist, left, right, ahead, behind, recon, recon3, targets, walls, rate)


def split_three(values):
    first = values.astype(jnp.bfloat16)
    rest = values - first.astype(jnp.float32)
    second = rest.astype(jnp.bfloat16)
    third = (rest - second.astype(jnp.float32)).astype(jnp.bfloat16)
    return jnp.concatenate([first, second, third], axis=0)


def inject(closure, plenum_moments, iface_cell, base):
    width = closure.shape[1]
    low = width // CELL_HI
    coded = jnp.concatenate(
        [
            plenum_moments.astype(jnp.bfloat16),
            (iface_cell // 256).astype(jnp.bfloat16)[:, None],
            (iface_cell % 256).astype(jnp.bfloat16)[:, None],
        ],
        axis=1,
    )
    gathered = lax.all_gather(coded, "space", axis=0, tiled=True)
    rows = gathered[:, :MOMENTS]
    cells = gathered[:, MOMENTS].astype(jnp.int32) * 256 + gathered[:, MOMENTS + 1].astype(jnp.int32)
    local = cells - base
    valid = (local >= 0) & (local < width)
    upper = jnp.where(valid, local // low, -1)
    lower = local % low
    extended = jnp.concatenate([rows, jnp.ones((rows.shape[0], 1), jnp.bfloat16)], axis=1)
    pick_hi = (upper[:, None] == jnp.arange(CELL_HI, dtype=jnp.int32)[None, :]).astype(jnp.bfloat16)
    spread = (pick_hi[:, :, None] * extended[:, None, :]).reshape(rows.shape[0], -1)
    pick_lo = (lower[:, None] == jnp.arange(low, dtype=jnp.int32)[None, :]).astype(jnp.bfloat16)
    folded = lax.dot_general(
        spread, pick_lo, (((0,), (0,)), ((), ())), preferred_element_type=jnp.float32
    )
    folded = folded.reshape(CELL_HI, MOMENTS + 1, low).transpose(1, 0, 2).reshape(MOMENTS + 1, width)
    fluid = folded[:MOMENTS]
    hit = folded[MOMENTS]
    return closure + hit[None, :] * (fluid - closure)


def ghost_walls(targets, ghost_source, ghost_owner, wall_cell):
    cells = targets.shape[1]
    peers = lax.axis_size("space")
    capacity = wall_cell.shape[2]
    slots = peers * capacity
    owner = ghost_owner[:, 0]
    marks = (owner[:, None] == jnp.arange(peers, dtype=jnp.int32)[None, :]).astype(jnp.int32)
    before = jnp.cumsum(marks, axis=0) - marks
    slot = jnp.sum(marks * before, axis=1)
    places = owner * capacity + slot
    at_place = (places[:, None] == jnp.arange(slots, dtype=jnp.int32)[None, :]).astype(jnp.int32)
    source_of = jnp.sum(at_place * (ghost_source[:, None] + 1), axis=0) - 1
    select = (jnp.arange(cells, dtype=jnp.int32)[:, None] == source_of[None, :]).astype(jnp.bfloat16)
    outgoing = jnp.dot(targets, select, preferred_element_type=jnp.float32).astype(jnp.bfloat16)
    arrived = lax.all_to_all(outgoing, "space", split_axis=1, concat_axis=1, tiled=True)
    walls = wall_cell.reshape(slots)
    land = (walls[:, None] == jnp.arange(cells, dtype=jnp.int32)[None, :]).astype(jnp.bfloat16)
    return jnp.dot(arrived, land, preferred_element_type=jnp.float32)


def per_device(
    dist,
    velocity,
    quad_weight,
    collision_rate,
    ghost_source,
    ghost_owner,
    wall_cell,
    plenum_moments,
    iface_cell,
):
    cells = dist.shape[1]
    courant = COURANT_SCALE * velocity[0]
    ahead = jnp.maximum(courant, 0.0)[:, None]
    behind = jnp.minimum(courant, 0.0)[:, None]
    left, right = halo_columns(dist)
    partial_moments = moments_call(
        dist, left, right, ahead, behind, moment_basis(velocity, quad_weight)
    )
    slab_base = lax.axis_index("space") * cells
    moments = lax.psum(partial_moments, "sect")
    targets = inject(es_targets(moments), plenum_moments, iface_cell, slab_base).astype(
        jnp.bfloat16
    )
    wall_moments = ghost_walls(targets, ghost_source, ghost_owner, wall_cell)
    recon = recon_basis(velocity)
    recon3 = jnp.concatenate([recon, recon, recon], axis=1)
    walls = split_three(WALL_SHARE * wall_moments)
    return relax_call(
        dist, left, right, ahead, behind, recon, recon3, targets, walls, collision_rate[None, :]
    )


def solution(mesh):
    in_specs = (
        P("sect", "space"),
        P(None, "sect"),
        P("sect"),
        P("space"),
        P("space"),
        P("space", None),
        P("space", None, None),
        P("space", None),
        P("space"),
    )
    out_specs = P("sect", "space")
    return jax.shard_map(
        per_device, mesh=mesh, in_specs=in_specs, out_specs=out_specs, check_vma=False
    )
```

time: 429 us -> 191 us (0.45)
  matrix products: 124 us -> 9.29 us
  other arithmetic: 87.5 us -> 20 us
  waiting for transfers between devices: 88.5 us -> 43.4 us
  Pallas kernels: 0 us -> 31.2 us
  blocking collectives: 50.4 us -> 28.4 us
  local copies, waits for them, and re-layouts: 42.8 us -> 27.6 us
    dot_general x34 -> x3, matrix products: 124 us -> 9.29 us  [the longest x1 7.7 us: inject(): lax.dot_general(spread, pick_lo, (((0,), (0,)), ((), ())), preferred_elem...]
    all_to_all x1, waiting for transfers between devices: 50.5 us -> 5.87 us  [ghost_walls(): lax.all_to_all(outgoing, 'space', split_axis=1, concat_axis=1, tiled=True)]
    convert_element_type x2 -> x5, other arithmetic: 32.3 us -> 0.84 us  [the longest x1 0.7 us: inject(): (iface_cell // 256).astype(jnp.bfloat16)[:, None]]
    pallas_call x0 -> x2, Pallas kernels: none -> 31.2 us  [the longest x1 18.6 us: relax_call(): pl.pallas_call(relax_kernel, grid=(steps,), in_specs=[row_spec(cells), ro...]
    all_gather x2 -> x1, blocking collectives: 50.4 us -> 28.4 us  [inject(): gathered = lax.all_gather(coded, 'space', axis=0, tiled=True)]
    reduce_sum x33 -> x2, other arithmetic: 18.8 us -> 0.25 us  [the longest x1 0.15 us: ghost_walls(): source_of = jnp.sum(at_place * (ghost_source[:, None] + 1), axis=0) - 1]
    scatter-add x1 -> x0, local copies, waits for them, and re-layouts: 17.6 us -> none  [per_device(): jnp.zeros((picked.shape[0], cells), jnp.float32).at[:, walls].add(arrived)]
    scatter-add x1 -> x0, other arithmetic: 15.2 us -> none  [per_device(): jnp.zeros((picked.shape[0], cells), jnp.float32).at[:, walls].add(arrived)]
  transfers between devices with their start and end apart: 4 -> 4, of which waited for: 2 -> 2; matrix products, arithmetic and copies ran while one was open for 31% -> 23% of each run, Pallas kernels for 0% -> 0%
where the time goes in v1:
time: 191 us; the launch traced here: 190 us
  waiting for transfers between devices  43.4 us (23%)
  Pallas kernels  31.2 us (16%)
  blocking collectives  28.4 us (15%)
  local copies, waits for them, and re-layouts  27.6 us (14%)
  other arithmetic  20 us (10%)
  starting transfers between devices  16.3 us (9%)
  between operations  13.7 us (7%)
  matrix products  9.29 us (5%)
    psum x1, waiting for transfers between devices, per_device(): moments = lax.psum(partial_moments, 'sect')  37.5 us
    all_gather x1, blocking collectives, inject(): gathered = lax.all_gather(coded, 'space', axis=0, tiled=True)  28.4 us
    pallas_call x1, Pallas kernels, relax_call(): pl.pallas_call(relax_kernel, grid=(steps,), in_specs=[row_spec(cells), ro...  18.6 us
    pallas_call x1, Pallas kernels, moments_call(): pl.pallas_call(moments_kernel, grid=(steps,), in_specs=[row_spec(cells),...  12.6 us
    all_to_all x1, starting transfers between devices, ghost_walls(): lax.all_to_all(outgoing, 'space', split_axis=1, concat_axis=1, tiled=True)  9.8 us
    dot_general x1, matrix products, inject(): lax.dot_general(spread, pick_lo, (((0,), (0,)), ((), ())), preferred_elem...  7.7 us
    dot_general x1, local copies, waits for them, and re-layouts, inject(): lax.dot_general(spread, pick_lo, (((0,), (0,)), ((), ())), preferred_elem...  7.34 us
    mul x1, local copies, waits for them, and re-layouts, inject(): pick_hi[:, :, None] * extended[:, None, :]  7.22 us
  transfers between devices with their start and end apart: 4, of which 2 were waited for; matrix products, arithmetic and copies ran while one was open for 23% of the time, Pallas kernels for 0%

profile of v1, /device:TPU:1, one launch (start us, length us, event | category | flops | bytes accessed | tf_op | source)
XLA Modules:
  0.0 189.8 jit_solution(3290429612092887080)
XLA Ops:
  6.5 2.2 %fusion.62 = (bf16[2000,1]{1,0:T(8,128)(2,1)S(1)}, bf16[2000,1]{1,0:T(8,128)(2,1)}) fusion(bf16[2000,2048]{1,0:T(8,128)(2,1)} %dist_ref.3), kind=kLoop, calls=%fused_computation.142 | loop fusion | bytes 16000 | tf_op jit(solution)/shard_map/slice | solution.py:62
  8.8 4.6 %collective-permute-start = (bf16[2000,1]{1,0:T(8,128)(2,1)}, bf16[2000,1]{1,0:T(8,128)(2,1)S(1)}, u32[]{:S(2)}, u32[]{:S(2)}) collective-permute-start(bf16[2000,1]{1,0:T(8,128)(2,1)} %get-tuple-element.44), channel_id=1, source_target_pairs={{0,1},{1,2},{2,3},{3,4},{4,5},{5,6},{6,7},{7,8},{8,9},{9,10},{10,1... | collective-permute-start | bytes 12008 | tf_op jit(solution)/shard_map/ppermute | solution.py:61
  13.4 1.9 %collective-permute-start.1 = (bf16[2000,1]{1,0:T(8,128)(2,1)S(1)}, bf16[2000,1]{1,0:T(8,128)(2,1)S(1)}, u32[]{:S(2)}, u32[]{:S(2)}) collective-permute-start(bf16[2000,1]{1,0:T(8,128)(2,1)S(1)} %get-tuple-element.43), channel_id=1, source_target_pairs={{1,0},{2,1},{3,2},{4,3},{5,4},{6,5},{7,6},{8,7},{9,8},{10,9},{11,1... | collective-permute-start | bytes 12008 | tf_op jit(solution)/shard_map/ppermute | solution.py:62
  15.3 0.5 broadcast.324
  15.8 1.7 fusion.48
  17.5 1.7 fusion.51
  19.2 0.8 stack.46
  20.1 0.7 reduce.53
  22.2 0.7 broadcast_multiply_fusion.1
  23.0 0.7 fusion.43
  23.7 0.8 convert_element_type.70
  24.5 28.4 %all_gather.3 = bf16[16384,22]{0,1:T(8,128)(2,1)S(1)} all-gather(bf16[512,22]{0,1:T(8,128)(2,1)S(1)} %pad_maximum_fusion.2), channel_id=1, replica_groups=mesh['sect'=4,'space'=32] {'space'}, dimensions={0}, use_global_device_ids=true | all-gather | bytes 743424 | tf_op jit(solution)/shard_map/all_gather | solution.py:235
  52.9 0.4 and_select_fusion
  53.3 0.3 and_select_fusion.2
  53.7 0.8 slice_select_fusion
  54.5 3.5 %broadcast_multiply_fusion = bf16[16384,8,21]{0,2,1:T(8,128)(2,1)} fusion(bf16[16384,21]{0,1:T(8,128)(2,1)S(1)} %slice_select_fusion, bf16[16384,8]{0,1:T(8,128)(2,1)S(1)} %fusion.13), kind=kLoop, calls=%fused_computation.8 | loop fusion | flops 2752512 | bytes 6455296 | tf_op jit(solution)/shard_map/mul | solution.py:244
  57.9 7.2 %mul.431 = bf16[16384,168]{0,1:T(8,128)(2,1)} reshape(bf16[16384,8,21]{0,2,1:T(8,128)(2,1)} %broadcast_multiply_fusion) | data formatting | bytes 11010048 | tf_op jit(solution)/shard_map/mul | solution.py:244
  65.2 7.3 %dot_general.14 = bf16[8,21,16384]{2,1,0:T(8,128)(2,1)} reshape(bf16[168,16384]{1,0:T(8,128)(2,1)} %bitcast.56) | data formatting | bytes 11010048 | tf_op jit(solution)/shard_map/dot_general | solution.py:246
  72.5 0.8 reduce-window.6
  73.3 0.2 slice_reduce_fusion
  73.7 0.3 stack.44
  73.9 0.4 copy.133
  74.3 0.3 stack.114
  74.6 0.7 fusion.16.basis_ref
  75.3 7.7 %fusion.9 = f32[21,8,256]{2,0,1:T(8,128)S(1)} fusion(bf16[8,21,16384]{2,1,0:T(8,128)(2,1)} %dot_general.14, s32[16384]{0:T(1024)S(1)} %bitcast.63), kind=kOutput, calls=%fused_computation.12 | convolution fusion | flops 1413480448 | bytes 5742592 | tf_op jit(solution)/shard_map/dot_general | solution.py:246
  83.1 0.1 select_reduce_fusion
  83.2 1.4 copy.160.behind_ref
  84.6 1.3 copy.159.ahead_ref
  86.2 0.8 copy-done.1
  86.9 0.8 copy-done.2
  87.7 12.6 %shard_map.100 = f32[20,2048]{1,0:T(8,128)} custom-call(bf16[2000,2048]{1,0:T(8,128)(2,1)} %dist_ref.3, bf16[2000,1]{1,0:T(8,128)(2,1)} %copy-done.1, bf16[2000,1]{1,0:T(8,128)(2,1)} %copy-done.2, f32[2000,1]{1,0:T(8,128)} %copy.159.ahead_ref, f32[2000,1]{1,0:T(8,128)} %copy.160.behind_ref, bf16[5,20,400]{2,1,0:T(8,128)(2,1)} %fusion.16.basis_ref), custom_call_target="tpu_custom_call" | custom-call | flops 196608000 | bytes 8355840 | tf_op jit(solution)/shard_map/pallas_call | solution.py:165
  100.4 37.5 %all-reduce.2.cloned.1.call-done = f32[20,2048]{1,0:T(8,128)} async-done(((f32[20,2048]{1,0:T(8,128)}), f32[20,2048]{1,0:T(8,128)}) %all-reduce.2.cloned.1.call-update) | async-done | bytes 163856 | tf_op jit(solution)/shard_map/psum | solution.py:295
  137.8 1.2 fusion.31
  139.1 0.8 slice.109
  139.9 1.2 fusion.32
  141.1 1.3 fusion.33
  142.4 1.2 fusion.34
  143.6 0.2 stack.115
  143.9 0.8 fusion.12
  144.7 0.2 copy.161
  144.8 0.8 reshape.222
  145.6 9.8 %all-to-all-start = ((bf16[32,2,160]{2,1,0:T(2,128)(2,1)}), bf16[32,2,160]{2,1,0:T(2,128)(2,1)S(1)}, u32[]{:S(2)}, u32[]{:S(2)}) async-start(bf16[32,2,160]{2,1,0:T(2,128)(2,1)} %reshape.222), calls=%async_computation | async-start | bytes 65536 | tf_op jit(solution)/shard_map/all_to_all | solution.py:269
  155.4 1.2 pad_maximum_fusion.recon3_ref
  156.8 5.9 %all-to-all-done = bf16[32,2,160]{2,1,0:T(2,128)(2,1)S(1)} async-done(((bf16[32,2,160]{2,1,0:T(2,128)(2,1)}), bf16[32,2,160]{2,1,0:T(2,128)(2,1)S(1)}, u32[]{:S(2)}, u32[]{:S(2)}) %all-to-all-start) | async-done | bytes 20512 | tf_op jit(solution)/shard_map/all_to_all | solution.py:269
  162.7 0.1 reshape.223
  162.8 0.8 fusion.63
  163.7 0.7 pad_maximum_fusion.1.walls_ref
  164.4 18.6 %shard_map.101 = bf16[2000,2048]{1,0:T(8,128)(2,1)} custom-call(bf16[2000,2048]{1,0:T(8,128)(2,1)} %dist_ref.3, bf16[2000,1]{1,0:T(8,128)(2,1)} %copy-done.1, bf16[2000,1]{1,0:T(8,128)(2,1)} %copy-done.2, f32[2000,1]{1,0:T(8,128)} %copy.159.ahead_ref, f32[2000,1]{1,0:T(8,128)} %copy.160.behind_ref, bf16[2000,20]{1,0:T(8,128)(2,1)} %copy-done, ...), custom_call_target="tpu_custom_call" | custom-call | flops 704512000 | bytes 16384000 | tf_op jit(solution)/shard_map/pallas_call | solution.py:190
  (59 shorter events, 2.2 us)
Async XLA Ops:
  6.5 131.3 %all-reduce.2.cloned.1.call-start = ((), (), s32[]{:S(2)}) async-start(), calls=%async_computation.1 | async-start | bytes 393216 | tf_op jit(solution)/shard_map/psum | solution.py:295
  8.8 77.4 %collective-permute-start = (bf16[2000,1]{1,0:T(8,128)(2,1)}, bf16[2000,1]{1,0:T(8,128)(2,1)S(1)}, u32[]{:S(2)}, u32[]{:S(2)}) collective-permute-start(bf16[2000,1]{1,0:T(8,128)(2,1)} %get-tuple-element.44), channel_id=1, source_target_pairs={{0,1},{1,2},{2,3},{3,4},{4,5},{5,6},{6,7},{7,8},{8,9},{9,10},{10,1... | collective-permute-start | bytes 12008 | tf_op jit(solution)/shard_map/ppermute | solution.py:61
  13.4 72.8 %collective-permute-start.1 = (bf16[2000,1]{1,0:T(8,128)(2,1)S(1)}, bf16[2000,1]{1,0:T(8,128)(2,1)S(1)}, u32[]{:S(2)}, u32[]{:S(2)}) collective-permute-start(bf16[2000,1]{1,0:T(8,128)(2,1)S(1)} %get-tuple-element.43), channel_id=1, source_target_pairs={{1,0},{2,1},{3,2},{4,3},{5,4},{6,5},{7,6},{8,7},{9,8},{10,9},{11,1... | collective-permute-start | bytes 12008 | tf_op jit(solution)/shard_map/ppermute | solution.py:62
  65.2 7.4 %copy-start.5 = (s32[256,1]{0,1:T(1,128)S(1)}, s32[256,1]{0,1:T(1,128)}, u32[]{:S(2)}) copy-start(s32[256,1]{0,1:T(1,128)} %param.15) | copy-start | bytes 3076
  65.2 8.5 %copy-start.7 = (s32[256]{0:T(256)S(1)}, s32[256]{0:T(256)}, u32[]{:S(2)}) copy-start(s32[256]{0:T(256)} %param.14) | copy-start | bytes 3076
  65.2 8.5 %copy-start.3 = (f32[3,2000]{1,0:T(4,128)S(1)}, f32[3,2000]{1,0:T(4,128)}, u32[]{:S(2)}) copy-start(f32[3,2000]{1,0:T(4,128)} %param.11) | copy-start | bytes 72004
  75.3 7.7 %copy-start.8 = (f32[20]{0:T(128)S(1)}, f32[20]{0:T(128)}, u32[]{:S(2)}) copy-start(f32[20]{0:T(128)} %constant.98) | copy-start | bytes 244
  83.1 72.3 %copy-start = (bf16[2000,20]{1,0:T(8,128)(2,1)}, bf16[2000,20]{1,0:T(8,128)(2,1)S(1)}, u32[]{:S(2)}) copy-start(bf16[2000,20]{1,0:T(8,128)(2,1)S(1)} %fusion.14.recon_ref) | copy-start | bytes 240004
  86.1 70.5 %copy-start.6 = (s32[1,32,16]{1,2,0:T(8,128)S(1)}, s32[1,32,16]{1,2,0:T(8,128)}, u32[]{:S(2)}) copy-start(s32[1,32,16]{1,2,0:T(8,128)} %param.16) | copy-start | bytes 6148
  86.1 0.8 copy-start.1
  86.9 0.8 copy-start.2
  143.9 20.5 %copy-start.4 = (bf16[20,2048]{1,0:T(8,128)(2,1)}, bf16[20,2048]{1,0:T(8,128)(2,1)S(1)}, u32[]{:S(2)}) copy-start(bf16[20,2048]{1,0:T(8,128)(2,1)S(1)} %add_convert_fusion.targets_ref) | copy-start | bytes 245764
  145.6 17.1 %all-to-all-start = ((bf16[32,2,160]{2,1,0:T(2,128)(2,1)}), bf16[32,2,160]{2,1,0:T(2,128)(2,1)S(1)}, u32[]{:S(2)}, u32[]{:S(2)}) async-start(bf16[32,2,160]{2,1,0:T(2,128)(2,1)} %reshape.222), calls=%async_computation | async-start | bytes 65536 | tf_op jit(solution)/shard_map/all_to_all | solution.py:269
Sparse Core Ops, SparseCore 0:
  100.5 37.3 all-reduce.1

commit v2 on v1

--- a/solution.py
+++ b/solution.py
@@ -221,9 +221,20 @@
     return jnp.concatenate([first, second, third], axis=0)
 
 
-def inject(closure, plenum_moments, iface_cell, base):
-    width = closure.shape[1]
+def sect_sum(values):
+    count = lax.axis_size("sect")
+    total = values
+    for shift in range(1, count):
+        pairs = [(i, (i + shift) % count) for i in range(count)]
+        total = total + lax.ppermute(values, "sect", pairs)
+    return total
+
+
+def interface_rows(plenum_moments, iface_cell, width, base):
     low = width // CELL_HI
+    count = lax.axis_size("sect")
+    share = plenum_moments.shape[0] // count
+    start = lax.axis_index("sect") * share
     coded = jnp.concatenate(
         [
             plenum_moments.astype(jnp.bfloat16),
@@ -232,6 +243,7 @@
         ],
         axis=1,
     )
+    coded = lax.dynamic_slice_in_dim(coded, start, share, axis=0)
     gathered = lax.all_gather(coded, "space", axis=0, tiled=True)
     rows = gathered[:, :MOMENTS]
     cells = gathered[:, MOMENTS].astype(jnp.int32) * 256 + gathered[:, MOMENTS + 1].astype(jnp.int32)
@@ -246,7 +258,10 @@
     folded = lax.dot_general(
         spread, pick_lo, (((0,), (0,)), ((), ())), preferred_element_type=jnp.float32
     )
-    folded = folded.reshape(CELL_HI, MOMENTS + 1, low).transpose(1, 0, 2).reshape(MOMENTS + 1, width)
+    return folded.reshape(CELL_HI, MOMENTS + 1, low).transpose(1, 0, 2).reshape(MOMENTS + 1, width)
+
+
+def inject(closure, folded):
     fluid = folded[:MOMENTS]
     hit = folded[MOMENTS]
     return closure + hit[None, :] * (fluid - closure)
@@ -292,10 +307,9 @@
         dist, left, right, ahead, behind, moment_basis(velocity, quad_weight)
     )
     slab_base = lax.axis_index("space") * cells
-    moments = lax.psum(partial_moments, "sect")
-    targets = inject(es_targets(moments), plenum_moments, iface_cell, slab_base).astype(
-        jnp.bfloat16
-    )
+    partial_rows = interface_rows(plenum_moments, iface_cell, cells, slab_base)
+    summed = sect_sum(jnp.concatenate([partial_moments, partial_rows], axis=0))
+    targets = inject(es_targets(summed[:MOMENTS]), summed[MOMENTS:]).astype(jnp.bfloat16)
     wall_moments = ghost_walls(targets, ghost_source, ghost_owner, wall_cell)
     recon = recon_basis(velocity)
     recon3 = jnp.concatenate([recon, recon, recon], axis=1)

time: 191 us -> 146 us (0.76)
  waiting for transfers between devices: 43.4 us -> 22.5 us
  between operations: 13.7 us -> 0.35 us
  matrix products: 9.29 us -> 4.18 us
  local copies, waits for them, and re-layouts: 27.6 us -> 25.3 us
  blocking collectives: 28.4 us -> 26.3 us
    psum x1 -> x0, waiting for transfers between devices: 37.5 us -> none  [per_device(): moments = lax.psum(partial_moments, 'sect')]
    ppermute x0 -> x3, waiting for transfers between devices: none -> 16.6 us  [sect_sum(): total = total + lax.ppermute(values, 'sect', pairs)]
    another operation x22, local copies, waits for them, and re-layouts: 3.17 us -> 14.9 us  [hermite(): return jnp.stack(stacked)]
    mul x1, local copies, waits for them, and re-layouts: 7.22 us -> 0.46 us  [interface_rows(): pick_hi[:, :, None] * extended[:, None, :]]
    dot_general x1, local copies, waits for them, and re-layouts: 7.34 us -> 1.59 us  [interface_rows(): lax.dot_general(spread, pick_lo, (((0,), (0,)), ((), ())), preferred_elem...]
    dot_general x1, matrix products: 7.7 us -> 2.59 us  [interface_rows(): lax.dot_general(spread, pick_lo, (((0,), (0,)), ((), ())), preferred_elem...]
    add x4 -> x5, other arithmetic: 4.9 us -> 0.38 us  [es_targets(): 0.5 * moments[10 + n]]
    ppermute x0 -> x3, starting transfers between devices: none -> 4.29 us  [sect_sum(): total = total + lax.ppermute(values, 'sect', pairs)]
  transfers between devices with their start and end apart: 4 -> 6, of which waited for: 2 -> 4; matrix products, arithmetic and copies ran while one was open for 23% -> 27% of each run, Pallas kernels for 0% -> 0%
where the time goes in v2:
time: 146 us; the launch traced here: 145 us
  Pallas kernels  31.2 us (21%)
  blocking collectives  26.3 us (18%)
  local copies, waits for them, and re-layouts  25.3 us (17%)
  waiting for transfers between devices  22.5 us (15%)
  other arithmetic  18.2 us (12%)
  starting transfers between devices  16.5 us (11%)
  matrix products  4.18 us (3%)
    all_gather x1, blocking collectives, interface_rows(): gathered = lax.all_gather(coded, 'space', axis=0, tiled=True)  26.3 us
    pallas_call x1, Pallas kernels, relax_call(): pl.pallas_call(relax_kernel, grid=(steps,), in_specs=[row_spec(cells), ro...  18.6 us
    ppermute x3, waiting for transfers between devices, sect_sum(): total = total + lax.ppermute(values, 'sect', pairs)  16.6 us
    another operation x22, local copies, waits for them, and re-layouts, hermite(): return jnp.stack(stacked)  14.9 us
    pallas_call x1, Pallas kernels, moments_call(): pl.pallas_call(moments_kernel, grid=(steps,), in_specs=[row_spec(cells),...  12.6 us
    all_to_all x1, waiting for transfers between devices, ghost_walls(): lax.all_to_all(outgoing, 'space', split_axis=1, concat_axis=1, tiled=True)  5.86 us
    all_to_all x1, starting transfers between devices, ghost_walls(): lax.all_to_all(outgoing, 'space', split_axis=1, concat_axis=1, tiled=True)  5.75 us
    ppermute x3, starting transfers between devices, sect_sum(): total = total + lax.ppermute(values, 'sect', pairs)  4.29 us
  transfers between devices with their start and end apart: 6, of which 4 were waited for; matrix products, arithmetic and copies ran while one was open for 27% of the time, Pallas kernels for 0%

profile of v2, /device:TPU:1, one launch (start us, length us, event | category | flops | bytes accessed | tf_op | source)
XLA Modules:
  0.0 144.5 jit_solution(3817649611115551908)
XLA Ops:
  0.0 2.4 %fusion.67 = (bf16[2000,1]{1,0:T(8,128)(2,1)}, bf16[2000,1]{1,0:T(8,128)(2,1)}) fusion(bf16[2000,2048]{1,0:T(8,128)(2,1)} %dist_ref.3), kind=kLoop, calls=%fused_computation.151 | loop fusion | bytes 16000 | tf_op jit(solution)/shard_map/slice | solution.py:62
  2.4 3.3 %collective-permute-start.1 = (bf16[2000,1]{1,0:T(8,128)(2,1)}, bf16[2000,1]{1,0:T(8,128)(2,1)S(1)}, u32[]{:S(2)}, u32[]{:S(2)}) collective-permute-start(bf16[2000,1]{1,0:T(8,128)(2,1)} %get-tuple-element.43), channel_id=1, source_target_pairs={{1,0},{2,1},{3,2},{4,3},{5,4},{6,5},{7,6},{8,7},{9,8},{10,9},{11,1... | collective-permute-start | bytes 12008 | tf_op jit(solution)/shard_map/ppermute | solution.py:62
  5.6 3.2 %collective-permute-start = (bf16[2000,1]{1,0:T(8,128)(2,1)}, bf16[2000,1]{1,0:T(8,128)(2,1)}, u32[]{:S(2)}, u32[]{:S(2)}) collective-permute-start(bf16[2000,1]{1,0:T(8,128)(2,1)} %get-tuple-element.44), channel_id=1, source_target_pairs={{0,1},{1,2},{2,3},{3,4},{4,5},{5,6},{6,7},{7,8},{8,9},{9,10},{10,1... | collective-permute-start | bytes 12008 | tf_op jit(solution)/shard_map/ppermute | solution.py:61
  8.9 0.8 stack.46
  10.2 2.2 %fusion.55 = (f32[2000]{0:T(1024)S(1)}, f32[1,2000]{1,0:T(1,128)S(1)}, f32[1,2000]{1,0:T(1,128)S(1)}, f32[1,2000]{1,0:T(1,128)S(1)}, f32[2000,1]{0,1:T(1,128)}, ...) fusion(f32[]{:T(128)} %broadcast.324, ...), kind=kLoop, calls=%fused_computation.140 | loop fusion | flops 46000 | bytes 144004 | tf_op jit(solution)/shard_map/sub | solution.py:77
  12.4 2.2 %fusion.53 = (f32[2000]{0:T(1024)S(1)}, f32[2000]{0:T(1024)S(1)}, f32[2000]{0:T(1024)S(1)}, f32[1,2000]{1,0:T(1,128)S(1)}, f32[2000]{0:T(1024)S(1)}, /*index=5*/...) fusion(f32[3,2000]{1,0:T(4,128)} %param.11, ...), kind=kLoop, calls=%fused_computation.134 | loop fusion | flops 40000 | bytes 168004 | tf_op jit(solution)/shard_map/sub | solution.py:72
  14.6 0.7 fusion.49
  15.3 0.7 broadcast_multiply_fusion.1
  16.1 0.8 convert_element_type.70
  16.9 0.7 fusion.23
  18.4 0.8 fusion.22
  19.2 1.2 multiply_add_fusion.9
  21.4 0.7 stack.123
  22.1 0.7 stack.122
  22.7 0.7 stack.118
  24.1 0.7 stack.119
  25.5 0.7 stack.117
  26.1 0.7 stack.120
  26.8 0.7 stack.126
  28.2 0.7 stack.124
  28.9 0.7 stack.129
  30.3 26.3 %all_gather.3 = bf16[4096,22]{0,1:T(8,128)(2,1)S(1)} all-gather(bf16[128,22]{0,1:T(8,128)(2,1)S(1)} %fusion.47), channel_id=1, replica_groups=mesh['sect'=4,'space'=32] {'space'}, dimensions={0}, use_global_device_ids=true | all-gather | bytes 185856 | tf_op jit(solution)/shard_map/all_gather | solution.py:247
  56.7 0.7 and_select_fusion
  57.4 0.7 slice_select_fusion
  58.2 1.0 stack.44
  59.2 1.3 copy.133
  61.2 1.6 %dot_general.14 = bf16[8,21,4096]{2,1,0:T(8,128)(2,1)} reshape(bf16[168,4096]{1,0:T(8,128)(2,1)S(1)} %bitcast.55) | data formatting | bytes 2752512 | tf_op jit(solution)/shard_map/dot_general | solution.py:258
  62.8 2.6 %stack.114 = f32[20,5,400]{2,0,1:T(8,128)S(1)} concatenate(f32[1,5,400]{2,0,1:T(1,128)S(1)} %stack.45, f32[3,5,400]{2,0,1:T(4,128)S(1)} %copy.135, f32[1,5,400]{2,0,1:T(1,128)} %stack.116, f32[1,5,400]{2,0,1:T(1,128)} %stack.117, f32[1,5,400]{2,0,1:T(1,128)} %stack.118, f32[1,5,400]{2,0,1:T(1,128)} %stack.119, f32[1,5,400]{2,0,1:T(1,128)} %stack.120, f32[1,5,400]{2,0,1:T(1,128)} %stack.121, ...), dimensions={0} | concatenate | bytes 320000 | tf_op jit(solution)/shard_map/stack | solution.py:83
  66.1 0.7 fusion.13.recon_ref
  66.8 2.6 %fusion.9 = f32[21,8,256]{2,0,1:T(8,128)S(1)} fusion(bf16[8,21,4096]{2,1,0:T(8,128)(2,1)} %dot_general.14, s32[4096]{0:T(1024)S(1)} %bitcast.63), kind=kOutput, calls=%fused_computation.11 | convolution fusion | flops 353370112 | bytes 1564672 | tf_op jit(solution)/shard_map/dot_general | solution.py:258
  69.4 1.3 copy.160.behind_ref
  70.8 1.4 copy.159.ahead_ref
  72.4 0.8 copy-done.2
  73.1 12.6 %shard_map.100 = f32[20,2048]{1,0:T(8,128)} custom-call(bf16[2000,2048]{1,0:T(8,128)(2,1)} %dist_ref.3, bf16[2000,1]{1,0:T(8,128)(2,1)} %collective-permute-done.left_ref, bf16[2000,1]{1,0:T(8,128)(2,1)} %copy-done.2, f32[2000,1]{1,0:T(8,128)} %copy.159.ahead_ref, f32[2000,1]{1,0:T(8,128)} %copy.160.behind_ref, bf16[5,20,400]{2,1,0:T(8,128)(2,1)} %fusion.19.basis_ref), custom_call_target="tpu_custom_call" | custom-call | flops 196608000 | bytes 8355840 | tf_op jit(solution)/shard_map/pallas_call | solution.py:165
  85.7 1.0 pad_maximum_fusion.1
  86.7 2.8 %collective-permute-start.3 = (f32[41,2048]{1,0:T(8,128)S(1)}, f32[41,2048]{1,0:T(8,128)S(1)}, u32[]{:S(2)}, u32[]{:S(2)}) collective-permute-start(f32[41,2048]{1,0:T(8,128)S(1)} %pad_maximum_fusion.1), channel_id=1, source_target_pairs={{0,64},{32,96},{64,0},{96,32},{1,65},{33,97},{65,1},{97,33},{2,66}... | collective-permute-start | bytes 1007624 | tf_op jit(solution)/shard_map/ppermute | solution.py:229
  89.5 0.9 collective-permute-start.4
  91.1 7.7 %collective-permute-done.3 = f32[41,2048]{1,0:T(8,128)S(1)} collective-permute-done((f32[41,2048]{1,0:T(8,128)S(1)}, f32[41,2048]{1,0:T(8,128)S(1)}, u32[]{:S(2)}, u32[]{:S(2)}) %collective-permute-start.3) | collective-permute-done | bytes 335904 | tf_op jit(solution)/shard_map/ppermute | solution.py:229
  98.8 8.5 %collective-permute-done.4 = f32[41,2048]{1,0:T(8,128)S(1)} collective-permute-done((f32[41,2048]{1,0:T(8,128)S(1)}, f32[41,2048]{1,0:T(8,128)S(1)}, u32[]{:S(2)}, u32[]{:S(2)}) %collective-permute-start.4) | collective-permute-done | bytes 335904 | tf_op jit(solution)/shard_map/ppermute | solution.py:229
  107.7 1.0 add_add_fusion
  109.5 0.8 fusion.12
  110.4 0.8 reshape.222
  111.2 5.7 %all-to-all-start = ((bf16[32,2,160]{2,1,0:T(2,128)(2,1)}), bf16[32,2,160]{2,1,0:T(2,128)(2,1)S(1)}, u32[]{:S(2)}, u32[]{:S(2)}) async-start(bf16[32,2,160]{2,1,0:T(2,128)(2,1)} %reshape.222), calls=%async_computation | async-start | bytes 65536 | tf_op jit(solution)/shard_map/all_to_all | solution.py:284
  117.0 1.2 pad_maximum_fusion.recon3_ref
  118.4 5.9 %all-to-all-done = bf16[32,2,160]{2,1,0:T(2,128)(2,1)S(1)} async-done(((bf16[32,2,160]{2,1,0:T(2,128)(2,1)}), bf16[32,2,160]{2,1,0:T(2,128)(2,1)S(1)}, u32[]{:S(2)}, u32[]{:S(2)}) %all-to-all-start) | async-done | bytes 20512 | tf_op jit(solution)/shard_map/all_to_all | solution.py:284
  124.4 0.8 fusion.68
  125.2 0.7 pad_maximum_fusion.2.walls_ref
  125.9 18.6 %shard_map.101 = bf16[2000,2048]{1,0:T(8,128)(2,1)} custom-call(bf16[2000,2048]{1,0:T(8,128)(2,1)} %dist_ref.3, bf16[2000,1]{1,0:T(8,128)(2,1)} %collective-permute-done.left_ref, bf16[2000,1]{1,0:T(8,128)(2,1)} %copy-done.2, f32[2000,1]{1,0:T(8,128)} %copy.159.ahead_ref, f32[2000,1]{1,0:T(8,128)} %copy.160.behind_ref, bf16[2000,20]{1,0:T(8,128)(2,1)} %copy-done, ...), custom_call_target="tpu_custom_call" | custom-call | flops 704512000 | bytes 16384000 | tf_op jit(solution)/shard_map/pallas_call | solution.py:190
  (66 shorter events, 9.0 us)
Async XLA Ops:
  2.4 70.0 %collective-permute-start.1 = (bf16[2000,1]{1,0:T(8,128)(2,1)}, bf16[2000,1]{1,0:T(8,128)(2,1)S(1)}, u32[]{:S(2)}, u32[]{:S(2)}) collective-permute-start(bf16[2000,1]{1,0:T(8,128)(2,1)} %get-tuple-element.43), channel_id=1, source_target_pairs={{1,0},{2,1},{3,2},{4,3},{5,4},{6,5},{7,6},{8,7},{9,8},{10,9},{11,1... | collective-permute-start | bytes 12008 | tf_op jit(solution)/shard_map/ppermute | solution.py:62
  5.6 66.7 %collective-permute-start = (bf16[2000,1]{1,0:T(8,128)(2,1)}, bf16[2000,1]{1,0:T(8,128)(2,1)}, u32[]{:S(2)}, u32[]{:S(2)}) collective-permute-start(bf16[2000,1]{1,0:T(8,128)(2,1)} %get-tuple-element.44), channel_id=1, source_target_pairs={{0,1},{1,2},{2,3},{3,4},{4,5},{5,6},{6,7},{7,8},{8,9},{9,10},{10,1... | collective-permute-start | bytes 12008 | tf_op jit(solution)/shard_map/ppermute | solution.py:61
  61.2 4.9 %copy-start.1 = (f32[20,2000]{0,1:T(8,128)S(1)}, f32[20,2000]{0,1:T(8,128)}, u32[]{:S(2)}) copy-start(f32[20,2000]{0,1:T(8,128)} %copy.133) | copy-start | bytes 480004
  61.2 5.6 %copy-start.6 = (s32[4096,1]{0,1:T(1,128)S(1)}, s32[4096,1]{0,1:T(1,128)}, u32[]{:S(2)}) copy-start(s32[4096,1]{0,1:T(1,128)} %get-tuple-element.40) | copy-start | bytes 49156
  61.2 8.2 %copy-start.9 = (s32[256]{0:T(256)S(1)}, s32[256]{0:T(256)}, u32[]{:S(2)}) copy-start(s32[256]{0:T(256)} %param.14) | copy-start | bytes 3076
  61.2 8.2 %copy-start.5 = (f32[2000,1]{0,1:T(1,128)S(1)}, f32[2000,1]{0,1:T(1,128)}, u32[]{:S(2)}) copy-start(f32[2000,1]{0,1:T(1,128)} %get-tuple-element.73) | copy-start | bytes 24004
  62.8 8.0 %copy-start.4 = (f32[2000,1]{0,1:T(1,128)S(1)}, f32[2000,1]{0,1:T(1,128)}, u32[]{:S(2)}) copy-start(f32[2000,1]{0,1:T(1,128)} %get-tuple-element.78) | copy-start | bytes 24004
  66.8 50.2 %copy-start = (bf16[2000,20]{1,0:T(8,128)(2,1)}, bf16[2000,20]{1,0:T(8,128)(2,1)S(1)}, u32[]{:S(2)}) copy-start(bf16[2000,20]{1,0:T(8,128)(2,1)S(1)} %fusion.13.recon_ref) | copy-start | bytes 240004
  72.3 18.7 %copy-start.8 = (s32[256,1]{0,1:T(1,128)S(1)}, s32[256,1]{0,1:T(1,128)}, u32[]{:S(2)}) copy-start(s32[256,1]{0,1:T(1,128)} %multiply_add_fusion.9) | copy-start | bytes 3076
  72.3 0.8 copy-start.2
  85.7 32.5 %copy-start.7 = (s32[1,32,16]{1,2,0:T(8,128)S(1)}, s32[1,32,16]{1,2,0:T(8,128)}, u32[]{:S(2)}) copy-start(s32[1,32,16]{1,2,0:T(8,128)} %param.16) | copy-start | bytes 6148
  86.7 12.1 %collective-permute-start.3 = (f32[41,2048]{1,0:T(8,128)S(1)}, f32[41,2048]{1,0:T(8,128)S(1)}, u32[]{:S(2)}, u32[]{:S(2)}) collective-permute-start(f32[41,2048]{1,0:T(8,128)S(1)} %pad_maximum_fusion.1), channel_id=1, source_target_pairs={{0,64},{32,96},{64,0},{96,32},{1,65},{33,97},{65,1},{97,33},{2,66}... | collective-permute-start | bytes 1007624 | tf_op jit(solution)/shard_map/ppermute | solution.py:229
  89.5 17.8 %collective-permute-start.4 = (f32[41,2048]{1,0:T(8,128)S(1)}, f32[41,2048]{1,0:T(8,128)S(1)}, u32[]{:S(2)}, u32[]{:S(2)}) collective-permute-start(f32[41,2048]{1,0:T(8,128)S(1)} %pad_maximum_fusion.1), channel_id=1, source_target_pairs={{0,96},{32,0},{64,32},{96,64},{1,97},{33,1},{65,33},{97,65},{2,98}... | collective-permute-start | bytes 1007624 | tf_op jit(solution)/shard_map/ppermute | solution.py:229
  90.4 17.4 %collective-permute-start.2 = (f32[41,2048]{1,0:T(8,128)S(1)}, f32[41,2048]{1,0:T(8,128)S(1)}, u32[]{:S(2)}, u32[]{:S(2)}) collective-permute-start(f32[41,2048]{1,0:T(8,128)S(1)} %pad_maximum_fusion.1), channel_id=1, source_target_pairs={{0,32},{32,64},{64,96},{96,0},{1,33},{33,65},{65,97},{97,1},{2,34}... | collective-permute-start | bytes 1007624 | tf_op jit(solution)/shard_map/ppermute | solution.py:229
  109.5 16.4 %copy-start.3 = (bf16[20,2048]{1,0:T(8,128)(2,1)}, bf16[20,2048]{1,0:T(8,128)(2,1)S(1)}, u32[]{:S(2)}) copy-start(bf16[20,2048]{1,0:T(8,128)(2,1)S(1)} %fusion.16.targets_ref) | copy-start | bytes 245764
  111.2 13.0 %all-to-all-start = ((bf16[32,2,160]{2,1,0:T(2,128)(2,1)}), bf16[32,2,160]{2,1,0:T(2,128)(2,1)S(1)}, u32[]{:S(2)}, u32[]{:S(2)}) async-start(bf16[32,2,160]{2,1,0:T(2,128)(2,1)} %reshape.222), calls=%async_computation | async-start | bytes 65536 | tf_op jit(solution)/shard_map/all_to_all | solution.py:284

commit v3 on v2

--- a/solution.py
+++ b/solution.py
@@ -1,11 +1,10 @@
-import functools
-
 import jax
 import jax.numpy as jnp
 from jax import lax
 from jax.experimental import pallas as pl
 from jax.experimental.pallas import tpu as pltpu
 from jax.sharding import PartitionSpec as P
+
 
 NV = 8000
 MOMENTS = 20
@@ -231,7 +230,6 @@
 
 
 def interface_rows(plenum_moments, iface_cell, width, base):
-    low = width // CELL_HI
     count = lax.axis_size("sect")
     share = plenum_moments.shape[0] // count
     start = lax.axis_index("sect") * share
@@ -244,7 +242,14 @@
         axis=1,
     )
     coded = lax.dynamic_slice_in_dim(coded, start, share, axis=0)
-    gathered = lax.all_gather(coded, "space", axis=0, tiled=True)
+    peers = lax.axis_size("space")
+    spread_out = jnp.broadcast_to(coded[None], (peers,) + coded.shape).reshape(peers * share, -1)
+    gathered = lax.all_to_all(spread_out, "space", 0, 0, tiled=True)
+    return fold_interface(gathered, width, base)
+
+
+def fold_interface(gathered, width, base):
+    low = width // CELL_HI
     rows = gathered[:, :MOMENTS]
     cells = gathered[:, MOMENTS].astype(jnp.int32) * 256 + gathered[:, MOMENTS + 1].astype(jnp.int32)
     local = cells - base
@@ -307,9 +312,10 @@
         dist, left, right, ahead, behind, moment_basis(velocity, quad_weight)
     )
     slab_base = lax.axis_index("space") * cells
+    moments = sect_sum(partial_moments)
     partial_rows = interface_rows(plenum_moments, iface_cell, cells, slab_base)
-    summed = sect_sum(jnp.concatenate([partial_moments, partial_rows], axis=0))
-    targets = inject(es_targets(summed[:MOMENTS]), summed[MOMENTS:]).astype(jnp.bfloat16)
+    rows = sect_sum(partial_rows.astype(jnp.bfloat16)).astype(jnp.float32)
+    targets = inject(es_targets(moments), rows).astype(jnp.bfloat16)
     wall_moments = ghost_walls(targets, ghost_source, ghost_owner, wall_cell)
     recon = recon_basis(velocity)
     recon3 = jnp.concatenate([recon, recon, recon], axis=1)
@@ -332,6 +338,5 @@
         P("space"),
     )
     out_specs = P("sect", "space")
-    return jax.shard_map(
-        per_device, mesh=mesh, in_specs=in_specs, out_specs=out_specs, check_vma=False
-    )
+
+    return jax.shard_map(per_device, mesh=mesh, in_specs=in_specs, out_specs=out_specs, check_vma=False)

time: 146 us -> 119 us (0.82)
  blocking collectives: 26.3 us -> 0 us
  starting transfers between devices: 16.5 us -> 28 us
  local copies, waits for them, and re-layouts: 25.3 us -> 15.2 us
  other arithmetic: 18.2 us -> 15.8 us
    all_gather x1 -> x0, blocking collectives: 26.3 us -> none  [interface_rows(): gathered = lax.all_gather(coded, 'space', axis=0, tiled=True)]
    another operation x22, local copies, waits for them, and re-layouts: 14.9 us -> 3.92 us  [hermite(): return jnp.stack(stacked)]
    all_to_all x0 -> x1, starting transfers between devices: none -> 9.59 us  [interface_rows(): gathered = lax.all_to_all(spread_out, 'space', 0, 0, tiled=True)]
    all_to_all x1, starting transfers between devices: 5.75 us -> 7.73 us  [ghost_walls(): lax.all_to_all(outgoing, 'space', split_axis=1, concat_axis=1, tiled=True)]
    concatenate x2 -> x1, other arithmetic: 1.72 us -> 0.09 us  [fold_interface(): jnp.concatenate([rows, jnp.ones((rows.shape[0], 1), jnp.bfloat16)], axis=1)]
    ppermute x3 -> x6, waiting for transfers between devices: 16.6 us -> 18 us  [sect_sum(): total = total + lax.ppermute(values, 'sect', pairs)]
    unnamed x25 -> x33, local copies, waits for them, and re-layouts: 1.91 us -> 3.25 us
    ppermute x3 -> x6, starting transfers between devices: 4.29 us -> 5.14 us  [sect_sum(): total = total + lax.ppermute(values, 'sect', pairs)]
  transfers between devices with their start and end apart: 6 -> 10, of which waited for: 4 -> 6; matrix products, arithmetic and copies ran while one was open for 27% -> 19% of each run, Pallas kernels for 0% -> 11%
where the time goes in v3:
time: 119 us; the launch traced here: 118 us
  Pallas kernels  31.2 us (26%)
  starting transfers between devices  28 us (24%)
  waiting for transfers between devices  23.9 us (20%)
  other arithmetic  15.8 us (13%)
  local copies, waits for them, and re-layouts  15.2 us (13%)
  matrix products  3.33 us (3%)
    pallas_call x1, Pallas kernels, relax_call(): pl.pallas_call(relax_kernel, grid=(steps,), in_specs=[row_spec(cells), ro...  18.6 us
    ppermute x6, waiting for transfers between devices, sect_sum(): total = total + lax.ppermute(values, 'sect', pairs)  18 us
    pallas_call x1, Pallas kernels, moments_call(): pl.pallas_call(moments_kernel, grid=(steps,), in_specs=[row_spec(cells),...  12.6 us
    all_to_all x1, starting transfers between devices, interface_rows(): gathered = lax.all_to_all(spread_out, 'space', 0, 0, tiled=True)  9.59 us
    all_to_all x1, starting transfers between devices, ghost_walls(): lax.all_to_all(outgoing, 'space', split_axis=1, concat_axis=1, tiled=True)  7.73 us
    all_to_all x1, waiting for transfers between devices, ghost_walls(): lax.all_to_all(outgoing, 'space', split_axis=1, concat_axis=1, tiled=True)  5.87 us
    ppermute x6, starting transfers between devices, sect_sum(): total = total + lax.ppermute(values, 'sect', pairs)  5.14 us
    another operation x22, local copies, waits for them, and re-layouts, hermite(): return jnp.stack(stacked)  3.92 us
  transfers between devices with their start and end apart: 10, of which 6 were waited for; matrix products, arithmetic and copies ran while one was open for 19% of the time, Pallas kernels for 11%

profile of v3, /device:TPU:1, one launch (start us, length us, event | category | flops | bytes accessed | tf_op | source)
XLA Modules:
  0.0 117.9 jit_solution(15767782492808246030)
XLA Ops:
  0.0 0.7 fusion.52
  0.7 0.8 convert_element_type.82
  1.6 0.7 broadcast_in_dim.12
  2.3 9.6 %all-to-all-start = ((bf16[32,128,22]{1,2,0:T(8,128)(2,1)}), bf16[32,128,22]{1,2,0:T(8,128)(2,1)S(1)}, u32[]{:S(2)}, u32[]{:S(2)}) async-start(bf16[32,128,22]{1,2,0:T(8,128)(2,1)} %broadcast_in_dim.12), calls=%async_computation | async-start | bytes 393216 | tf_op jit(solution)/shard_map/all_to_all | solution.py:247
  11.9 2.3 %fusion.70 = (bf16[2000,1]{1,0:T(8,128)(2,1)}, bf16[2000,1]{1,0:T(8,128)(2,1)}) fusion(bf16[2000,2048]{1,0:T(8,128)(2,1)} %dist_ref.3), kind=kLoop, calls=%fused_computation.153 | loop fusion | bytes 16000 | tf_op jit(solution)/shard_map/slice | solution.py:61
  14.3 2.1 %collective-permute-start.1 = (bf16[2000,1]{1,0:T(8,128)(2,1)}, bf16[2000,1]{1,0:T(8,128)(2,1)S(1)}, u32[]{:S(2)}, u32[]{:S(2)}) collective-permute-start(bf16[2000,1]{1,0:T(8,128)(2,1)} %get-tuple-element.43), channel_id=1, source_target_pairs={{1,0},{2,1},{3,2},{4,3},{5,4},{6,5},{7,6},{8,7},{9,8},{10,9},{11,1... | collective-permute-start | bytes 12008 | tf_op jit(solution)/shard_map/ppermute | solution.py:61
  16.4 3.4 %collective-permute-start = (bf16[2000,1]{1,0:T(8,128)(2,1)}, bf16[2000,1]{1,0:T(8,128)(2,1)S(1)}, u32[]{:S(2)}, u32[]{:S(2)}) collective-permute-start(bf16[2000,1]{1,0:T(8,128)(2,1)} %get-tuple-element.44), channel_id=1, source_target_pairs={{0,1},{1,2},{2,3},{3,4},{4,5},{5,6},{6,7},{7,8},{8,9},{9,10},{10,1... | collective-permute-start | bytes 12008 | tf_op jit(solution)/shard_map/ppermute | solution.py:60
  19.8 0.8 stack.46
  20.7 0.6 broadcast.325
  21.3 1.7 %fusion.59 = (f32[2000]{0:T(1024)S(1)}, f32[1,2000]{1,0:T(1,128)S(1)}, f32[1,2000]{1,0:T(1,128)S(1)}, f32[1,2000]{1,0:T(1,128)S(1)}, f32[2000,1]{0,1:T(1,128)S(1...) fusion(f32[]{:T(128)} %broadcast.325, ...), kind=kLoop, calls=%fused_computation.142 | loop fusion | flops 46000 | bytes 144004 | tf_op jit(solution)/shard_map/sub | solution.py:76
  23.0 1.8 %fusion.56 = (f32[2000]{0:T(1024)S(1)}, f32[2000]{0:T(1024)S(1)}, f32[2000]{0:T(1024)S(1)}, f32[1,2000]{1,0:T(1,128)S(1)}, f32[2000]{0:T(1024)S(1)}, /*index=5*/...) fusion(f32[3,2000]{1,0:T(4,128)} %param.11, ...), kind=kLoop, calls=%fused_computation.136 | loop fusion | flops 40000 | bytes 168004 | tf_op jit(solution)/shard_map/sub | solution.py:71
  24.8 0.7 broadcast_add_fusion.4
  25.5 0.7 broadcast_multiply_fusion.1
  26.2 0.7 fusion.26
  26.9 0.6 reduce-window.6
  27.7 0.8 fusion.25
  28.5 0.7 multiply_add_fusion.9
  29.8 0.7 reduce.53
  31.3 1.0 stack.44
  33.0 0.7 fusion.22.basis_ref
  33.9 1.4 %copy.163.behind_ref = f32[2000,1]{1,0:T(8,128)} copy(f32[2000,1]{0,1:T(1,128)S(1)} %get-tuple-element.74) | data formatting | bytes 16000 | tf_op jit(solution)/shard_map/min | solution.py:309
  35.3 1.3 %copy.162.ahead_ref = f32[2000,1]{1,0:T(8,128)} copy(f32[2000,1]{0,1:T(1,128)S(1)} %get-tuple-element.79) | data formatting | bytes 16000 | tf_op jit(solution)/shard_map/max | solution.py:308
  36.7 0.8 copy-done.1
  37.4 0.8 copy-done.2
  38.2 12.6 %shard_map.100 = f32[20,2048]{1,0:T(8,128)} custom-call(bf16[2000,2048]{1,0:T(8,128)(2,1)} %dist_ref.3, bf16[2000,1]{1,0:T(8,128)(2,1)} %copy-done.2, bf16[2000,1]{1,0:T(8,128)(2,1)} %copy-done.1, f32[2000,1]{1,0:T(8,128)} %copy.162.ahead_ref, f32[2000,1]{1,0:T(8,128)} %copy.163.behind_ref, bf16[5,20,400]{2,1,0:T(8,128)(2,1)} %fusion.22.basis_ref), custom_call_target="tpu_custom_call" | custom-call | flops 196608000 | bytes 8355840 | tf_op jit(solution)/shard_map/pallas_call | solution.py:164
  50.8 2.5 %collective-permute-start.4 = (f32[20,2048]{1,0:T(8,128)}, f32[20,2048]{1,0:T(8,128)S(1)}, u32[]{:S(2)}, u32[]{:S(2)}) collective-permute-start(f32[20,2048]{1,0:T(8,128)} %shard_map.100), channel_id=1, source_target_pairs={{0,96},{32,0},{64,32},{96,64},{1,97},{33,1},{65,33},{97,65},{2,98}... | collective-permute-start | bytes 491528 | tf_op jit(solution)/shard_map/ppermute | solution.py:228
  53.3 0.5 collective-permute-start.3
  53.8 0.6 collective-permute-start.2
  54.4 7.6 %collective-permute-done.4 = f32[20,2048]{1,0:T(8,128)S(1)} collective-permute-done((f32[20,2048]{1,0:T(8,128)}, f32[20,2048]{1,0:T(8,128)S(1)}, u32[]{:S(2)}, u32[]{:S(2)}) %collective-permute-start.4) | collective-permute-done | bytes 163872 | tf_op jit(solution)/shard_map/ppermute | solution.py:228
  62.1 3.8 %collective-permute-done.2 = f32[20,2048]{1,0:T(8,128)S(1)} collective-permute-done((f32[20,2048]{1,0:T(8,128)}, f32[20,2048]{1,0:T(8,128)S(1)}, u32[]{:S(2)}, u32[]{:S(2)}) %collective-permute-start.2) | collective-permute-done | bytes 163872 | tf_op jit(solution)/shard_map/ppermute | solution.py:228
  65.9 1.0 add_add_fusion
  67.1 0.5 copy-done.3
  67.6 0.7 fusion.40
  68.4 0.7 and_select_fusion
  70.4 1.7 %fusion.12 = bf16[21,8,256]{2,0,1:T(8,128)(2,1)S(1)} fusion(bf16[8,21,4096]{2,1,0:T(8,128)(2,1)S(1)} %dot_general.14, s32[4096]{0:T(1024)} %bitcast.78), kind=kOutput, calls=%fused_computation.12 | convolution fusion | flops 353413120 | bytes 1478656 | tf_op jit(solution)/shard_map/dot_general | solution.py:263
  72.4 0.5 collective-permute-start.6
  73.0 0.9 collective-permute-start.5
  74.2 2.1 %collective-permute-done.7 = bf16[21,2048]{1,0:T(8,128)(2,1)S(1)} collective-permute-done((bf16[21,2048]{1,0:T(8,128)(2,1)S(1)}, bf16[21,2048]{1,0:T(8,128)(2,1)S(1)}, u32[]{:S(2)}, u32[]{:S(2)}) %collective-permute-start.7) | collective-permute-done | bytes 86048 | tf_op jit(solution)/shard_map/ppermute | solution.py:228
  76.3 1.1 collective-permute-done.6
  77.4 3.3 %collective-permute-done.5 = bf16[21,2048]{1,0:T(8,128)(2,1)S(1)} collective-permute-done((bf16[21,2048]{1,0:T(8,128)(2,1)S(1)}, bf16[21,2048]{1,0:T(8,128)(2,1)S(1)}, u32[]{:S(2)}, u32[]{:S(2)}) %collective-permute-start.5) | collective-permute-done | bytes 86048 | tf_op jit(solution)/shard_map/ppermute | solution.py:228
  80.9 0.8 fusion.15
  81.8 0.8 reshape.225
  82.6 7.7 %all-to-all-start.1 = ((bf16[32,2,160]{2,1,0:T(2,128)(2,1)}), bf16[32,2,160]{2,1,0:T(2,128)(2,1)S(1)}, u32[]{:S(2)}, u32[]{:S(2)}) async-start(bf16[32,2,160]{2,1,0:T(2,128)(2,1)} %reshape.225), calls=%async_computation.1 | async-start | bytes 65536 | tf_op jit(solution)/shard_map/all_to_all | solution.py:289
  90.3 1.2 %pad_maximum_fusion.recon3_ref = bf16[2000,60]{1,0:T(8,128)(2,1)} fusion(bf16[2000,20]{1,0:T(8,128)(2,1)S(1)} %fusion.16.recon_ref), kind=kLoop, calls=%fused_computation.19 | loop fusion | flops 720000 | bytes 320000 | tf_op jit(solution)/shard_map/concatenate | solution.py:321
  91.7 5.9 %all-to-all-done.1 = bf16[32,2,160]{2,1,0:T(2,128)(2,1)S(1)} async-done(((bf16[32,2,160]{2,1,0:T(2,128)(2,1)}), bf16[32,2,160]{2,1,0:T(2,128)(2,1)S(1)}, u32[]{:S(2)}, u32[]{:S(2)}) %all-to-all-start.1) | async-done | bytes 20512 | tf_op jit(solution)/shard_map/all_to_all | solution.py:289
  97.7 0.8 fusion.71
  98.6 0.7 pad_maximum_fusion.1.walls_ref
  99.3 18.6 %shard_map.101 = bf16[2000,2048]{1,0:T(8,128)(2,1)} custom-call(bf16[2000,2048]{1,0:T(8,128)(2,1)} %dist_ref.3, bf16[2000,1]{1,0:T(8,128)(2,1)} %copy-done.2, bf16[2000,1]{1,0:T(8,128)(2,1)} %copy-done.1, f32[2000,1]{1,0:T(8,128)} %copy.162.ahead_ref, f32[2000,1]{1,0:T(8,128)} %copy.163.behind_ref, bf16[2000,20]{1,0:T(8,128)(2,1)} %copy-done, ...), custom_call_target="tpu_custom_call" | custom-call | flops 704512000 | bytes 16384000 | tf_op jit(solution)/shard_map/pallas_call | solution.py:189
  (84 shorter events, 5.3 us)
Async XLA Ops:
  0.0 33.7 %copy-start.12 = (f32[20]{0:T(128)S(1)}, f32[20]{0:T(128)}, u32[]{:S(2)}) copy-start(f32[20]{0:T(128)} %constant.107) | copy-start | bytes 244
  2.3 65.9 %all-to-all-start = ((bf16[32,128,22]{1,2,0:T(8,128)(2,1)}), bf16[32,128,22]{1,2,0:T(8,128)(2,1)S(1)}, u32[]{:S(2)}, u32[]{:S(2)}) async-start(bf16[32,128,22]{1,2,0:T(8,128)(2,1)} %broadcast_in_dim.12), calls=%async_computation | async-start | bytes 393216 | tf_op jit(solution)/shard_map/all_to_all | solution.py:247
  14.3 22.4 %collective-permute-start.1 = (bf16[2000,1]{1,0:T(8,128)(2,1)}, bf16[2000,1]{1,0:T(8,128)(2,1)S(1)}, u32[]{:S(2)}, u32[]{:S(2)}) collective-permute-start(bf16[2000,1]{1,0:T(8,128)(2,1)} %get-tuple-element.43), channel_id=1, source_target_pairs={{1,0},{2,1},{3,2},{4,3},{5,4},{6,5},{7,6},{8,7},{9,8},{10,9},{11,1... | collective-permute-start | bytes 12008 | tf_op jit(solution)/shard_map/ppermute | solution.py:61
  16.4 20.3 %collective-permute-start = (bf16[2000,1]{1,0:T(8,128)(2,1)}, bf16[2000,1]{1,0:T(8,128)(2,1)S(1)}, u32[]{:S(2)}, u32[]{:S(2)}) collective-permute-start(bf16[2000,1]{1,0:T(8,128)(2,1)} %get-tuple-element.44), channel_id=1, source_target_pairs={{0,1},{1,2},{2,3},{3,4},{4,5},{5,6},{6,7},{7,8},{8,9},{9,10},{10,1... | collective-permute-start | bytes 12008 | tf_op jit(solution)/shard_map/ppermute | solution.py:60
  33.8 56.6 %copy-start = (bf16[2000,20]{1,0:T(8,128)(2,1)}, bf16[2000,20]{1,0:T(8,128)(2,1)S(1)}, u32[]{:S(2)}) copy-start(bf16[2000,20]{1,0:T(8,128)(2,1)S(1)} %fusion.16.recon_ref) | copy-start | bytes 240004
  36.6 32.5 %copy-start.11 = (pred[21]{0:T(512)(128)(4,1)S(1)}, pred[21]{0:T(512)(128)(4,1)}, u32[]{:S(2)}) copy-start(pred[21]{0:T(512)(128)(4,1)} %constant.102.clone.1) | copy-start | bytes 67
  36.6 0.8 copy-start.1
  37.4 0.8 copy-start.2
  50.8 11.3 %collective-permute-start.4 = (f32[20,2048]{1,0:T(8,128)}, f32[20,2048]{1,0:T(8,128)S(1)}, u32[]{:S(2)}, u32[]{:S(2)}) collective-permute-start(f32[20,2048]{1,0:T(8,128)} %shard_map.100), channel_id=1, source_target_pairs={{0,96},{32,0},{64,32},{96,64},{1,97},{33,1},{65,33},{97,65},{2,98}... | collective-permute-start | bytes 491528 | tf_op jit(solution)/shard_map/ppermute | solution.py:228
  53.3 8.8 %collective-permute-start.3 = (f32[20,2048]{1,0:T(8,128)}, f32[20,2048]{1,0:T(8,128)S(1)}, u32[]{:S(2)}, u32[]{:S(2)}) collective-permute-start(f32[20,2048]{1,0:T(8,128)} %shard_map.100), channel_id=1, source_target_pairs={{0,64},{32,96},{64,0},{96,32},{1,65},{33,97},{65,1},{97,33},{2,66}... | collective-permute-start | bytes 491528 | tf_op jit(solution)/shard_map/ppermute | solution.py:228
  53.8 12.1 %collective-permute-start.2 = (f32[20,2048]{1,0:T(8,128)}, f32[20,2048]{1,0:T(8,128)S(1)}, u32[]{:S(2)}, u32[]{:S(2)}) collective-permute-start(f32[20,2048]{1,0:T(8,128)} %shard_map.100), channel_id=1, source_target_pairs={{0,32},{32,64},{64,96},{96,0},{1,33},{33,65},{65,97},{97,1},{2,34}... | collective-permute-start | bytes 491528 | tf_op jit(solution)/shard_map/ppermute | solution.py:228
  66.9 0.7 copy-start.3
  69.9 4.0 %slice-start = ((f32[20,2048]{1,0:T(8,128)}), f32[4,2048]{1,0:T(4,128)S(1)}, s32[]{:S(2)}) async-start(f32[20,2048]{1,0:T(8,128)} %copy-done.3), calls=%async_computation.2 | async-start | bytes 65536 | tf_op jit(solution)/shard_map/slice | solution.py:95
  70.4 3.4 %copy-start.4 = (f32[20,2048]{1,0:T(8,128)S(1)}, f32[20,2048]{1,0:T(8,128)}, u32[]{:S(2)}) copy-start(f32[20,2048]{1,0:T(8,128)} %copy-done.3) | copy-start | bytes 491524
  70.4 3.5 %copy-start.6 = (f32[1,2048]{1,0:T(1,128)S(1)}, f32[1,2048]{1,0:T(1,128)}, u32[]{:S(2)}) copy-start(f32[1,2048]{1,0:T(1,128)} %get-tuple-element.48) | copy-start | bytes 24580
  70.4 3.5 %copy-start.7 = (f32[1,2048]{1,0:T(1,128)S(1)}, f32[1,2048]{1,0:T(1,128)}, u32[]{:S(2)}) copy-start(f32[1,2048]{1,0:T(1,128)} %get-tuple-element.59) | copy-start | bytes 24580
  70.4 3.5 %copy-start.8 = (f32[1,2048]{1,0:T(1,128)S(1)}, f32[1,2048]{1,0:T(1,128)}, u32[]{:S(2)}) copy-start(f32[1,2048]{1,0:T(1,128)} %get-tuple-element.60) | copy-start | bytes 24580
  70.4 3.5 %copy-start.9 = (f32[1,2048]{1,0:T(1,128)S(1)}, f32[1,2048]{1,0:T(1,128)}, u32[]{:S(2)}) copy-start(f32[1,2048]{1,0:T(1,128)} %get-tuple-element.61) | copy-start | bytes 24580
  70.4 21.1 %copy-start.10 = (s32[1,32,16]{1,2,0:T(8,128)S(1)}, s32[1,32,16]{1,2,0:T(8,128)}, u32[]{:S(2)}) copy-start(s32[1,32,16]{1,2,0:T(8,128)} %param.16) | copy-start | bytes 6148
  72.3 4.0 %collective-permute-start.7 = (bf16[21,2048]{1,0:T(8,128)(2,1)S(1)}, bf16[21,2048]{1,0:T(8,128)(2,1)S(1)}, u32[]{:S(2)}, u32[]{:S(2)}) collective-permute-start(bf16[21,2048]{1,0:T(8,128)(2,1)S(1)} %bitcast.70), channel_id=1, source_target_pairs={{0,96},{32,0},{64,32},{96,64},{1,97},{33,1},{65,33},{97,65},{2,98}... | collective-permute-start | bytes 258056 | tf_op jit(solution)/shard_map/ppermute | solution.py:228
  72.4 5.0 %collective-permute-start.6 = (bf16[21,2048]{1,0:T(8,128)(2,1)S(1)}, bf16[21,2048]{1,0:T(8,128)(2,1)S(1)}, u32[]{:S(2)}, u32[]{:S(2)}) collective-permute-start(bf16[21,2048]{1,0:T(8,128)(2,1)S(1)} %bitcast.71), channel_id=1, source_target_pairs={{0,64},{32,96},{64,0},{96,32},{1,65},{33,97},{65,1},{97,33},{2,66}... | collective-permute-start | bytes 258056 | tf_op jit(solution)/shard_map/ppermute | solution.py:228
  73.0 7.8 %collective-permute-start.5 = (bf16[21,2048]{1,0:T(8,128)(2,1)S(1)}, bf16[21,2048]{1,0:T(8,128)(2,1)S(1)}, u32[]{:S(2)}, u32[]{:S(2)}) collective-permute-start(bf16[21,2048]{1,0:T(8,128)(2,1)S(1)} %bitcast.72), channel_id=1, source_target_pairs={{0,32},{32,64},{64,96},{96,0},{1,33},{33,65},{65,97},{97,1},{2,34}... | collective-permute-start | bytes 258056 | tf_op jit(solution)/shard_map/ppermute | solution.py:228
  80.8 18.4 %copy-start.5 = (bf16[20,2048]{1,0:T(8,128)(2,1)}, bf16[20,2048]{1,0:T(8,128)(2,1)S(1)}, u32[]{:S(2)}) copy-start(bf16[20,2048]{1,0:T(8,128)(2,1)S(1)} %fusion.19.targets_ref) | copy-start | bytes 245764
  82.6 15.0 %all-to-all-start.1 = ((bf16[32,2,160]{2,1,0:T(2,128)(2,1)}), bf16[32,2,160]{2,1,0:T(2,128)(2,1)S(1)}, u32[]{:S(2)}, u32[]{:S(2)}) async-start(bf16[32,2,160]{2,1,0:T(2,128)(2,1)} %reshape.225), calls=%async_computation.1 | async-start | bytes 65536 | tf_op jit(solution)/shard_map/all_to_all | solution.py:289

commit v4 on v3

--- a/solution.py
+++ b/solution.py
@@ -115,7 +115,7 @@
 def transport_block(dist_ref, left_ref, right_ref, ahead_ref, behind_ref):
     centre = dist_ref[...].astype(jnp.float32)
     width = centre.shape[1]
-    column = lax.broadcasted_iota(jnp.int32, centre.shape, 1)
+    column = lax.broadcasted_iota(jnp.int32, (1, width), 1)
     left = jnp.where(
         column == 0, left_ref[...].astype(jnp.float32), pltpu.roll(centre, 1, 1)
     )
@@ -139,14 +139,11 @@
 
 
 def relax_kernel(
-    dist_ref, left_ref, right_ref, ahead_ref, behind_ref, recon_ref, recon3_ref, targets_ref,
-    walls_ref, rate_ref, out_ref,
+    dist_ref, left_ref, right_ref, ahead_ref, behind_ref, recon3_ref, gain_ref, keep_ref, out_ref,
 ):
     read = transport_block(dist_ref, left_ref, right_ref, ahead_ref, behind_ref).astype(jnp.float32)
-    equilibrium = jnp.dot(recon_ref[...], targets_ref[...], preferred_element_type=jnp.float32)
-    wall_half = jnp.dot(recon3_ref[...], walls_ref[...], preferred_element_type=jnp.float32)
-    rate = rate_ref[...]
-    out_ref[...] = (read + rate * (equilibrium - read) + wall_half).astype(out_ref.dtype)
+    gained = jnp.dot(recon3_ref[...], gain_ref[...], preferred_element_type=jnp.float32)
+    out_ref[...] = (read * keep_ref[...] + gained).astype(out_ref.dtype)
 
 
 def row_spec(width):
@@ -183,7 +180,7 @@
     )(dist, left, right, ahead, behind, blocks)
 
 
-def relax_call(dist, left, right, ahead, behind, recon, recon3, targets, walls, rate):
+def relax_call(dist, left, right, ahead, behind, recon3, gain, keep):
     rows, cells = dist.shape
     steps = rows // ROW_BLOCK
     return pl.pallas_call(
@@ -195,29 +192,28 @@
             row_spec(1),
             row_spec(1),
             row_spec(1),
-            row_spec(recon.shape[1]),
             row_spec(recon3.shape[1]),
-            full_spec(targets.shape),
-            full_spec(walls.shape),
-            full_spec(rate.shape),
+            full_spec(gain.shape),
+            full_spec(keep.shape),
         ],
         out_specs=row_spec(cells),
         out_shape=jax.ShapeDtypeStruct((rows, cells), jnp.bfloat16),
         compiler_params=pltpu.CompilerParams(dimension_semantics=("parallel",)),
         cost_estimate=pl.CostEstimate(
-            flops=2 * rows * cells * 80 + 12 * rows * cells,
+            flops=2 * rows * cells * 60 + 10 * rows * cells,
             bytes_accessed=rows * cells * 4,
             transcendentals=0,
         ),
-    )(dist, left, right, ahead, behind, recon, recon3, targets, walls, rate)
+    )(dist, left, right, ahead, behind, recon3, gain, keep)
 
 
 def split_three(values):
-    first = values.astype(jnp.bfloat16)
-    rest = values - first.astype(jnp.float32)
-    second = rest.astype(jnp.bfloat16)
-    third = (rest - second.astype(jnp.float32)).astype(jnp.bfloat16)
-    return jnp.concatenate([first, second, third], axis=0)
+    first = lax.reduce_precision(values, exponent_bits=8, mantissa_bits=7)
+    rest = values - first
+    second = lax.reduce_precision(rest, exponent_bits=8, mantissa_bits=7)
+    third = rest - second
+    parts = [first, second, third]
+    return jnp.concatenate([part.astype(jnp.bfloat16) for part in parts], axis=0)
 
 
 def sect_sum(values):
@@ -319,10 +315,9 @@
     wall_moments = ghost_walls(targets, ghost_source, ghost_owner, wall_cell)
     recon = recon_basis(velocity)
     recon3 = jnp.concatenate([recon, recon, recon], axis=1)
-    walls = split_three(WALL_SHARE * wall_moments)
-    return relax_call(
-        dist, left, right, ahead, behind, recon, recon3, targets, walls, collision_rate[None, :]
-    )
+    rate = collision_rate[None, :]
+    gain = split_three(rate * targets.astype(jnp.float32) + WALL_SHARE * wall_moments)
+    return relax_call(dist, left, right, ahead, behind, recon3, gain, 1.0 - rate)
 
 
 def solution(mesh):

time: 119 us -> 128 us (1.076)
  local copies, waits for them, and re-layouts: 15.2 us -> 25 us
  Pallas kernels: 31.2 us -> 28.2 us
  other arithmetic: 15.8 us -> 18.4 us
    another operation x22, local copies, waits for them, and re-layouts: 3.92 us -> 14.5 us  [hermite(): return jnp.stack(stacked)]
    pallas_call x1, Pallas kernels: 18.6 us -> 15.6 us  [relax_call(): pl.pallas_call(relax_kernel, grid=(steps,), in_specs=[row_spec(cells), ro...]
    unnamed x33 -> x19, local copies, waits for them, and re-layouts: 3.25 us -> 2.75 us
  transfers between devices with their start and end apart: 10 -> 10, of which waited for: 6 -> 6; matrix products, arithmetic and copies ran while one was open for 19% -> 28% of each run, Pallas kernels for 11% -> 10%
where the time goes in v4:
time: 128 us; the launch traced here: 127 us
  Pallas kernels  28.2 us (22%)
  starting transfers between devices  28 us (22%)
  local copies, waits for them, and re-layouts  25 us (20%)
  waiting for transfers between devices  24.6 us (19%)
  other arithmetic  18.4 us (14%)
  matrix products  2.6 us (2%)
    ppermute x6, waiting for transfers between devices, sect_sum(): total = total + lax.ppermute(values, 'sect', pairs)  18.1 us
    pallas_call x1, Pallas kernels, relax_call(): pl.pallas_call(relax_kernel, grid=(steps,), in_specs=[row_spec(cells), ro...  15.6 us
    another operation x22, local copies, waits for them, and re-layouts, hermite(): return jnp.stack(stacked)  14.5 us
    pallas_call x1, Pallas kernels, moments_call(): pl.pallas_call(moments_kernel, grid=(steps,), in_specs=[row_spec(cells),...  12.6 us
    all_to_all x1, starting transfers between devices, interface_rows(): gathered = lax.all_to_all(spread_out, 'space', 0, 0, tiled=True)  9.59 us
    all_to_all x1, starting transfers between devices, ghost_walls(): lax.all_to_all(outgoing, 'space', split_axis=1, concat_axis=1, tiled=True)  7.74 us
    all_to_all x1, waiting for transfers between devices, ghost_walls(): lax.all_to_all(outgoing, 'space', split_axis=1, concat_axis=1, tiled=True)  6.49 us
    ppermute x6, starting transfers between devices, sect_sum(): total = total + lax.ppermute(values, 'sect', pairs)  5.14 us
  transfers between devices with their start and end apart: 10, of which 6 were waited for; matrix products, arithmetic and copies ran while one was open for 28% of the time, Pallas kernels for 10%

profile of v4, /device:TPU:1, one launch (start us, length us, event | category | flops | bytes accessed | tf_op | source)
XLA Modules:
  0.0 127.1 jit_solution(15829390384523802385)
XLA Ops:
  0.0 0.7 fusion.53
  0.7 0.8 convert_element_type.80
  1.6 0.7 broadcast_in_dim.9
  2.3 9.6 %all-to-all-start = ((bf16[32,128,22]{1,2,0:T(8,128)(2,1)}), bf16[32,128,22]{1,2,0:T(8,128)(2,1)S(1)}, u32[]{:S(2)}, u32[]{:S(2)}) async-start(bf16[32,128,22]{1,2,0:T(8,128)(2,1)} %broadcast_in_dim.9), calls=%async_computation | async-start | bytes 393216 | tf_op jit(solution)/shard_map/all_to_all | solution.py:243
  11.9 1.4 %fusion.71 = (bf16[2000,1]{1,0:T(8,128)(2,1)S(1)}, bf16[2000,1]{1,0:T(8,128)(2,1)S(1)}) fusion(bf16[2000,2048]{1,0:T(8,128)(2,1)} %dist_ref.3), kind=kLoop, calls=%fused_computation.157 | loop fusion | bytes 16000 | tf_op jit(solution)/shard_map/slice | solution.py:61
  13.3 2.1 %collective-permute-start.1 = (bf16[2000,1]{1,0:T(8,128)(2,1)S(1)}, bf16[2000,1]{1,0:T(8,128)(2,1)S(1)}, u32[]{:S(2)}, u32[]{:S(2)}) collective-permute-start(bf16[2000,1]{1,0:T(8,128)(2,1)S(1)} %get-tuple-element.43), channel_id=1, source_target_pairs={{1,0},{2,1},{3,2},{4,3},{5,4},{6,5},{7,6},{8,7},{9,8},{10,9},{11,1... | collective-permute-start | bytes 12008 | tf_op jit(solution)/shard_map/ppermute | solution.py:61
  15.5 3.4 %collective-permute-start = (bf16[2000,1]{1,0:T(8,128)(2,1)S(1)}, bf16[2000,1]{1,0:T(8,128)(2,1)S(1)}, u32[]{:S(2)}, u32[]{:S(2)}) collective-permute-start(bf16[2000,1]{1,0:T(8,128)(2,1)S(1)} %get-tuple-element.44), channel_id=1, source_target_pairs={{0,1},{1,2},{2,3},{3,4},{4,5},{5,6},{6,7},{7,8},{8,9},{9,10},{10,1... | collective-permute-start | bytes 12008 | tf_op jit(solution)/shard_map/ppermute | solution.py:60
  18.9 0.8 stack.46
  20.3 2.2 %fusion.60 = (f32[2000]{0:T(1024)S(1)}, f32[1,2000]{1,0:T(1,128)S(1)}, f32[1,2000]{1,0:T(1,128)S(1)}, f32[1,2000]{1,0:T(1,128)S(1)}, f32[2000,1]{0,1:T(1,128)}, ...) fusion(f32[]{:T(128)} %broadcast.327, ...), kind=kLoop, calls=%fused_computation.146 | loop fusion | flops 46000 | bytes 144004 | tf_op jit(solution)/shard_map/sub | solution.py:76
  22.4 2.2 %fusion.57 = (f32[2000]{0:T(1024)S(1)}, f32[2000]{0:T(1024)S(1)}, f32[2000]{0:T(1024)S(1)}, f32[1,2000]{1,0:T(1,128)S(1)}, f32[2000]{0:T(1024)S(1)}, /*index=5*/...) fusion(f32[3,2000]{1,0:T(4,128)} %param.11, ...), kind=kLoop, calls=%fused_computation.140 | loop fusion | flops 40000 | bytes 168004 | tf_op jit(solution)/shard_map/sub | solution.py:71
  24.6 1.2 broadcast_add_fusion.4
  25.8 0.7 broadcast_multiply_fusion.1
  26.6 0.7 fusion.27
  28.1 0.8 fusion.26
  28.9 1.2 multiply_add_fusion.9
  30.3 0.7 stack.127
  31.0 0.7 stack.125
  32.4 0.7 stack.122
  35.1 0.7 stack.116
  35.8 0.7 stack.117
  36.5 0.7 stack.120
  37.8 0.7 stack.131
  40.5 1.0 stack.44
  41.9 0.7 fusion.17
  42.6 1.2 pad_maximum_fusion.recon3_ref
  43.8 2.6 %stack.114 = f32[20,5,400]{2,0,1:T(8,128)S(1)} concatenate(f32[1,5,400]{2,0,1:T(1,128)S(1)} %stack.45, f32[3,5,400]{2,0,1:T(4,128)S(1)} %copy.137, f32[1,5,400]{2,0,1:T(1,128)} %stack.116, f32[1,5,400]{2,0,1:T(1,128)} %stack.117, f32[1,5,400]{2,0,1:T(1,128)} %stack.118, f32[1,5,400]{2,0,1:T(1,128)} %stack.119, f32[1,5,400]{2,0,1:T(1,128)} %stack.120, f32[1,5,400]{2,0,1:T(1,128)} %stack.121, ...), dimensions={0} | concatenate | bytes 320000 | tf_op jit(solution)/shard_map/stack | solution.py:82
  47.1 0.8 select_reduce_fusion
  47.9 2.0 %copy.163.behind_ref = f32[2000,1]{1,0:T(8,128)} copy(f32[2000,1]{0,1:T(1,128)} %get-tuple-element.74) | data formatting | bytes 16000 | tf_op jit(solution)/shard_map/min | solution.py:305
  49.9 1.4 %copy.162.ahead_ref = f32[2000,1]{1,0:T(8,128)} copy(f32[2000,1]{0,1:T(1,128)S(1)} %copy-done.2) | data formatting | bytes 16000 | tf_op jit(solution)/shard_map/max | solution.py:304
  51.3 0.8 copy-done
  52.1 0.8 copy-done.1
  52.9 12.6 %shard_map.100 = f32[20,2048]{1,0:T(8,128)} custom-call(bf16[2000,2048]{1,0:T(8,128)(2,1)} %dist_ref.3, bf16[2000,1]{1,0:T(8,128)(2,1)} %copy-done.1, bf16[2000,1]{1,0:T(8,128)(2,1)} %copy-done, f32[2000,1]{1,0:T(8,128)} %copy.162.ahead_ref, f32[2000,1]{1,0:T(8,128)} %copy.163.behind_ref, bf16[5,20,400]{2,1,0:T(8,128)(2,1)} %fusion.23.basis_ref), custom_call_target="tpu_custom_call" | custom-call | flops 196608000 | bytes 8355840 | tf_op jit(solution)/shard_map/pallas_call | solution.py:161
  65.5 2.5 %collective-permute-start.4 = (f32[20,2048]{1,0:T(8,128)}, f32[20,2048]{1,0:T(8,128)S(1)}, u32[]{:S(2)}, u32[]{:S(2)}) collective-permute-start(f32[20,2048]{1,0:T(8,128)} %shard_map.100), channel_id=1, source_target_pairs={{0,96},{32,0},{64,32},{96,64},{1,97},{33,1},{65,33},{97,65},{2,98}... | collective-permute-start | bytes 491528 | tf_op jit(solution)/shard_map/ppermute | solution.py:224
  69.1 7.6 %collective-permute-done.4 = f32[20,2048]{1,0:T(8,128)S(1)} collective-permute-done((f32[20,2048]{1,0:T(8,128)}, f32[20,2048]{1,0:T(8,128)S(1)}, u32[]{:S(2)}, u32[]{:S(2)}) %collective-permute-start.4) | collective-permute-done | bytes 163872 | tf_op jit(solution)/shard_map/ppermute | solution.py:224
  76.7 3.8 %collective-permute-done.2 = f32[20,2048]{1,0:T(8,128)S(1)} collective-permute-done((f32[20,2048]{1,0:T(8,128)}, f32[20,2048]{1,0:T(8,128)S(1)}, u32[]{:S(2)}, u32[]{:S(2)}) %collective-permute-start.2) | collective-permute-done | bytes 163872 | tf_op jit(solution)/shard_map/ppermute | solution.py:224
  80.6 1.0 add_add_fusion
  83.4 1.0 fusion.13
  85.2 0.9 collective-permute-start.5
  86.4 2.1 %collective-permute-done.7 = bf16[21,2048]{1,0:T(8,128)(2,1)S(1)} collective-permute-done((bf16[21,2048]{1,0:T(8,128)(2,1)S(1)}, bf16[21,2048]{1,0:T(8,128)(2,1)S(1)}, u32[]{:S(2)}, u32[]{:S(2)}) %collective-permute-start.7) | collective-permute-done | bytes 86048 | tf_op jit(solution)/shard_map/ppermute | solution.py:224
  88.5 1.1 collective-permute-done.6
  89.6 3.3 %collective-permute-done.5 = bf16[21,2048]{1,0:T(8,128)(2,1)S(1)} collective-permute-done((bf16[21,2048]{1,0:T(8,128)(2,1)S(1)}, bf16[21,2048]{1,0:T(8,128)(2,1)S(1)}, u32[]{:S(2)}, u32[]{:S(2)}) %collective-permute-start.5) | collective-permute-done | bytes 86048 | tf_op jit(solution)/shard_map/ppermute | solution.py:224
  93.1 0.8 fusion.16
  94.0 0.8 reshape.227
  94.8 7.7 %all-to-all-start.1 = ((bf16[32,2,160]{2,1,0:T(2,128)(2,1)}), bf16[32,2,160]{2,1,0:T(2,128)(2,1)S(1)}, u32[]{:S(2)}, u32[]{:S(2)}) async-start(bf16[32,2,160]{2,1,0:T(2,128)(2,1)} %reshape.227), calls=%async_computation.1 | async-start | bytes 65536 | tf_op jit(solution)/shard_map/all_to_all | solution.py:285
  103.3 6.5 %all-to-all-done.1 = bf16[32,2,160]{2,1,0:T(2,128)(2,1)S(1)} async-done(((bf16[32,2,160]{2,1,0:T(2,128)(2,1)}), bf16[32,2,160]{2,1,0:T(2,128)(2,1)S(1)}, u32[]{:S(2)}, u32[]{:S(2)}) %all-to-all-start.1) | async-done | bytes 20512 | tf_op jit(solution)/shard_map/all_to_all | solution.py:285
  109.9 0.8 reduce-precision_convert_fusion.1
  110.8 0.8 pad_maximum_fusion.1.gain_ref
  111.5 15.6 %shard_map.101 = bf16[2000,2048]{1,0:T(8,128)(2,1)} custom-call(bf16[2000,2048]{1,0:T(8,128)(2,1)} %dist_ref.3, bf16[2000,1]{1,0:T(8,128)(2,1)} %copy-done.1, bf16[2000,1]{1,0:T(8,128)(2,1)} %copy-done, f32[2000,1]{1,0:T(8,128)} %copy.162.ahead_ref, f32[2000,1]{1,0:T(8,128)} %copy.163.behind_ref, bf16[2000,60]{1,0:T(8,128)(2,1)} %pad_maximum_fusion.recon3_ref, ...), custom_call_target="tpu_custom_call" | custom-call | flops 532480000 | bytes 16384000 | tf_op jit(solution)/shard_map/pallas_call | solution.py:186
  (70 shorter events, 13.2 us)
Async XLA Ops:
  2.3 79.5 %all-to-all-start = ((bf16[32,128,22]{1,2,0:T(8,128)(2,1)}), bf16[32,128,22]{1,2,0:T(8,128)(2,1)S(1)}, u32[]{:S(2)}, u32[]{:S(2)}) async-start(bf16[32,128,22]{1,2,0:T(8,128)(2,1)} %broadcast_in_dim.9), calls=%async_computation | async-start | bytes 393216 | tf_op jit(solution)/shard_map/all_to_all | solution.py:243
  13.3 38.0 %collective-permute-start.1 = (bf16[2000,1]{1,0:T(8,128)(2,1)S(1)}, bf16[2000,1]{1,0:T(8,128)(2,1)S(1)}, u32[]{:S(2)}, u32[]{:S(2)}) collective-permute-start(bf16[2000,1]{1,0:T(8,128)(2,1)S(1)} %get-tuple-element.43), channel_id=1, source_target_pairs={{1,0},{2,1},{3,2},{4,3},{5,4},{6,5},{7,6},{8,7},{9,8},{10,9},{11,1... | collective-permute-start | bytes 12008 | tf_op jit(solution)/shard_map/ppermute | solution.py:61
  15.5 35.8 %collective-permute-start = (bf16[2000,1]{1,0:T(8,128)(2,1)S(1)}, bf16[2000,1]{1,0:T(8,128)(2,1)S(1)}, u32[]{:S(2)}, u32[]{:S(2)}) collective-permute-start(bf16[2000,1]{1,0:T(8,128)(2,1)S(1)} %get-tuple-element.44), channel_id=1, source_target_pairs={{0,1},{1,2},{2,3},{3,4},{4,5},{5,6},{6,7},{7,8},{8,9},{9,10},{10,1... | collective-permute-start | bytes 12008 | tf_op jit(solution)/shard_map/ppermute | solution.py:60
  41.6 8.4 %copy-start.2 = (f32[2000,1]{0,1:T(1,128)S(1)}, f32[2000,1]{0,1:T(1,128)}, u32[]{:S(2)}) copy-start(f32[2000,1]{0,1:T(1,128)} %get-tuple-element.79) | copy-start | bytes 24004
  51.3 30.8 %copy-start.5 = (pred[21]{0:T(512)(128)(4,1)S(1)}, pred[21]{0:T(512)(128)(4,1)}, u32[]{:S(2)}) copy-start(pred[21]{0:T(512)(128)(4,1)} %constant.103.clone.1) | copy-start | bytes 67
  51.3 0.8 copy-start
  52.1 0.8 copy-start.1
  65.5 11.3 %collective-permute-start.4 = (f32[20,2048]{1,0:T(8,128)}, f32[20,2048]{1,0:T(8,128)S(1)}, u32[]{:S(2)}, u32[]{:S(2)}) collective-permute-start(f32[20,2048]{1,0:T(8,128)} %shard_map.100), channel_id=1, source_target_pairs={{0,96},{32,0},{64,32},{96,64},{1,97},{33,1},{65,33},{97,65},{2,98}... | collective-permute-start | bytes 491528 | tf_op jit(solution)/shard_map/ppermute | solution.py:224
  68.0 8.8 %collective-permute-start.3 = (f32[20,2048]{1,0:T(8,128)}, f32[20,2048]{1,0:T(8,128)S(1)}, u32[]{:S(2)}, u32[]{:S(2)}) collective-permute-start(f32[20,2048]{1,0:T(8,128)} %shard_map.100), channel_id=1, source_target_pairs={{0,64},{32,96},{64,0},{96,32},{1,65},{33,97},{65,1},{97,33},{2,66}... | collective-permute-start | bytes 491528 | tf_op jit(solution)/shard_map/ppermute | solution.py:224
  68.5 12.1 %collective-permute-start.2 = (f32[20,2048]{1,0:T(8,128)}, f32[20,2048]{1,0:T(8,128)S(1)}, u32[]{:S(2)}, u32[]{:S(2)}) collective-permute-start(f32[20,2048]{1,0:T(8,128)} %shard_map.100), channel_id=1, source_target_pairs={{0,32},{32,64},{64,96},{96,0},{1,33},{33,65},{65,97},{97,1},{2,34}... | collective-permute-start | bytes 491528 | tf_op jit(solution)/shard_map/ppermute | solution.py:224
  83.4 19.1 %copy-start.4 = (f32[2048]{0:T(1024)S(1)}, f32[2048]{0:T(1024)}, u32[]{:S(2)}) copy-start(f32[2048]{0:T(1024)} %param.13) | copy-start | bytes 24580
  83.4 19.7 %copy-start.3 = (s32[1,32,16]{1,2,0:T(8,128)S(1)}, s32[1,32,16]{1,2,0:T(8,128)}, u32[]{:S(2)}) copy-start(s32[1,32,16]{1,2,0:T(8,128)} %param.16) | copy-start | bytes 6148
  84.5 4.0 %collective-permute-start.7 = (bf16[21,2048]{1,0:T(8,128)(2,1)S(1)}, bf16[21,2048]{1,0:T(8,128)(2,1)S(1)}, u32[]{:S(2)}, u32[]{:S(2)}) collective-permute-start(bf16[21,2048]{1,0:T(8,128)(2,1)S(1)} %bitcast.70), channel_id=1, source_target_pairs={{0,96},{32,0},{64,32},{96,64},{1,97},{33,1},{65,33},{97,65},{2,98}... | collective-permute-start | bytes 258056 | tf_op jit(solution)/shard_map/ppermute | solution.py:224
  84.6 5.0 %collective-permute-start.6 = (bf16[21,2048]{1,0:T(8,128)(2,1)S(1)}, bf16[21,2048]{1,0:T(8,128)(2,1)S(1)}, u32[]{:S(2)}, u32[]{:S(2)}) collective-permute-start(bf16[21,2048]{1,0:T(8,128)(2,1)S(1)} %bitcast.71), channel_id=1, source_target_pairs={{0,64},{32,96},{64,0},{96,32},{1,65},{33,97},{65,1},{97,33},{2,66}... | collective-permute-start | bytes 258056 | tf_op jit(solution)/shard_map/ppermute | solution.py:224
  85.2 7.8 %collective-permute-start.5 = (bf16[21,2048]{1,0:T(8,128)(2,1)S(1)}, bf16[21,2048]{1,0:T(8,128)(2,1)S(1)}, u32[]{:S(2)}, u32[]{:S(2)}) collective-permute-start(bf16[21,2048]{1,0:T(8,128)(2,1)S(1)} %bitcast.72), channel_id=1, source_target_pairs={{0,32},{32,64},{64,96},{96,0},{1,33},{33,65},{65,97},{97,1},{2,34}... | collective-permute-start | bytes 258056 | tf_op jit(solution)/shard_map/ppermute | solution.py:224
  94.8 15.0 %all-to-all-start.1 = ((bf16[32,2,160]{2,1,0:T(2,128)(2,1)}), bf16[32,2,160]{2,1,0:T(2,128)(2,1)S(1)}, u32[]{:S(2)}, u32[]{:S(2)}) async-start(bf16[32,2,160]{2,1,0:T(2,128)(2,1)} %reshape.227), calls=%async_computation.1 | async-start | bytes 65536 | tf_op jit(solution)/shard_map/all_to_all | solution.py:285

commit v5 on v4

--- a/solution.py
+++ b/solution.py
@@ -62,24 +62,41 @@
     return before, after
 
 
+def hermite_tables():
+    factors = [[0, 0, 0]]
+    corrections = [[4, 4, 4]]
+    for i in range(3):
+        factors.append([i + 1, 0, 0])
+        corrections.append([4, 4, 4])
+    for i, j in ORDER_TWO:
+        factors.append([i + 1, j + 1, 0])
+        corrections.append([0 if i == j else 4, 4, 4])
+    for i, j, k in ORDER_THREE:
+        factors.append([i + 1, j + 1, k + 1])
+        corrections.append(
+            [k + 1 if i == j else 4, j + 1 if i == k else 4, i + 1 if j == k else 4]
+        )
+    return factors, corrections
+
+
 def hermite(velocity):
-    unity_row = jnp.ones_like(velocity[0])
-    stacked = [unity_row, velocity[0], velocity[1], velocity[2]]
-    for i, j in ORDER_TWO:
-        element = velocity[i] * velocity[j]
-        if i == j:
-            element = element - 1.0
-        stacked.append(element)
-    for i, j, k in ORDER_THREE:
-        element = velocity[i] * velocity[j] * velocity[k]
-        if i == j:
-            element = element - velocity[k]
-        if i == k:
-            element = element - velocity[j]
-        if j == k:
-            element = element - velocity[i]
-        stacked.append(element)
-    return jnp.stack(stacked)
+    factors, corrections = hermite_tables()
+    width = velocity.shape[1]
+    extended = jnp.concatenate(
+        [jnp.ones((1, width), jnp.float32), velocity, jnp.zeros((1, width), jnp.float32)], axis=0
+    )
+    rows = jnp.arange(5, dtype=jnp.int32)
+
+    def pick(column):
+        chosen = jnp.array(column, dtype=jnp.int32)
+        select = (chosen[:, None] == rows[None, :]).astype(jnp.float32)
+        return jnp.sum(select[:, :, None] * extended[None, :, :], axis=1)
+
+    first, second, third = [pick([f[n] for f in factors]) for n in range(3)]
+    element = first * second * third
+    for n in range(3):
+        element = element - pick([c[n] for c in corrections])
+    return element
 
 
 def moment_basis(velocity, weight):
@@ -112,7 +129,7 @@
     return jnp.stack(stacked)
 
 
-def transport_block(dist_ref, left_ref, right_ref, ahead_ref, behind_ref):
+def transport_block(dist_ref, left_ref, right_ref, courant_ref):
     centre = dist_ref[...].astype(jnp.float32)
     width = centre.shape[1]
     column = lax.broadcasted_iota(jnp.int32, (1, width), 1)
@@ -124,24 +141,25 @@
         right_ref[...].astype(jnp.float32),
         pltpu.roll(centre, width - 1, 1),
     )
-    ahead = ahead_ref[...]
-    behind = behind_ref[...]
+    courant = courant_ref[...]
+    ahead = jnp.maximum(courant, 0.0)
+    behind = jnp.minimum(courant, 0.0)
     return (centre - ahead * (centre - left) - behind * (right - centre)).astype(jnp.bfloat16)
 
 
-def moments_kernel(dist_ref, left_ref, right_ref, ahead_ref, behind_ref, basis_ref, out_ref):
+def moments_kernel(dist_ref, left_ref, right_ref, courant_ref, basis_ref, out_ref):
     @pl.when(pl.program_id(0) == 0)
     def _():
         out_ref[...] = jnp.zeros_like(out_ref)
 
-    read = transport_block(dist_ref, left_ref, right_ref, ahead_ref, behind_ref)
+    read = transport_block(dist_ref, left_ref, right_ref, courant_ref)
     out_ref[...] += jnp.dot(basis_ref[0], read, preferred_element_type=jnp.float32)
 
 
 def relax_kernel(
-    dist_ref, left_ref, right_ref, ahead_ref, behind_ref, recon3_ref, gain_ref, keep_ref, out_ref,
+    dist_ref, left_ref, right_ref, courant_ref, recon3_ref, gain_ref, keep_ref, out_ref,
 ):
-    read = transport_block(dist_ref, left_ref, right_ref, ahead_ref, behind_ref).astype(jnp.float32)
+    read = transport_block(dist_ref, left_ref, right_ref, courant_ref).astype(jnp.float32)
     gained = jnp.dot(recon3_ref[...], gain_ref[...], preferred_element_type=jnp.float32)
     out_ref[...] = (read * keep_ref[...] + gained).astype(out_ref.dtype)
 
@@ -154,7 +172,7 @@
     return pl.BlockSpec(shape, lambda i: (0,) * len(shape))
 
 
-def moments_call(dist, left, right, ahead, behind, basis):
+def moments_call(dist, left, right, courant, basis):
     rows, cells = dist.shape
     steps = rows // ROW_BLOCK
     blocks = basis.reshape(MOMENTS, steps, ROW_BLOCK).transpose(1, 0, 2)
@@ -163,7 +181,6 @@
         grid=(steps,),
         in_specs=[
             row_spec(cells),
-            row_spec(1),
             row_spec(1),
             row_spec(1),
             row_spec(1),
@@ -177,10 +194,10 @@
             bytes_accessed=rows * cells * 2 + MOMENTS * cells * 4,
             transcendentals=0,
         ),
-    )(dist, left, right, ahead, behind, blocks)
-
-
-def relax_call(dist, left, right, ahead, behind, recon3, gain, keep):
+    )(dist, left, right, courant, blocks)
+
+
+def relax_call(dist, left, right, courant, recon3, gain, keep):
     rows, cells = dist.shape
     steps = rows // ROW_BLOCK
     return pl.pallas_call(
@@ -188,7 +205,6 @@
         grid=(steps,),
         in_specs=[
             row_spec(cells),
-            row_spec(1),
             row_spec(1),
             row_spec(1),
             row_spec(1),
@@ -204,7 +220,7 @@
             bytes_accessed=rows * cells * 4,
             transcendentals=0,
         ),
-    )(dist, left, right, ahead, behind, recon3, gain, keep)
+    )(dist, left, right, courant, recon3, gain, keep)
 
 
 def split_three(values):
@@ -300,12 +316,10 @@
     iface_cell,
 ):
     cells = dist.shape[1]
-    courant = COURANT_SCALE * velocity[0]
-    ahead = jnp.maximum(courant, 0.0)[:, None]
-    behind = jnp.minimum(courant, 0.0)[:, None]
+    courant = (COURANT_SCALE * velocity[0])[:, None]
     left, right = halo_columns(dist)
     partial_moments = moments_call(
-        dist, left, right, ahead, behind, moment_basis(velocity, quad_weight)
+        dist, left, right, courant, moment_basis(velocity, quad_weight)
     )
     slab_base = lax.axis_index("space") * cells
     moments = sect_sum(partial_moments)
@@ -317,7 +331,7 @@
     recon3 = jnp.concatenate([recon, recon, recon], axis=1)
     rate = collision_rate[None, :]
     gain = split_three(rate * targets.astype(jnp.float32) + WALL_SHARE * wall_moments)
-    return relax_call(dist, left, right, ahead, behind, recon3, gain, 1.0 - rate)
+    return relax_call(dist, left, right, courant, recon3, gain, 1.0 - rate)
 
 
 def solution(mesh):

time: 128 us -> 112 us (0.88)
  local copies, waits for them, and re-layouts: 25 us -> 11.2 us
  other arithmetic: 18.4 us -> 16.9 us
    another operation x24 -> x1, local copies, waits for them, and re-layouts: 14.5 us -> 0.01 us  [the longest x22 14.5 us: hermite(): return jnp.stack(stacked)]
    sub x3 -> x1, other arithmetic: 4.96 us -> 0.6 us  [per_device(): return relax_call(dist, left, right, courant, recon3, gain, 1.0 - rate)]
    reduce_sum x0 -> x3, local copies, waits for them, and re-layouts: none -> 3.02 us  [pick(): return jnp.sum(select[:, :, None] * extended[None, :, :], axis=1)]
    min x1 -> x0, local copies, waits for them, and re-layouts: 2.03 us -> none  [per_device(): behind = jnp.minimum(courant, 0.0)[:, None]]
    convert_element_type x0 -> x3, other arithmetic: none -> 2.01 us  [pick(): select = (chosen[:, None] == rows[None, :]).astype(jnp.float32)]
    unnamed x19 -> x15, local copies, waits for them, and re-layouts: 2.75 us -> 1.16 us
    max x1 -> x0, local copies, waits for them, and re-layouts: 1.37 us -> none  [per_device(): ahead = jnp.maximum(courant, 0.0)[:, None]]
  transfers between devices with their start and end apart: 10 -> 10, of which waited for: 6 -> 6; matrix products, arithmetic and copies ran while one was open for 28% -> 20% of each run, Pallas kernels for 10% -> 11%
where the time goes in v5:
time: 112 us
  starting transfers between devices  28.2 us (25%)
  Pallas kernels  28.1 us (25%)
  waiting for transfers between devices  24.4 us (22%)
  other arithmetic  16.9 us (15%)
  local copies, waits for them, and re-layouts  11.2 us (10%)
  matrix products  2.59 us (2%)
    ppermute x6, waiting for transfers between devices, sect_sum(): total = total + lax.ppermute(values, 'sect', pairs)  17.9 us
    pallas_call x1, Pallas kernels, relax_call(): pl.pallas_call(relax_kernel, grid=(steps,), in_specs=[row_spec(cells), ro...  15.5 us
    pallas_call x1, Pallas kernels, moments_call(): pl.pallas_call(moments_kernel, grid=(steps,), in_specs=[row_spec(cells),...  12.7 us
    all_to_all x1, starting transfers between devices, interface_rows(): gathered = lax.all_to_all(spread_out, 'space', 0, 0, tiled=True)  9.59 us
    all_to_all x1, starting transfers between devices, ghost_walls(): lax.all_to_all(outgoing, 'space', split_axis=1, concat_axis=1, tiled=True)  7.89 us
    all_to_all x1, waiting for transfers between devices, ghost_walls(): lax.all_to_all(outgoing, 'space', split_axis=1, concat_axis=1, tiled=True)  6.49 us
    ppermute x6, starting transfers between devices, sect_sum(): total = total + lax.ppermute(values, 'sect', pairs)  5.14 us
    ppermute x1, starting transfers between devices, halo_columns(): before = lax.ppermute(shard[:, length - 1:], 'space', up)  3.42 us
  transfers between devices with their start and end apart: 10, of which 6 were waited for; matrix products, arithmetic and copies ran while one was open for 20% of the time, Pallas kernels for 11%

profile of v5, /device:TPU:1, one launch (start us, length us, event | category | flops | bytes accessed | tf_op | source)
XLA Modules:
  0.0 111.7 jit_solution(8454920981738329618)
XLA Ops:
  0.0 0.7 fusion.58
  0.7 0.8 convert_element_type.172
  1.6 0.7 broadcast_in_dim.9
  2.3 9.6 %all-to-all-start = ((bf16[32,128,22]{1,2,0:T(8,128)(2,1)}), bf16[32,128,22]{1,2,0:T(8,128)(2,1)S(1)}, u32[]{:S(2)}, u32[]{:S(2)}) async-start(bf16[32,128,22]{1,2,0:T(8,128)(2,1)} %broadcast_in_dim.9), calls=%async_computation | async-start | bytes 393216 | tf_op jit(solution)/shard_map/all_to_all | solution.py:259
  11.9 2.4 %fusion.61 = (bf16[2000,1]{1,0:T(8,128)(2,1)}, bf16[2000,1]{1,0:T(8,128)(2,1)}) fusion(bf16[2000,2048]{1,0:T(8,128)(2,1)} %dist_ref.3), kind=kLoop, calls=%fused_computation.142 | loop fusion | bytes 16000 | tf_op jit(solution)/shard_map/slice | solution.py:61
  14.3 2.1 %collective-permute-start.1 = (bf16[2000,1]{1,0:T(8,128)(2,1)}, bf16[2000,1]{1,0:T(8,128)(2,1)}, u32[]{:S(2)}, u32[]{:S(2)}) collective-permute-start(bf16[2000,1]{1,0:T(8,128)(2,1)} %get-tuple-element.22), channel_id=1, source_target_pairs={{1,0},{2,1},{3,2},{4,3},{5,4},{6,5},{7,6},{8,7},{9,8},{10,9},{11,1... | collective-permute-start | bytes 12008 | tf_op jit(solution)/shard_map/ppermute | solution.py:61
  16.4 3.4 %collective-permute-start = (bf16[2000,1]{1,0:T(8,128)(2,1)}, bf16[2000,1]{1,0:T(8,128)(2,1)}, u32[]{:S(2)}, u32[]{:S(2)}) collective-permute-start(bf16[2000,1]{1,0:T(8,128)(2,1)} %get-tuple-element.23), channel_id=1, source_target_pairs={{0,1},{1,2},{2,3},{3,4},{4,5},{5,6},{6,7},{7,8},{8,9},{9,10},{10,1... | collective-permute-start | bytes 12008 | tf_op jit(solution)/shard_map/ppermute | solution.py:60
  19.9 0.7 broadcast_add_fusion.1
  20.6 0.7 fusion.56
  21.3 0.7 broadcast_multiply_fusion.1
  22.1 0.8 multiply_bitcast_fusion
  22.8 0.7 fusion.27
  23.5 0.6 reduce-window.6
  24.3 0.8 fusion.26
  25.1 0.7 multiply_add_fusion.9
  25.8 0.7 fusion.52
  26.5 0.7 fusion.54
  27.1 0.8 maximum_maximum_fusion
  28.0 0.6 multiply_reduce_fusion.2
  29.3 1.3 %copy.65 = f32[20,2000]{0,1:T(8,128)} copy(f32[20,2000]{1,0:T(8,128)S(1)} %get-tuple-element.7) | data formatting | bytes 320000 | tf_op jit(solution)/shard_map/reduce_sum | solution.py:93
  30.7 1.3 %copy.66 = f32[20,2000]{0,1:T(8,128)} copy(f32[20,2000]{1,0:T(8,128)S(1)} %get-tuple-element.8) | data formatting | bytes 320000 | tf_op jit(solution)/shard_map/reduce_sum | solution.py:93
  32.0 1.7 %fusion.17 = (bf16[2000,20]{1,0:T(8,128)(2,1)S(1)}, f32[20,2000]{0,1:T(8,128)S(1)}) fusion(f32[20]{0:T(128)S(1)} %copy-done.3, f32[20,2000]{0,1:T(8,128)} %copy.66, f32[20,2000]{0,1:T(8,128)} %copy.65, f32[20,2000]{0,1:T(8,128)S(1)} %copy.63, f32[20,2000]{0,1:T(8,128)S(1)} %copy.64), kind=kLoop, calls=%fused_computation.25 | loop fusion | flops 240000 | bytes 880080 | tf_op jit(solution)/shard_map/convert_element_type | solution.py:108
  33.7 1.2 %pad_maximum_fusion.recon3_ref = bf16[2000,60]{1,0:T(8,128)(2,1)} fusion(bf16[2000,20]{1,0:T(8,128)(2,1)S(1)} %get-tuple-element.20), kind=kLoop, calls=%fused_computation.26 | loop fusion | flops 720000 | bytes 320000 | tf_op jit(solution)/shard_map/concatenate | solution.py:331
  35.4 0.7 fusion.23.basis_ref
  36.2 1.3 %copy.76.courant_ref = f32[2000,1]{1,0:T(8,128)} copy(f32[2000,1]{0,1:T(1,128)S(1)} %multiply_bitcast_fusion) | data formatting | bytes 16000 | tf_op jit(solution)/shard_map/mul | solution.py:319
  37.5 12.7 %shard_map.208 = f32[20,2048]{1,0:T(8,128)} custom-call(bf16[2000,2048]{1,0:T(8,128)(2,1)} %dist_ref.3, bf16[2000,1]{1,0:T(8,128)(2,1)} %collective-permute-done.left_ref, bf16[2000,1]{1,0:T(8,128)(2,1)} %collective-permute-done.1.right_ref, f32[2000,1]{1,0:T(8,128)} %copy.76.courant_ref, bf16[5,20,400]{2,1,0:T(8,128)(2,1)} %fusion.23.basis_ref), custom_call_target="tpu_custom_call" | custom-call | flops 196608000 | bytes 8355840 | tf_op jit(solution)/shard_map/pallas_call | solution.py:179
  50.2 2.5 %collective-permute-start.4 = (f32[20,2048]{1,0:T(8,128)}, f32[20,2048]{1,0:T(8,128)S(1)}, u32[]{:S(2)}, u32[]{:S(2)}) collective-permute-start(f32[20,2048]{1,0:T(8,128)} %shard_map.208), channel_id=1, source_target_pairs={{0,96},{32,0},{64,32},{96,64},{1,97},{33,1},{65,33},{97,65},{2,98}... | collective-permute-start | bytes 491528 | tf_op jit(solution)/shard_map/ppermute | solution.py:240
  52.7 0.5 collective-permute-start.3
  53.2 0.6 collective-permute-start.2
  53.8 7.7 %collective-permute-done.4 = f32[20,2048]{1,0:T(8,128)S(1)} collective-permute-done((f32[20,2048]{1,0:T(8,128)}, f32[20,2048]{1,0:T(8,128)S(1)}, u32[]{:S(2)}, u32[]{:S(2)}) %collective-permute-start.4) | collective-permute-done | bytes 163872 | tf_op jit(solution)/shard_map/ppermute | solution.py:240
  61.5 3.9 %collective-permute-done.2 = f32[20,2048]{1,0:T(8,128)S(1)} collective-permute-done((f32[20,2048]{1,0:T(8,128)}, f32[20,2048]{1,0:T(8,128)S(1)}, u32[]{:S(2)}, u32[]{:S(2)}) %collective-permute-start.2) | collective-permute-done | bytes 163872 | tf_op jit(solution)/shard_map/ppermute | solution.py:240
  65.4 1.0 add_add_fusion
  67.3 0.5 mul.500
  67.8 0.4 dot_general.14
  68.3 1.0 fusion.13
  69.4 0.6 collective-permute-start.6
  70.0 0.9 collective-permute-start.5
  71.2 2.1 %collective-permute-done.7 = bf16[21,2048]{1,0:T(8,128)(2,1)S(1)} collective-permute-done((bf16[21,2048]{1,0:T(8,128)(2,1)S(1)}, bf16[21,2048]{1,0:T(8,128)(2,1)S(1)}, u32[]{:S(2)}, u32[]{:S(2)}) %collective-permute-start.7) | collective-permute-done | bytes 86048 | tf_op jit(solution)/shard_map/ppermute | solution.py:240
  73.3 1.2 %collective-permute-done.6 = bf16[21,2048]{1,0:T(8,128)(2,1)S(1)} collective-permute-done((bf16[21,2048]{1,0:T(8,128)(2,1)S(1)}, bf16[21,2048]{1,0:T(8,128)(2,1)S(1)}, u32[]{:S(2)}, u32[]{:S(2)}) %collective-permute-start.6) | collective-permute-done | bytes 86048 | tf_op jit(solution)/shard_map/ppermute | solution.py:240
  74.5 3.0 %collective-permute-done.5 = bf16[21,2048]{1,0:T(8,128)(2,1)S(1)} collective-permute-done((bf16[21,2048]{1,0:T(8,128)(2,1)S(1)}, bf16[21,2048]{1,0:T(8,128)(2,1)S(1)}, u32[]{:S(2)}, u32[]{:S(2)}) %collective-permute-start.5) | collective-permute-done | bytes 86048 | tf_op jit(solution)/shard_map/ppermute | solution.py:240
  77.6 0.8 fusion.16
  78.5 0.8 reshape.365
  79.3 7.9 %all-to-all-start.1 = ((bf16[32,2,160]{2,1,0:T(2,128)(2,1)}), bf16[32,2,160]{2,1,0:T(2,128)(2,1)S(1)}, u32[]{:S(2)}, u32[]{:S(2)}) async-start(bf16[32,2,160]{2,1,0:T(2,128)(2,1)} %reshape.365), calls=%async_computation.1 | async-start | bytes 65536 | tf_op jit(solution)/shard_map/all_to_all | solution.py:301
  87.2 0.6 broadcast_subtract_fusion
  88.0 6.5 %all-to-all-done.1 = bf16[32,2,160]{2,1,0:T(2,128)(2,1)S(1)} async-done(((bf16[32,2,160]{2,1,0:T(2,128)(2,1)}), bf16[32,2,160]{2,1,0:T(2,128)(2,1)S(1)}, u32[]{:S(2)}, u32[]{:S(2)}) %all-to-all-start.1) | async-done | bytes 20512 | tf_op jit(solution)/shard_map/all_to_all | solution.py:301
  94.6 0.8 reduce-precision_convert_fusion.1
  95.5 0.8 pad_maximum_fusion.1.gain_ref
  96.2 15.5 %shard_map.209 = bf16[2000,2048]{1,0:T(8,128)(2,1)} custom-call(bf16[2000,2048]{1,0:T(8,128)(2,1)} %dist_ref.3, bf16[2000,1]{1,0:T(8,128)(2,1)} %collective-permute-done.left_ref, bf16[2000,1]{1,0:T(8,128)(2,1)} %collective-permute-done.1.right_ref, f32[2000,1]{1,0:T(8,128)} %copy.76.courant_ref, bf16[2000,60]{1,0:T(8,128)(2,1)} %pad_maximum_fusion.recon3_ref, ...), custom_call_target="tpu_custom_call" | custom-call | flops 532480000 | bytes 16384000 | tf_op jit(solution)/shard_map/pallas_call | solution.py:203
  (52 shorter events, 3.6 us)
Async XLA Ops:
  2.3 64.4 %all-to-all-start = ((bf16[32,128,22]{1,2,0:T(8,128)(2,1)}), bf16[32,128,22]{1,2,0:T(8,128)(2,1)S(1)}, u32[]{:S(2)}, u32[]{:S(2)}) async-start(bf16[32,128,22]{1,2,0:T(8,128)(2,1)} %broadcast_in_dim.9), calls=%async_computation | async-start | bytes 393216 | tf_op jit(solution)/shard_map/all_to_all | solution.py:259
  11.9 20.1 %copy-start.3 = (f32[20]{0:T(128)S(1)}, f32[20]{0:T(128)}, u32[]{:S(2)}) copy-start(f32[20]{0:T(128)} %constant.119) | copy-start | bytes 244
  14.3 23.3 %collective-permute-start.1 = (bf16[2000,1]{1,0:T(8,128)(2,1)}, bf16[2000,1]{1,0:T(8,128)(2,1)}, u32[]{:S(2)}, u32[]{:S(2)}) collective-permute-start(bf16[2000,1]{1,0:T(8,128)(2,1)} %get-tuple-element.22), channel_id=1, source_target_pairs={{1,0},{2,1},{3,2},{4,3},{5,4},{6,5},{7,6},{8,7},{9,8},{10,9},{11,1... | collective-permute-start | bytes 12008 | tf_op jit(solution)/shard_map/ppermute | solution.py:61
  16.4 21.1 %collective-permute-start = (bf16[2000,1]{1,0:T(8,128)(2,1)}, bf16[2000,1]{1,0:T(8,128)(2,1)}, u32[]{:S(2)}, u32[]{:S(2)}) collective-permute-start(bf16[2000,1]{1,0:T(8,128)(2,1)} %get-tuple-element.23), channel_id=1, source_target_pairs={{0,1},{1,2},{2,3},{3,4},{4,5},{5,6},{6,7},{7,8},{8,9},{9,10},{10,1... | collective-permute-start | bytes 12008 | tf_op jit(solution)/shard_map/ppermute | solution.py:60
  37.5 29.4 %copy-start.2 = (pred[21]{0:T(512)(128)(4,1)S(1)}, pred[21]{0:T(512)(128)(4,1)}, u32[]{:S(2)}) copy-start(pred[21]{0:T(512)(128)(4,1)} %constant.109.clone.1) | copy-start | bytes 67
  50.2 11.3 %collective-permute-start.4 = (f32[20,2048]{1,0:T(8,128)}, f32[20,2048]{1,0:T(8,128)S(1)}, u32[]{:S(2)}, u32[]{:S(2)}) collective-permute-start(f32[20,2048]{1,0:T(8,128)} %shard_map.208), channel_id=1, source_target_pairs={{0,96},{32,0},{64,32},{96,64},{1,97},{33,1},{65,33},{97,65},{2,98}... | collective-permute-start | bytes 491528 | tf_op jit(solution)/shard_map/ppermute | solution.py:240
  52.7 8.9 %collective-permute-start.3 = (f32[20,2048]{1,0:T(8,128)}, f32[20,2048]{1,0:T(8,128)S(1)}, u32[]{:S(2)}, u32[]{:S(2)}) collective-permute-start(f32[20,2048]{1,0:T(8,128)} %shard_map.208), channel_id=1, source_target_pairs={{0,64},{32,96},{64,0},{96,32},{1,65},{33,97},{65,1},{97,33},{2,66}... | collective-permute-start | bytes 491528 | tf_op jit(solution)/shard_map/ppermute | solution.py:240
  53.2 12.3 %collective-permute-start.2 = (f32[20,2048]{1,0:T(8,128)}, f32[20,2048]{1,0:T(8,128)S(1)}, u32[]{:S(2)}, u32[]{:S(2)}) collective-permute-start(f32[20,2048]{1,0:T(8,128)} %shard_map.208), channel_id=1, source_target_pairs={{0,32},{32,64},{64,96},{96,0},{1,33},{33,65},{65,97},{97,1},{2,34}... | collective-permute-start | bytes 491528 | tf_op jit(solution)/shard_map/ppermute | solution.py:240
  68.3 19.0 %copy-start.1 = (f32[2048]{0:T(1024)S(1)}, f32[2048]{0:T(1024)}, u32[]{:S(2)}) copy-start(f32[2048]{0:T(1024)} %param.25) | copy-start | bytes 24580
  68.3 19.6 %copy-start = (s32[1,32,16]{1,2,0:T(8,128)S(1)}, s32[1,32,16]{1,2,0:T(8,128)}, u32[]{:S(2)}) copy-start(s32[1,32,16]{1,2,0:T(8,128)} %param.28) | copy-start | bytes 6148
  69.3 4.0 %collective-permute-start.7 = (bf16[21,2048]{1,0:T(8,128)(2,1)S(1)}, bf16[21,2048]{1,0:T(8,128)(2,1)S(1)}, u32[]{:S(2)}, u32[]{:S(2)}) collective-permute-start(bf16[21,2048]{1,0:T(8,128)(2,1)S(1)} %bitcast.72), channel_id=1, source_target_pairs={{0,96},{32,0},{64,32},{96,64},{1,97},{33,1},{65,33},{97,65},{2,98}... | collective-permute-start | bytes 258056 | tf_op jit(solution)/shard_map/ppermute | solution.py:240
  69.4 5.1 %collective-permute-start.6 = (bf16[21,2048]{1,0:T(8,128)(2,1)S(1)}, bf16[21,2048]{1,0:T(8,128)(2,1)S(1)}, u32[]{:S(2)}, u32[]{:S(2)}) collective-permute-start(bf16[21,2048]{1,0:T(8,128)(2,1)S(1)} %bitcast.73), channel_id=1, source_target_pairs={{0,64},{32,96},{64,0},{96,32},{1,65},{33,97},{65,1},{97,33},{2,66}... | collective-permute-start | bytes 258056 | tf_op jit(solution)/shard_map/ppermute | solution.py:240
  70.0 7.5 %collective-permute-start.5 = (bf16[21,2048]{1,0:T(8,128)(2,1)S(1)}, bf16[21,2048]{1,0:T(8,128)(2,1)S(1)}, u32[]{:S(2)}, u32[]{:S(2)}) collective-permute-start(bf16[21,2048]{1,0:T(8,128)(2,1)S(1)} %bitcast.74), channel_id=1, source_target_pairs={{0,32},{32,64},{64,96},{96,0},{1,33},{33,65},{65,97},{97,1},{2,34}... | collective-permute-start | bytes 258056 | tf_op jit(solution)/shard_map/ppermute | solution.py:240
  79.3 15.2 %all-to-all-start.1 = ((bf16[32,2,160]{2,1,0:T(2,128)(2,1)}), bf16[32,2,160]{2,1,0:T(2,128)(2,1)S(1)}, u32[]{:S(2)}, u32[]{:S(2)}) async-start(bf16[32,2,160]{2,1,0:T(2,128)(2,1)} %reshape.365), calls=%async_computation.1 | async-start | bytes 65536 | tf_op jit(solution)/shard_map/all_to_all | solution.py:301

commit v6 on v5

--- a/solution.py
+++ b/solution.py
@@ -147,13 +147,12 @@
     return (centre - ahead * (centre - left) - behind * (right - centre)).astype(jnp.bfloat16)
 
 
-def moments_kernel(dist_ref, left_ref, right_ref, courant_ref, basis_ref, out_ref):
+def moments_kernel(dist_ref, basis_ref, out_ref):
     @pl.when(pl.program_id(0) == 0)
     def _():
         out_ref[...] = jnp.zeros_like(out_ref)
 
-    read = transport_block(dist_ref, left_ref, right_ref, courant_ref)
-    out_ref[...] += jnp.dot(basis_ref[0], read, preferred_element_type=jnp.float32)
+    out_ref[...] += jnp.dot(basis_ref[0], dist_ref[...], preferred_element_type=jnp.float32)
 
 
 def relax_kernel(
@@ -172,29 +171,43 @@
     return pl.BlockSpec(shape, lambda i: (0,) * len(shape))
 
 
-def moments_call(dist, left, right, courant, basis):
+def moments_call(dist, basis):
     rows, cells = dist.shape
     steps = rows // ROW_BLOCK
-    blocks = basis.reshape(MOMENTS, steps, ROW_BLOCK).transpose(1, 0, 2)
+    height = basis.shape[0]
+    blocks = basis.reshape(height, steps, ROW_BLOCK).transpose(1, 0, 2)
     return pl.pallas_call(
         moments_kernel,
         grid=(steps,),
         in_specs=[
             row_spec(cells),
-            row_spec(1),
-            row_spec(1),
-            row_spec(1),
-            pl.BlockSpec((1, MOMENTS, ROW_BLOCK), lambda i: (i, 0, 0)),
+            pl.BlockSpec((1, height, ROW_BLOCK), lambda i: (i, 0, 0)),
         ],
-        out_specs=full_spec((MOMENTS, cells)),
-        out_shape=jax.ShapeDtypeStruct((MOMENTS, cells), jnp.float32),
+        out_specs=full_spec((height, cells)),
+        out_shape=jax.ShapeDtypeStruct((height, cells), jnp.float32),
         compiler_params=pltpu.CompilerParams(dimension_semantics=("arbitrary",)),
         cost_estimate=pl.CostEstimate(
-            flops=2 * rows * cells * MOMENTS + 8 * rows * cells,
-            bytes_accessed=rows * cells * 2 + MOMENTS * cells * 4,
+            flops=2 * rows * cells * height,
+            bytes_accessed=rows * cells * 2 + height * cells * 4,
             transcendentals=0,
         ),
-    )(dist, left, right, courant, blocks)
+    )(dist, blocks)
+
+
+def stencil_moments(dist, left, right, courant, basis):
+    ahead = jnp.maximum(courant[:, 0], 0.0)
+    behind = jnp.minimum(courant[:, 0], 0.0)
+    weights = basis.astype(jnp.float32)
+    stencil = [weights * (1.0 - ahead + behind)[None, :], weights * ahead[None, :], -weights * behind[None, :]]
+    stacked = split_three(jnp.concatenate(stencil, axis=0))
+    products = moments_call(dist, stacked)
+    parts = products.reshape(3, 3, MOMENTS, dist.shape[1])
+    parts = (parts[0] + parts[1]) + parts[2]
+    edge_left = jnp.sum(stencil[1] * left[:, 0].astype(jnp.float32)[None, :], axis=1)
+    edge_right = jnp.sum(stencil[2] * right[:, 0].astype(jnp.float32)[None, :], axis=1)
+    from_left = jnp.concatenate([edge_left[:, None], parts[1][:, :-1]], axis=1)
+    from_right = jnp.concatenate([parts[2][:, 1:], edge_right[:, None]], axis=1)
+    return (parts[0] + from_left) + from_right
 
 
 def relax_call(dist, left, right, courant, recon3, gain, keep):
@@ -318,7 +331,7 @@
     cells = dist.shape[1]
     courant = (COURANT_SCALE * velocity[0])[:, None]
     left, right = halo_columns(dist)
-    partial_moments = moments_call(
+    partial_moments = stencil_moments(
         dist, left, right, courant, moment_basis(velocity, quad_weight)
     )
     slab_base = lax.axis_index("space") * cells

time: 112 us -> 113 us (level)
  Pallas kernels: 28.1 us -> 22.8 us
  local copies, waits for them, and re-layouts: 11.2 us -> 16.4 us
    pallas_call x1, Pallas kernels: 12.7 us -> 7.3 us  [moments_call(): pl.pallas_call(moments_kernel, grid=(steps,), in_specs=[row_spec(cells),...]
    reduce_sum x0 -> x1, other arithmetic: none -> 3.54 us  [stencil_moments(): jnp.sum(stencil[2] * right[:, 0].astype(jnp.float32)[None, :], axis=1)]
    add x0 -> x3, other arithmetic: none -> 2.87 us  [the longest x1 1.47 us: stencil_moments(): parts = parts[0] + parts[1] + parts[2]]
    convert_element_type x3, other arithmetic: 2.01 us -> 0.01 us  [pick(): select = (chosen[:, None] == rows[None, :]).astype(jnp.float32)]
    convert_element_type x1, other arithmetic: 1.75 us -> 0.06 us  [recon_basis(): return (hermite(velocity) / norms[:, None]).T.astype(jnp.bfloat16)]
    unnamed x15 -> x47, local copies, waits for them, and re-layouts: 1.16 us -> 2.3 us
  transfers between devices with their start and end apart: 10 -> 10, of which waited for: 6 -> 6; matrix products, arithmetic and copies ran while one was open for 20% -> 22% of each run, Pallas kernels for 11% -> 7%
where the time goes in v6:
time: 113 us; the launch traced here: 112 us
  starting transfers between devices  28 us (25%)
  waiting for transfers between devices  24 us (21%)
  Pallas kernels  22.8 us (20%)
  other arithmetic  16.7 us (15%)
  local copies, waits for them, and re-layouts  16.4 us (15%)
  matrix products  3.34 us (3%)
    ppermute x6, waiting for transfers between devices, sect_sum(): total = total + lax.ppermute(values, 'sect', pairs)  17.9 us
    pallas_call x1, Pallas kernels, relax_call(): pl.pallas_call(relax_kernel, grid=(steps,), in_specs=[row_spec(cells), ro...  15.5 us
    all_to_all x1, starting transfers between devices, interface_rows(): gathered = lax.all_to_all(spread_out, 'space', 0, 0, tiled=True)  9.64 us
    all_to_all x1, starting transfers between devices, ghost_walls(): lax.all_to_all(outgoing, 'space', split_axis=1, concat_axis=1, tiled=True)  7.59 us
    pallas_call x1, Pallas kernels, moments_call(): pl.pallas_call(moments_kernel, grid=(steps,), in_specs=[row_spec(cells),...  7.3 us
    all_to_all x1, waiting for transfers between devices, ghost_walls(): lax.all_to_all(outgoing, 'space', split_axis=1, concat_axis=1, tiled=True)  6.04 us
    ppermute x6, starting transfers between devices, sect_sum(): total = total + lax.ppermute(values, 'sect', pairs)  5.22 us
    reduce_sum x3, local copies, waits for them, and re-layouts, pick(): return jnp.sum(select[:, :, None] * extended[None, :, :], axis=1)  3.98 us
  transfers between devices with their start and end apart: 10, of which 6 were waited for; matrix products, arithmetic and copies ran while one was open for 22% of the time, Pallas kernels for 7%

profile of v6, /device:TPU:1, one launch (start us, length us, event | category | flops | bytes accessed | tf_op | source)
XLA Modules:
  0.0 111.9 jit_solution(9558759562095714005)
XLA Ops:
  0.1 0.7 fusion.65
  0.9 0.8 convert_element_type.226
  1.7 0.7 broadcast_in_dim.15
  2.4 9.6 %all-to-all-start = ((bf16[32,128,22]{1,2,0:T(8,128)(2,1)}), bf16[32,128,22]{1,2,0:T(8,128)(2,1)}, u32[]{:S(2)}, u32[]{:S(2)}) async-start(bf16[32,128,22]{1,2,0:T(8,128)(2,1)} %broadcast_in_dim.15), calls=%async_computation | async-start | bytes 393216 | tf_op jit(solution)/shard_map/all_to_all | solution.py:272
  12.1 2.4 %fusion.69 = (bf16[2000,1]{1,0:T(8,128)(2,1)}, bf16[2000,1]{1,0:T(8,128)(2,1)}) fusion(bf16[2000,2048]{1,0:T(8,128)(2,1)} %dist_ref.3), kind=kLoop, calls=%fused_computation.170 | loop fusion | bytes 16000 | tf_op jit(solution)/shard_map/slice | solution.py:61
  14.5 2.2 %collective-permute-start.1 = (bf16[2000,1]{1,0:T(8,128)(2,1)}, bf16[2000,1]{1,0:T(8,128)(2,1)S(1)}, u32[]{:S(2)}, u32[]{:S(2)}) collective-permute-start(bf16[2000,1]{1,0:T(8,128)(2,1)} %get-tuple-element.30), channel_id=1, source_target_pairs={{1,0},{2,1},{3,2},{4,3},{5,4},{6,5},{7,6},{8,7},{9,8},{10,9},{11,1... | collective-permute-start | bytes 12008 | tf_op jit(solution)/shard_map/ppermute | solution.py:61
  16.7 3.4 %collective-permute-start = (bf16[2000,1]{1,0:T(8,128)(2,1)}, bf16[2000,1]{1,0:T(8,128)(2,1)S(1)}, u32[]{:S(2)}, u32[]{:S(2)}) collective-permute-start(bf16[2000,1]{1,0:T(8,128)(2,1)} %get-tuple-element.31), channel_id=1, source_target_pairs={{0,1},{1,2},{2,3},{3,4},{4,5},{5,6},{6,7},{7,8},{8,9},{9,10},{10,1... | collective-permute-start | bytes 12008 | tf_op jit(solution)/shard_map/ppermute | solution.py:60
  20.1 0.6 broadcast_subtract_fusion
  20.7 0.6 reduce-window.6
  21.8 0.6 broadcast_add_fusion
  22.5 0.5 broadcast.442
  23.0 1.3 %add_reduce_fusion = (f32[2000]{0:T(1024)S(1)}, f32[2000]{0:T(1024)S(1)}, f32[2000]{0:T(1024)S(1)}, f32[1,2000]{1,0:T(1,128)S(1)}, f32[1,2000]{1,0:T(1,128)S(1)}, /*index=5*/f32[2000,1]{0,1:T(1,128)}) fusion(f32[]{:T(128)} %broadcast.442, f32[3,2000]{1,0:T(4,128)S(1)} %copy-done.4), kind=kLoop, calls=%fused_computation.138 | loop fusion | flops 10000 | bytes 56004 | tf_op jit(solution)/shard_map/add | solution.py:201
  24.3 1.2 %multiply_reduce_fusion.2 = (f32[20,2000]{1,0:T(8,128)}, f32[20,2000]{1,0:T(8,128)S(1)}, f32[20,2000]{1,0:T(8,128)S(1)}, f32[20,2000]{1,0:T(8,128)S(1)}, f32[20,2000]{1,0:T(8,128)S(1)}) fusion(f32[20,5]{0,1:T(8,128)S(1)} %get-tuple-element.61, f32[5,2000]{1,0:T(8,128)S(1)} %pad_maximum_fusion.3, f32[20,5]{0,1:T(8,128)S(1)} %get-tuple-element.60, ...), kind=kLoop, calls=%fused_computation.29 | loop fusion | flops 1800000 | bytes 842000 | tf_op jit(solution)/shard_map/reduce_sum | solution.py:93
  25.7 0.7 eq.366
  26.6 0.4 copy.69
  26.9 1.3 %copy.70 = f32[20,2000]{0,1:T(8,128)S(1)} copy(f32[20,2000]{1,0:T(8,128)} %get-tuple-element.7) | data formatting | bytes 320000 | tf_op jit(solution)/shard_map/reduce_sum | solution.py:93
  28.2 1.4 %copy.71 = f32[20,2000]{0,1:T(8,128)} copy(f32[20,2000]{1,0:T(8,128)S(1)} %get-tuple-element.9) | data formatting | bytes 320000 | tf_op jit(solution)/shard_map/reduce_sum | solution.py:93
  29.6 1.3 %copy.72 = f32[20,2000]{0,1:T(8,128)} copy(f32[20,2000]{1,0:T(8,128)S(1)} %get-tuple-element.10) | data formatting | bytes 320000 | tf_op jit(solution)/shard_map/reduce_sum | solution.py:93
  30.9 2.0 %copy.83.courant_ref = f32[2000,1]{1,0:T(8,128)} copy(f32[2000,1]{0,1:T(1,128)} %get-tuple-element.56) | data formatting | bytes 16000 | tf_op jit(solution)/shard_map/mul | solution.py:332
  34.0 3.5 %fusion.21 = (f32[20]{0:T(128)S(1)}, f32[20]{0:T(128)S(1)}, f32[20,2000]{0,1:T(8,128)S(1)}) fusion(f32[2000]{0:T(1024)S(1)} %convert_reduce_fusion, f32[2000]{0:T(1024)S(1)} %bitcast.83, f32[2000]{0:T(1024)S(1)} %broadcast_multiply_fusion.1, f32[2000]{0:T(1024)S(1)} %convert_reduce_fusion.1, f32[2000]{0:T(1024)S(1)} %bitcast.82, f32[20,2000]{0,1:T(8,128)} %copy.72, ...), kind=kLoop, calls=%fused_computation.22 | loop fusion | flops 559960 | bytes 840160 | tf_op jit(solution)/shard_map/reduce_sum | solution.py:207
  37.8 0.4 copy.74
  38.5 1.1 %maximum_bitcast_fusion.basis_ref = bf16[5,180,400]{2,1,0:T(8,128)(2,1)} fusion(bf16[60,5,400]{2,0,1:T(8,128)(2,1)S(1)} %get-tuple-element.34, bf16[60,5,400]{2,0,1:T(8,128)(2,1)S(1)} %get-tuple-element.33, bf16[60,5,400]{2,0,1:T(8,128)(2,1)S(1)} %get-tuple-element.32), kind=kLoop, calls=%fused_computation.36 | loop fusion | flops 2160000 | bytes 1440000 | tf_op jit(solution)/shard_map/transpose | solution.py:178
  39.6 7.3 %shard_map.208 = f32[180,2048]{1,0:T(8,128)} custom-call(bf16[2000,2048]{1,0:T(8,128)(2,1)} %dist_ref.3, bf16[5,180,400]{2,1,0:T(8,128)(2,1)} %maximum_bitcast_fusion.basis_ref), custom_call_target="tpu_custom_call" | custom-call | flops 1474560000 | bytes 9666560 | tf_op jit(solution)/shard_map/pallas_call | solution.py:179
  46.9 1.5 %slice_add_fusion = f32[60,2048]{1,0:T(8,128)S(1)} fusion(f32[180,2048]{1,0:T(8,128)} %shard_map.208), kind=kLoop, calls=%fused_computation.40 | loop fusion | flops 245760 | bytes 1966080 | tf_op jit(solution)/shard_map/add | solution.py:205
  48.6 2.5 %collective-permute-start.4 = (f32[20,2048]{1,0:T(8,128)S(1)}, f32[20,2048]{1,0:T(8,128)S(1)}, u32[]{:S(2)}, u32[]{:S(2)}) collective-permute-start(f32[20,2048]{1,0:T(8,128)S(1)} %fusion.29), channel_id=1, source_target_pairs={{0,96},{32,0},{64,32},{96,64},{1,97},{33,1},{65,33},{97,65},{2,98}... | collective-permute-start | bytes 491528 | tf_op jit(solution)/shard_map/ppermute | solution.py:253
  51.2 0.5 collective-permute-start.3
  51.7 0.6 collective-permute-start.2
  52.4 7.3 %collective-permute-done.4 = f32[20,2048]{1,0:T(8,128)S(1)} collective-permute-done((f32[20,2048]{1,0:T(8,128)S(1)}, f32[20,2048]{1,0:T(8,128)S(1)}, u32[]{:S(2)}, u32[]{:S(2)}) %collective-permute-start.4) | collective-permute-done | bytes 163872 | tf_op jit(solution)/shard_map/ppermute | solution.py:253
  59.7 4.0 %collective-permute-done.2 = f32[20,2048]{1,0:T(8,128)S(1)} collective-permute-done((f32[20,2048]{1,0:T(8,128)S(1)}, f32[20,2048]{1,0:T(8,128)S(1)}, u32[]{:S(2)}, u32[]{:S(2)}) %collective-permute-start.2) | collective-permute-done | bytes 163872 | tf_op jit(solution)/shard_map/ppermute | solution.py:253
  63.9 0.5 copy-done.2
  64.5 1.0 copy.91
  65.6 0.7 and_select_fusion
  66.6 0.5 mul.595
  67.1 0.4 dot_general.14
  67.6 1.7 %fusion.13 = bf16[21,8,256]{2,0,1:T(8,128)(2,1)S(1)} fusion(bf16[8,21,4096]{2,1,0:T(8,128)(2,1)S(1)} %dot_general.14, s32[4096]{0:T(1024)} %bitcast.85), kind=kOutput, calls=%fused_computation.16 | convolution fusion | flops 353413120 | bytes 1478656 | tf_op jit(solution)/shard_map/dot_general | solution.py:288
  69.6 0.5 collective-permute-start.6
  70.1 0.8 collective-permute-start.5
  71.3 2.1 %collective-permute-done.7 = bf16[21,2048]{1,0:T(8,128)(2,1)S(1)} collective-permute-done((bf16[21,2048]{1,0:T(8,128)(2,1)S(1)}, bf16[21,2048]{1,0:T(8,128)(2,1)S(1)}, u32[]{:S(2)}, u32[]{:S(2)}) %collective-permute-start.7) | collective-permute-done | bytes 86048 | tf_op jit(solution)/shard_map/ppermute | solution.py:253
  73.4 1.2 %collective-permute-done.6 = bf16[21,2048]{1,0:T(8,128)(2,1)S(1)} collective-permute-done((bf16[21,2048]{1,0:T(8,128)(2,1)S(1)}, bf16[21,2048]{1,0:T(8,128)(2,1)S(1)}, u32[]{:S(2)}, u32[]{:S(2)}) %collective-permute-start.6) | collective-permute-done | bytes 86048 | tf_op jit(solution)/shard_map/ppermute | solution.py:253
  74.6 3.3 %collective-permute-done.5 = bf16[21,2048]{1,0:T(8,128)(2,1)S(1)} collective-permute-done((bf16[21,2048]{1,0:T(8,128)(2,1)S(1)}, bf16[21,2048]{1,0:T(8,128)(2,1)S(1)}, u32[]{:S(2)}, u32[]{:S(2)}) %collective-permute-start.5) | collective-permute-done | bytes 86048 | tf_op jit(solution)/shard_map/ppermute | solution.py:253
  78.1 0.8 fusion.16
  79.0 0.8 reshape.463
  79.8 7.6 %all-to-all-start.1 = ((bf16[32,2,160]{2,1,0:T(2,128)(2,1)}), bf16[32,2,160]{2,1,0:T(2,128)(2,1)S(1)}, u32[]{:S(2)}, u32[]{:S(2)}) async-start(bf16[32,2,160]{2,1,0:T(2,128)(2,1)} %reshape.463), calls=%async_computation.1 | async-start | bytes 65536 | tf_op jit(solution)/shard_map/all_to_all | solution.py:314
  87.4 1.2 %pad_maximum_fusion.1.recon3_ref = bf16[2000,60]{1,0:T(8,128)(2,1)} fusion(bf16[2000,20]{1,0:T(8,128)(2,1)S(1)} %fusion.23), kind=kLoop, calls=%fused_computation.45 | loop fusion | flops 720000 | bytes 320000 | tf_op jit(solution)/shard_map/concatenate | solution.py:344
  88.6 6.0 %all-to-all-done.1 = bf16[32,2,160]{2,1,0:T(2,128)(2,1)S(1)} async-done(((bf16[32,2,160]{2,1,0:T(2,128)(2,1)}), bf16[32,2,160]{2,1,0:T(2,128)(2,1)S(1)}, u32[]{:S(2)}, u32[]{:S(2)}) %all-to-all-start.1) | async-done | bytes 20512 | tf_op jit(solution)/shard_map/all_to_all | solution.py:314
  94.8 0.8 reduce-precision_convert_fusion.3
  95.6 0.8 pad_maximum_fusion.2.gain_ref
  96.4 15.5 %shard_map.209 = bf16[2000,2048]{1,0:T(8,128)(2,1)} custom-call(bf16[2000,2048]{1,0:T(8,128)(2,1)} %dist_ref.3, bf16[2000,1]{1,0:T(8,128)(2,1)} %copy-done.1, bf16[2000,1]{1,0:T(8,128)(2,1)} %copy-done, f32[2000,1]{1,0:T(8,128)} %copy.83.courant_ref, bf16[2000,60]{1,0:T(8,128)(2,1)} %pad_maximum_fusion.1.recon3_ref, ...), custom_call_target="tpu_custom_call" | custom-call | flops 532480000 | bytes 16384000 | tf_op jit(solution)/shard_map/pallas_call | solution.py:216
  (100 shorter events, 4.6 us)
Async XLA Ops:
  0.0 20.1 %copy-start.19 = (s32[20]{0:T(128)S(1)}, s32[20]{0:T(128)}, u32[]{:S(2)}) copy-start(s32[20]{0:T(128)} %constant.118.clone) | copy-start | bytes 244
  0.0 22.4 %copy-start.17 = (s32[20]{0:T(128)S(1)}, s32[20]{0:T(128)}, u32[]{:S(2)}) copy-start(s32[20]{0:T(128)} %constant.115.clone) | copy-start | bytes 244
  0.0 22.4 %copy-start.18 = (s32[20]{0:T(128)S(1)}, s32[20]{0:T(128)}, u32[]{:S(2)}) copy-start(s32[20]{0:T(128)} %constant.114.clone) | copy-start | bytes 244
  0.0 22.4 %copy-start.15 = (s32[20]{0:T(128)S(1)}, s32[20]{0:T(128)}, u32[]{:S(2)}) copy-start(s32[20]{0:T(128)} %constant.117.clone) | copy-start | bytes 244
  0.0 22.4 %copy-start.16 = (s32[20]{0:T(128)S(1)}, s32[20]{0:T(128)}, u32[]{:S(2)}) copy-start(s32[20]{0:T(128)} %constant.116.clone) | copy-start | bytes 244
  0.0 20.0 %copy-start.12 = (s32[256]{0:T(256)S(1)}, s32[256]{0:T(256)}, u32[]{:S(2)}) copy-start(s32[256]{0:T(256)} %param.26) | copy-start | bytes 3076
  0.0 20.0 %copy-start.7 = (f32[2000]{0:T(1024)S(1)}, f32[2000]{0:T(1024)}, u32[]{:S(2)}) copy-start(f32[2000]{0:T(1024)} %param.24) | copy-start | bytes 24004
  0.1 20.0 %copy-start.8 = (f32[2048]{0:T(1024)S(1)}, f32[2048]{0:T(1024)}, u32[]{:S(2)}) copy-start(f32[2048]{0:T(1024)} %param.25) | copy-start | bytes 24580
  0.1 20.6 %copy-start.5 = (s32[256,1]{0,1:T(1,128)S(1)}, s32[256,1]{0,1:T(1,128)}, u32[]{:S(2)}) copy-start(s32[256,1]{0,1:T(1,128)} %param.27) | copy-start | bytes 3076
  0.1 22.9 %copy-start.4 = (f32[3,2000]{1,0:T(4,128)S(1)}, f32[3,2000]{1,0:T(4,128)}, u32[]{:S(2)}) copy-start(f32[3,2000]{1,0:T(4,128)} %param.23) | copy-start | bytes 72004
  2.4 62.0 %all-to-all-start = ((bf16[32,128,22]{1,2,0:T(8,128)(2,1)}), bf16[32,128,22]{1,2,0:T(8,128)(2,1)}, u32[]{:S(2)}, u32[]{:S(2)}) async-start(bf16[32,128,22]{1,2,0:T(8,128)(2,1)} %broadcast_in_dim.15), calls=%async_computation | async-start | bytes 393216 | tf_op jit(solution)/shard_map/all_to_all | solution.py:272
  12.1 13.5 %copy-start.6 = (s32[1,32,16]{1,2,0:T(8,128)S(1)}, s32[1,32,16]{1,2,0:T(8,128)}, u32[]{:S(2)}) copy-start(s32[1,32,16]{1,2,0:T(8,128)} %param.28) | copy-start | bytes 6148
  14.5 18.5 %collective-permute-start.1 = (bf16[2000,1]{1,0:T(8,128)(2,1)}, bf16[2000,1]{1,0:T(8,128)(2,1)S(1)}, u32[]{:S(2)}, u32[]{:S(2)}) collective-permute-start(bf16[2000,1]{1,0:T(8,128)(2,1)} %get-tuple-element.30), channel_id=1, source_target_pairs={{1,0},{2,1},{3,2},{4,3},{5,4},{6,5},{7,6},{8,7},{9,8},{10,9},{11,1... | collective-permute-start | bytes 12008 | tf_op jit(solution)/shard_map/ppermute | solution.py:61
  16.7 16.5 %collective-permute-start = (bf16[2000,1]{1,0:T(8,128)(2,1)}, bf16[2000,1]{1,0:T(8,128)(2,1)S(1)}, u32[]{:S(2)}, u32[]{:S(2)}) collective-permute-start(bf16[2000,1]{1,0:T(8,128)(2,1)} %get-tuple-element.31), channel_id=1, source_target_pairs={{0,1},{1,2},{2,3},{3,4},{4,5},{5,6},{6,7},{7,8},{8,9},{9,10},{10,1... | collective-permute-start | bytes 12008 | tf_op jit(solution)/shard_map/ppermute | solution.py:60
  33.0 0.8 copy-start
  33.2 0.8 copy-start.1
  46.9 5.4 %copy-start.14 = (f32[20]{0:T(128)S(1)}, f32[20]{0:T(128)}, u32[]{:S(2)}) copy-start(f32[20]{0:T(128)} %constant.121) | copy-start | bytes 244
  48.6 17.6 %copy-start.13 = (pred[21]{0:T(512)(128)(4,1)S(1)}, pred[21]{0:T(512)(128)(4,1)}, u32[]{:S(2)}) copy-start(pred[21]{0:T(512)(128)(4,1)} %constant.111.clone.1) | copy-start | bytes 67
  48.6 11.0 %collective-permute-start.4 = (f32[20,2048]{1,0:T(8,128)S(1)}, f32[20,2048]{1,0:T(8,128)S(1)}, u32[]{:S(2)}, u32[]{:S(2)}) collective-permute-start(f32[20,2048]{1,0:T(8,128)S(1)} %fusion.29), channel_id=1, source_target_pairs={{0,96},{32,0},{64,32},{96,64},{1,97},{33,1},{65,33},{97,65},{2,98}... | collective-permute-start | bytes 491528 | tf_op jit(solution)/shard_map/ppermute | solution.py:253
  51.2 8.5 %collective-permute-start.3 = (f32[20,2048]{1,0:T(8,128)S(1)}, f32[20,2048]{1,0:T(8,128)S(1)}, u32[]{:S(2)}, u32[]{:S(2)}) collective-permute-start(f32[20,2048]{1,0:T(8,128)S(1)} %fusion.29), channel_id=1, source_target_pairs={{0,64},{32,96},{64,0},{96,32},{1,65},{33,97},{65,1},{97,33},{2,66}... | collective-permute-start | bytes 491528 | tf_op jit(solution)/shard_map/ppermute | solution.py:253
  51.7 11.9 %collective-permute-start.2 = (f32[20,2048]{1,0:T(8,128)S(1)}, f32[20,2048]{1,0:T(8,128)S(1)}, u32[]{:S(2)}, u32[]{:S(2)}) collective-permute-start(f32[20,2048]{1,0:T(8,128)S(1)} %fusion.29), channel_id=1, source_target_pairs={{0,32},{32,64},{64,96},{96,0},{1,33},{33,65},{65,97},{97,1},{2,34}... | collective-permute-start | bytes 491528 | tf_op jit(solution)/shard_map/ppermute | solution.py:253
  63.7 0.7 copy-start.2
  67.5 3.4 %copy-start.3 = (f32[20,2048]{1,0:T(8,128)S(1)}, f32[20,2048]{1,0:T(8,128)}, u32[]{:S(2)}) copy-start(f32[20,2048]{1,0:T(8,128)} %copy-done.2) | copy-start | bytes 491524
  67.5 3.5 %slice-start = ((f32[20,2048]{1,0:T(8,128)}), f32[4,2048]{1,0:T(4,128)S(1)}, s32[]{:S(2)}) async-start(f32[20,2048]{1,0:T(8,128)} %copy-done.2), calls=%async_computation.2 | async-start | bytes 65536 | tf_op jit(solution)/shard_map/slice | solution.py:112
  69.3 8.7 %copy-start.11 = (s32[512]{0:T(512)S(1)}, s32[512]{0:T(512)}, u32[]{:S(2)}) copy-start(s32[512]{0:T(512)} %broadcast_add_fusion) | copy-start | bytes 6148
  69.4 4.0 %collective-permute-start.7 = (bf16[21,2048]{1,0:T(8,128)(2,1)S(1)}, bf16[21,2048]{1,0:T(8,128)(2,1)S(1)}, u32[]{:S(2)}, u32[]{:S(2)}) collective-permute-start(bf16[21,2048]{1,0:T(8,128)(2,1)S(1)} %bitcast.74), channel_id=1, source_target_pairs={{0,96},{32,0},{64,32},{96,64},{1,97},{33,1},{65,33},{97,65},{2,98}... | collective-permute-start | bytes 258056 | tf_op jit(solution)/shard_map/ppermute | solution.py:253
  69.6 5.0 %collective-permute-start.6 = (bf16[21,2048]{1,0:T(8,128)(2,1)S(1)}, bf16[21,2048]{1,0:T(8,128)(2,1)S(1)}, u32[]{:S(2)}, u32[]{:S(2)}) collective-permute-start(bf16[21,2048]{1,0:T(8,128)(2,1)S(1)} %bitcast.75), channel_id=1, source_target_pairs={{0,64},{32,96},{64,0},{96,32},{1,65},{33,97},{65,1},{97,33},{2,66}... | collective-permute-start | bytes 258056 | tf_op jit(solution)/shard_map/ppermute | solution.py:253
  70.1 7.8 %collective-permute-start.5 = (bf16[21,2048]{1,0:T(8,128)(2,1)S(1)}, bf16[21,2048]{1,0:T(8,128)(2,1)S(1)}, u32[]{:S(2)}, u32[]{:S(2)}) collective-permute-start(bf16[21,2048]{1,0:T(8,128)(2,1)S(1)} %bitcast.76), channel_id=1, source_target_pairs={{0,32},{32,64},{64,96},{96,0},{1,33},{33,65},{65,97},{97,1},{2,34}... | collective-permute-start | bytes 258056 | tf_op jit(solution)/shard_map/ppermute | solution.py:253
  71.3 23.5 %copy-start.9 = (f32[2048]{0:T(1024)S(1)}, f32[2048]{0:T(1024)}, u32[]{:S(2)}) copy-start(f32[2048]{0:T(1024)} %param.25) | copy-start | bytes 24580
  71.3 23.5 %copy-start.10 = (s32[512]{0:T(512)S(1)}, s32[512]{0:T(512)}, u32[]{:S(2)}) copy-start(s32[512]{0:T(512)} %eq.366) | copy-start | bytes 6148
  79.8 14.9 %all-to-all-start.1 = ((bf16[32,2,160]{2,1,0:T(2,128)(2,1)}), bf16[32,2,160]{2,1,0:T(2,128)(2,1)S(1)}, u32[]{:S(2)}, u32[]{:S(2)}) async-start(bf16[32,2,160]{2,1,0:T(2,128)(2,1)} %reshape.463), calls=%async_computation.1 | async-start | bytes 65536 | tf_op jit(solution)/shard_map/all_to_all | solution.py:314

commit v7 on v6

--- a/solution.py
+++ b/solution.py
@@ -248,9 +248,11 @@
 def sect_sum(values):
     count = lax.axis_size("sect")
     total = values
-    for shift in range(1, count):
-        pairs = [(i, (i + shift) % count) for i in range(count)]
-        total = total + lax.ppermute(values, "sect", pairs)
+    step = 1
+    while step < count:
+        pairs = [(i, i ^ step) for i in range(count)]
+        total = total + lax.ppermute(total, "sect", pairs)
+        step *= 2
     return total
 
 

time: 113 us -> 109 us (0.965)
  waiting for transfers between devices: 24 us -> 17.9 us
  starting transfers between devices: 28 us -> 30.2 us
  local copies, waits for them, and re-layouts: 16.4 us -> 18.3 us
    ppermute x6 -> x4, waiting for transfers between devices: 17.9 us -> 11.9 us  [sect_sum(): total = total + lax.ppermute(total, 'sect', pairs)]
    all_to_all x1, starting transfers between devices: 7.59 us -> 9.59 us  [ghost_walls(): lax.all_to_all(outgoing, 'space', split_axis=1, concat_axis=1, tiled=True)]
    dot_general x1, local copies, waits for them, and re-layouts: 0.45 us -> 1.79 us  [fold_interface(): lax.dot_general(spread, pick_lo, (((0,), (0,)), ((), ())), preferred_elem...]
    unnamed x47 -> x43, local copies, waits for them, and re-layouts: 2.3 us -> 1.79 us
    ppermute x6 -> x4, starting transfers between devices: 5.22 us -> 5.45 us  [sect_sum(): total = total + lax.ppermute(total, 'sect', pairs)]
  transfers between devices with their start and end apart: 10 -> 8, of which waited for: 6 -> 4; matrix products, arithmetic and copies ran while one was open for 22% -> 28% of each run, Pallas kernels for 7% -> 7%
where the time goes in v7:
time: 109 us
  starting transfers between devices  30.2 us (28%)
  Pallas kernels  22.8 us (21%)
  local copies, waits for them, and re-layouts  18.3 us (17%)
  waiting for transfers between devices  17.9 us (16%)
  other arithmetic  16.2 us (15%)
  matrix products  2.6 us (2%)
    pallas_call x1, Pallas kernels, relax_call(): pl.pallas_call(relax_kernel, grid=(steps,), in_specs=[row_spec(cells), ro...  15.5 us
    ppermute x4, waiting for transfers between devices, sect_sum(): total = total + lax.ppermute(total, 'sect', pairs)  11.9 us
    all_to_all x1, starting transfers between devices, interface_rows(): gathered = lax.all_to_all(spread_out, 'space', 0, 0, tiled=True)  9.64 us
    all_to_all x1, starting transfers between devices, ghost_walls(): lax.all_to_all(outgoing, 'space', split_axis=1, concat_axis=1, tiled=True)  9.59 us
    pallas_call x1, Pallas kernels, moments_call(): pl.pallas_call(moments_kernel, grid=(steps,), in_specs=[row_spec(cells),...  7.3 us
    all_to_all x1, waiting for transfers between devices, ghost_walls(): lax.all_to_all(outgoing, 'space', split_axis=1, concat_axis=1, tiled=True)  6.03 us
    ppermute x4, starting transfers between devices, sect_sum(): total = total + lax.ppermute(total, 'sect', pairs)  5.45 us
    reduce_sum x3, local copies, waits for them, and re-layouts, pick(): return jnp.sum(select[:, :, None] * extended[None, :, :], axis=1)  3.97 us
  transfers between devices with their start and end apart: 8, of which 4 were waited for; matrix products, arithmetic and copies ran while one was open for 28% of the time, Pallas kernels for 7%

profile of v7, /device:TPU:1, one launch (start us, length us, event | category | flops | bytes accessed | tf_op | source)
XLA Modules:
  0.0 108.6 jit_solution(3709947561476947611)
XLA Ops:
  0.1 0.7 fusion.65
  0.9 0.8 convert_element_type.226
  1.7 0.7 broadcast_in_dim.15
  2.4 9.6 %all-to-all-start = ((bf16[32,128,22]{1,2,0:T(8,128)(2,1)}), bf16[32,128,22]{1,2,0:T(8,128)(2,1)}, u32[]{:S(2)}, u32[]{:S(2)}) async-start(bf16[32,128,22]{1,2,0:T(8,128)(2,1)} %broadcast_in_dim.15), calls=%async_computation | async-start | bytes 393216 | tf_op jit(solution)/shard_map/all_to_all | solution.py:274
  12.1 2.4 %fusion.69 = (bf16[2000,1]{1,0:T(8,128)(2,1)}, bf16[2000,1]{1,0:T(8,128)(2,1)}) fusion(bf16[2000,2048]{1,0:T(8,128)(2,1)} %dist_ref.3), kind=kLoop, calls=%fused_computation.169 | loop fusion | bytes 16000 | tf_op jit(solution)/shard_map/slice | solution.py:61
  14.5 2.2 %collective-permute-start.1 = (bf16[2000,1]{1,0:T(8,128)(2,1)}, bf16[2000,1]{1,0:T(8,128)(2,1)S(1)}, u32[]{:S(2)}, u32[]{:S(2)}) collective-permute-start(bf16[2000,1]{1,0:T(8,128)(2,1)} %get-tuple-element.30), channel_id=1, source_target_pairs={{1,0},{2,1},{3,2},{4,3},{5,4},{6,5},{7,6},{8,7},{9,8},{10,9},{11,1... | collective-permute-start | bytes 12008 | tf_op jit(solution)/shard_map/ppermute | solution.py:61
  16.7 3.4 %collective-permute-start = (bf16[2000,1]{1,0:T(8,128)(2,1)}, bf16[2000,1]{1,0:T(8,128)(2,1)S(1)}, u32[]{:S(2)}, u32[]{:S(2)}) collective-permute-start(bf16[2000,1]{1,0:T(8,128)(2,1)} %get-tuple-element.31), channel_id=1, source_target_pairs={{0,1},{1,2},{2,3},{3,4},{4,5},{5,6},{6,7},{7,8},{8,9},{9,10},{10,1... | collective-permute-start | bytes 12008 | tf_op jit(solution)/shard_map/ppermute | solution.py:60
  20.1 0.6 broadcast_subtract_fusion
  20.7 0.6 reduce-window.6
  21.7 0.5 broadcast.442
  22.2 1.3 %add_reduce_fusion = (f32[2000]{0:T(1024)S(1)}, f32[2000]{0:T(1024)S(1)}, f32[2000]{0:T(1024)S(1)}, f32[1,2000]{1,0:T(1,128)S(1)}, f32[1,2000]{1,0:T(1,128)S(1)}, /*index=5*/f32[2000,1]{0,1:T(1,128)}) fusion(f32[]{:T(128)} %broadcast.442, f32[3,2000]{1,0:T(4,128)S(1)} %copy-done.2), kind=kLoop, calls=%fused_computation.137 | loop fusion | flops 10000 | bytes 56004 | tf_op jit(solution)/shard_map/add | solution.py:201
  23.5 1.2 %multiply_reduce_fusion.2 = (f32[20,2000]{1,0:T(8,128)}, f32[20,2000]{1,0:T(8,128)S(1)}, f32[20,2000]{1,0:T(8,128)S(1)}, f32[20,2000]{1,0:T(8,128)S(1)}, f32[20,2000]{1,0:T(8,128)S(1)}) fusion(f32[20,5]{0,1:T(8,128)S(1)} %get-tuple-element.61, f32[5,2000]{1,0:T(8,128)S(1)} %pad_maximum_fusion.3, f32[20,5]{0,1:T(8,128)S(1)} %get-tuple-element.60, ...), kind=kLoop, calls=%fused_computation.29 | loop fusion | flops 1800000 | bytes 842000 | tf_op jit(solution)/shard_map/reduce_sum | solution.py:93
  24.8 0.7 select_reduce_fusion
  25.7 0.7 eq.366
  26.6 0.4 copy.69
  27.0 1.3 %copy.70 = f32[20,2000]{0,1:T(8,128)S(1)} copy(f32[20,2000]{1,0:T(8,128)} %get-tuple-element.7) | data formatting | bytes 320000 | tf_op jit(solution)/shard_map/reduce_sum | solution.py:93
  28.2 1.4 %copy.71 = f32[20,2000]{0,1:T(8,128)} copy(f32[20,2000]{1,0:T(8,128)S(1)} %get-tuple-element.9) | data formatting | bytes 320000 | tf_op jit(solution)/shard_map/reduce_sum | solution.py:93
  29.6 1.3 %copy.72 = f32[20,2000]{0,1:T(8,128)} copy(f32[20,2000]{1,0:T(8,128)S(1)} %get-tuple-element.10) | data formatting | bytes 320000 | tf_op jit(solution)/shard_map/reduce_sum | solution.py:93
  30.9 2.0 %copy.83.courant_ref = f32[2000,1]{1,0:T(8,128)} copy(f32[2000,1]{0,1:T(1,128)} %get-tuple-element.56) | data formatting | bytes 16000 | tf_op jit(solution)/shard_map/mul | solution.py:334
  33.0 0.2 convert_reduce_fusion
  33.2 0.2 convert_reduce_fusion.1
  33.4 0.3 copy-done
  33.7 0.3 copy-done.1
  34.0 3.5 %fusion.21 = (f32[20]{0:T(128)S(1)}, f32[20]{0:T(128)S(1)}, f32[20,2000]{0,1:T(8,128)S(1)}) fusion(f32[2000]{0:T(1024)S(1)} %convert_reduce_fusion, f32[2000]{0:T(1024)S(1)} %bitcast.81, f32[2000]{0:T(1024)S(1)} %broadcast_multiply_fusion.1, f32[2000]{0:T(1024)S(1)} %convert_reduce_fusion.1, f32[2000]{0:T(1024)S(1)} %bitcast.80, f32[20,2000]{0,1:T(8,128)} %copy.72, ...), kind=kLoop, calls=%fused_computation.22 | loop fusion | flops 559960 | bytes 840160 | tf_op jit(solution)/shard_map/reduce_sum | solution.py:207
  37.8 0.4 copy.74
  38.5 1.1 %maximum_bitcast_fusion.basis_ref = bf16[5,180,400]{2,1,0:T(8,128)(2,1)} fusion(bf16[60,5,400]{2,0,1:T(8,128)(2,1)S(1)} %get-tuple-element.34, bf16[60,5,400]{2,0,1:T(8,128)(2,1)S(1)} %get-tuple-element.33, bf16[60,5,400]{2,0,1:T(8,128)(2,1)S(1)} %get-tuple-element.32), kind=kLoop, calls=%fused_computation.36 | loop fusion | flops 2160000 | bytes 1440000 | tf_op jit(solution)/shard_map/transpose | solution.py:178
  39.6 7.3 %shard_map.208 = f32[180,2048]{1,0:T(8,128)} custom-call(bf16[2000,2048]{1,0:T(8,128)(2,1)} %dist_ref.3, bf16[5,180,400]{2,1,0:T(8,128)(2,1)} %maximum_bitcast_fusion.basis_ref), custom_call_target="tpu_custom_call" | custom-call | flops 1474560000 | bytes 9666560 | tf_op jit(solution)/shard_map/pallas_call | solution.py:179
  46.9 1.5 %slice_add_fusion = f32[60,2048]{1,0:T(8,128)S(1)} fusion(f32[180,2048]{1,0:T(8,128)} %shard_map.208), kind=kLoop, calls=%fused_computation.40 | loop fusion | flops 245760 | bytes 1966080 | tf_op jit(solution)/shard_map/add | solution.py:205
  48.6 1.3 %collective-permute-start.2 = (f32[20,2048]{1,0:T(8,128)S(1)}, f32[20,2048]{1,0:T(8,128)S(1)}, u32[]{:S(2)}, u32[]{:S(2)}) collective-permute-start(f32[20,2048]{1,0:T(8,128)S(1)} %fusion.29), channel_id=1, source_target_pairs={{0,32},{32,0},{64,96},{96,64},{1,33},{33,1},{65,97},{97,65},{2,34}... | collective-permute-start | bytes 491528 | tf_op jit(solution)/shard_map/ppermute | solution.py:254
  49.9 5.0 %collective-permute-done.2 = f32[20,2048]{1,0:T(8,128)S(1)} collective-permute-done((f32[20,2048]{1,0:T(8,128)S(1)}, f32[20,2048]{1,0:T(8,128)S(1)}, u32[]{:S(2)}, u32[]{:S(2)}) %collective-permute-start.2) | collective-permute-done | bytes 163872 | tf_op jit(solution)/shard_map/ppermute | solution.py:254
  54.9 2.8 %collective-permute-start.3 = (f32[20,2048]{1,0:T(8,128)S(1)}, f32[20,2048]{1,0:T(8,128)S(1)}, u32[]{:S(2)}, u32[]{:S(2)}) collective-permute-start(f32[20,2048]{1,0:T(8,128)S(1)} %add.252), channel_id=1, source_target_pairs={{0,64},{32,96},{64,0},{96,32},{1,65},{33,97},{65,1},{97,33},{2,66}... | collective-permute-start | bytes 491528 | tf_op jit(solution)/shard_map/ppermute | solution.py:254
  57.7 1.0 copy.91
  59.3 1.5 %mul.595 = bf16[4096,168]{0,1:T(8,128)(2,1)} reshape(bf16[4096,8,21]{0,2,1:T(8,128)(2,1)S(1)} %broadcast_multiply_fusion) | data formatting | bytes 2752512 | tf_op jit(solution)/shard_map/mul | solution.py:288
  60.8 1.8 %dot_general.14 = bf16[8,21,4096]{2,1,0:T(8,128)(2,1)S(1)} reshape(bf16[168,4096]{1,0:T(8,128)(2,1)} %bitcast.68) | data formatting | bytes 2752512 | tf_op jit(solution)/shard_map/dot_general | solution.py:290
  62.6 1.0 fusion.13
  63.7 0.4 collective-permute-start.4
  64.1 3.5 %collective-permute-done.4 = bf16[21,2048]{1,0:T(8,128)(2,1)S(1)} collective-permute-done((bf16[21,2048]{1,0:T(8,128)(2,1)S(1)}, bf16[21,2048]{1,0:T(8,128)(2,1)S(1)}, u32[]{:S(2)}, u32[]{:S(2)}) %collective-permute-start.4) | collective-permute-done | bytes 86048 | tf_op jit(solution)/shard_map/ppermute | solution.py:254
  67.6 0.9 collective-permute-start.5
  69.0 0.2 stack.3
  69.2 3.4 %collective-permute-done.5 = bf16[21,2048]{1,0:T(8,128)(2,1)S(1)} collective-permute-done((bf16[21,2048]{1,0:T(8,128)(2,1)S(1)}, bf16[21,2048]{1,0:T(8,128)(2,1)S(1)}, u32[]{:S(2)}, u32[]{:S(2)}) %collective-permute-start.5) | collective-permute-done | bytes 86048 | tf_op jit(solution)/shard_map/ppermute | solution.py:254
  72.8 0.8 fusion.16
  73.7 0.8 reshape.463
  74.5 9.6 %all-to-all-start.1 = ((bf16[32,2,160]{2,1,0:T(2,128)(2,1)}), bf16[32,2,160]{2,1,0:T(2,128)(2,1)S(1)}, u32[]{:S(2)}, u32[]{:S(2)}) async-start(bf16[32,2,160]{2,1,0:T(2,128)(2,1)} %reshape.463), calls=%async_computation.1 | async-start | bytes 65536 | tf_op jit(solution)/shard_map/all_to_all | solution.py:316
  84.1 1.2 %pad_maximum_fusion.1.recon3_ref = bf16[2000,60]{1,0:T(8,128)(2,1)} fusion(bf16[2000,20]{1,0:T(8,128)(2,1)S(1)} %fusion.23), kind=kLoop, calls=%fused_computation.45 | loop fusion | flops 720000 | bytes 320000 | tf_op jit(solution)/shard_map/concatenate | solution.py:346
  85.3 6.0 %all-to-all-done.1 = bf16[32,2,160]{2,1,0:T(2,128)(2,1)S(1)} async-done(((bf16[32,2,160]{2,1,0:T(2,128)(2,1)}), bf16[32,2,160]{2,1,0:T(2,128)(2,1)S(1)}, u32[]{:S(2)}, u32[]{:S(2)}) %all-to-all-start.1) | async-done | bytes 20512 | tf_op jit(solution)/shard_map/all_to_all | solution.py:316
  91.5 0.8 reduce-precision_convert_fusion.3
  92.3 0.8 pad_maximum_fusion.2.gain_ref
  93.1 15.5 %shard_map.209 = bf16[2000,2048]{1,0:T(8,128)(2,1)} custom-call(bf16[2000,2048]{1,0:T(8,128)(2,1)} %dist_ref.3, bf16[2000,1]{1,0:T(8,128)(2,1)} %copy-done.1, bf16[2000,1]{1,0:T(8,128)(2,1)} %copy-done, f32[2000,1]{1,0:T(8,128)} %copy.83.courant_ref, bf16[2000,60]{1,0:T(8,128)(2,1)} %pad_maximum_fusion.1.recon3_ref, ...), custom_call_target="tpu_custom_call" | custom-call | flops 532480000 | bytes 16384000 | tf_op jit(solution)/shard_map/pallas_call | solution.py:216
  (93 shorter events, 3.1 us)
Async XLA Ops:
  0.0 20.1 %copy-start.17 = (s32[20]{0:T(128)S(1)}, s32[20]{0:T(128)}, u32[]{:S(2)}) copy-start(s32[20]{0:T(128)} %constant.118.clone) | copy-start | bytes 244
  0.0 21.6 %copy-start.15 = (s32[20]{0:T(128)S(1)}, s32[20]{0:T(128)}, u32[]{:S(2)}) copy-start(s32[20]{0:T(128)} %constant.115.clone) | copy-start | bytes 244
  0.0 21.7 %copy-start.16 = (s32[20]{0:T(128)S(1)}, s32[20]{0:T(128)}, u32[]{:S(2)}) copy-start(s32[20]{0:T(128)} %constant.114.clone) | copy-start | bytes 244
  0.0 21.7 %copy-start.13 = (s32[20]{0:T(128)S(1)}, s32[20]{0:T(128)}, u32[]{:S(2)}) copy-start(s32[20]{0:T(128)} %constant.117.clone) | copy-start | bytes 244
  0.0 21.7 %copy-start.14 = (s32[20]{0:T(128)S(1)}, s32[20]{0:T(128)}, u32[]{:S(2)}) copy-start(s32[20]{0:T(128)} %constant.116.clone) | copy-start | bytes 244
  0.0 20.0 %copy-start.10 = (s32[256]{0:T(256)S(1)}, s32[256]{0:T(256)}, u32[]{:S(2)}) copy-start(s32[256]{0:T(256)} %param.26) | copy-start | bytes 3076
  0.0 20.0 %copy-start.5 = (f32[2000]{0:T(1024)S(1)}, f32[2000]{0:T(1024)}, u32[]{:S(2)}) copy-start(f32[2000]{0:T(1024)} %param.24) | copy-start | bytes 24004
  0.1 20.0 %copy-start.6 = (f32[2048]{0:T(1024)S(1)}, f32[2048]{0:T(1024)}, u32[]{:S(2)}) copy-start(f32[2048]{0:T(1024)} %param.25) | copy-start | bytes 24580
  0.1 20.6 %copy-start.3 = (s32[256,1]{0,1:T(1,128)S(1)}, s32[256,1]{0,1:T(1,128)}, u32[]{:S(2)}) copy-start(s32[256,1]{0,1:T(1,128)} %param.27) | copy-start | bytes 3076
  0.1 22.2 %copy-start.2 = (f32[3,2000]{1,0:T(4,128)S(1)}, f32[3,2000]{1,0:T(4,128)}, u32[]{:S(2)}) copy-start(f32[3,2000]{1,0:T(4,128)} %param.23) | copy-start | bytes 72004
  2.4 55.3 %all-to-all-start = ((bf16[32,128,22]{1,2,0:T(8,128)(2,1)}), bf16[32,128,22]{1,2,0:T(8,128)(2,1)}, u32[]{:S(2)}, u32[]{:S(2)}) async-start(bf16[32,128,22]{1,2,0:T(8,128)(2,1)} %broadcast_in_dim.15), calls=%async_computation | async-start | bytes 393216 | tf_op jit(solution)/shard_map/all_to_all | solution.py:274
  12.1 13.5 %copy-start.4 = (s32[1,32,16]{1,2,0:T(8,128)S(1)}, s32[1,32,16]{1,2,0:T(8,128)}, u32[]{:S(2)}) copy-start(s32[1,32,16]{1,2,0:T(8,128)} %param.28) | copy-start | bytes 6148
  14.5 18.5 %collective-permute-start.1 = (bf16[2000,1]{1,0:T(8,128)(2,1)}, bf16[2000,1]{1,0:T(8,128)(2,1)S(1)}, u32[]{:S(2)}, u32[]{:S(2)}) collective-permute-start(bf16[2000,1]{1,0:T(8,128)(2,1)} %get-tuple-element.30), channel_id=1, source_target_pairs={{1,0},{2,1},{3,2},{4,3},{5,4},{6,5},{7,6},{8,7},{9,8},{10,9},{11,1... | collective-permute-start | bytes 12008 | tf_op jit(solution)/shard_map/ppermute | solution.py:61
  16.7 16.5 %collective-permute-start = (bf16[2000,1]{1,0:T(8,128)(2,1)}, bf16[2000,1]{1,0:T(8,128)(2,1)S(1)}, u32[]{:S(2)}, u32[]{:S(2)}) collective-permute-start(bf16[2000,1]{1,0:T(8,128)(2,1)} %get-tuple-element.31), channel_id=1, source_target_pairs={{0,1},{1,2},{2,3},{3,4},{4,5},{5,6},{6,7},{7,8},{8,9},{9,10},{10,1... | collective-permute-start | bytes 12008 | tf_op jit(solution)/shard_map/ppermute | solution.py:60
  33.0 0.8 copy-start
  33.2 0.8 copy-start.1
  46.9 3.0 %copy-start.8 = (s32[512]{0:T(512)S(1)}, s32[512]{0:T(512)}, u32[]{:S(2)}) copy-start(s32[512]{0:T(512)} %select_reduce_fusion) | copy-start | bytes 6148
  48.4 10.6 %copy-start.12 = (pred[21]{0:T(512)(128)(4,1)S(1)}, pred[21]{0:T(512)(128)(4,1)}, u32[]{:S(2)}) copy-start(pred[21]{0:T(512)(128)(4,1)} %constant.111.clone.1) | copy-start | bytes 67
  48.6 6.3 %collective-permute-start.2 = (f32[20,2048]{1,0:T(8,128)S(1)}, f32[20,2048]{1,0:T(8,128)S(1)}, u32[]{:S(2)}, u32[]{:S(2)}) collective-permute-start(f32[20,2048]{1,0:T(8,128)S(1)} %fusion.29), channel_id=1, source_target_pairs={{0,32},{32,0},{64,96},{96,64},{1,33},{33,1},{65,97},{97,65},{2,34}... | collective-permute-start | bytes 491528 | tf_op jit(solution)/shard_map/ppermute | solution.py:254
  54.9 13.7 %collective-permute-start.3 = (f32[20,2048]{1,0:T(8,128)S(1)}, f32[20,2048]{1,0:T(8,128)S(1)}, u32[]{:S(2)}, u32[]{:S(2)}) collective-permute-start(f32[20,2048]{1,0:T(8,128)S(1)} %add.252), channel_id=1, source_target_pairs={{0,64},{32,96},{64,0},{96,32},{1,65},{33,97},{65,1},{97,33},{2,66}... | collective-permute-start | bytes 491528 | tf_op jit(solution)/shard_map/ppermute | solution.py:254
  62.6 1.5 %copy-start.11 = (f32[20]{0:T(128)S(1)}, f32[20]{0:T(128)}, u32[]{:S(2)}) copy-start(f32[20]{0:T(128)} %constant.121) | copy-start | bytes 244
  63.7 3.9 %collective-permute-start.4 = (bf16[21,2048]{1,0:T(8,128)(2,1)S(1)}, bf16[21,2048]{1,0:T(8,128)(2,1)S(1)}, u32[]{:S(2)}, u32[]{:S(2)}) collective-permute-start(bf16[21,2048]{1,0:T(8,128)(2,1)S(1)} %bitcast.75), channel_id=1, source_target_pairs={{0,32},{32,0},{64,96},{96,64},{1,33},{33,1},{65,97},{97,65},{2,34}... | collective-permute-start | bytes 258056 | tf_op jit(solution)/shard_map/ppermute | solution.py:254
  67.6 5.1 %collective-permute-start.5 = (bf16[21,2048]{1,0:T(8,128)(2,1)S(1)}, bf16[21,2048]{1,0:T(8,128)(2,1)S(1)}, u32[]{:S(2)}, u32[]{:S(2)}) collective-permute-start(bf16[21,2048]{1,0:T(8,128)(2,1)S(1)} %add.293), channel_id=1, source_target_pairs={{0,64},{32,96},{64,0},{96,32},{1,65},{33,97},{65,1},{97,33},{2,66}... | collective-permute-start | bytes 258056 | tf_op jit(solution)/shard_map/ppermute | solution.py:254
  69.2 22.3 %copy-start.7 = (f32[2048]{0:T(1024)S(1)}, f32[2048]{0:T(1024)}, u32[]{:S(2)}) copy-start(f32[2048]{0:T(1024)} %param.25) | copy-start | bytes 24580
  69.2 22.2 %copy-start.9 = (s32[512]{0:T(512)S(1)}, s32[512]{0:T(512)}, u32[]{:S(2)}) copy-start(s32[512]{0:T(512)} %eq.366) | copy-start | bytes 6148
  74.5 16.8 %all-to-all-start.1 = ((bf16[32,2,160]{2,1,0:T(2,128)(2,1)}), bf16[32,2,160]{2,1,0:T(2,128)(2,1)S(1)}, u32[]{:S(2)}, u32[]{:S(2)}) async-start(bf16[32,2,160]{2,1,0:T(2,128)(2,1)} %reshape.463), calls=%async_computation.1 | async-start | bytes 65536 | tf_op jit(solution)/shard_map/all_to_all | solution.py:316

commit v8 on v7

--- a/solution.py
+++ b/solution.py
@@ -299,8 +299,7 @@
     return closure + hit[None, :] * (fluid - closure)
 
 
-def ghost_walls(targets, ghost_source, ghost_owner, wall_cell):
-    cells = targets.shape[1]
+def ghost_tables(cells, ghost_source, ghost_owner, wall_cell):
     peers = lax.axis_size("space")
     capacity = wall_cell.shape[2]
     slots = peers * capacity
@@ -312,10 +311,14 @@
     at_place = (places[:, None] == jnp.arange(slots, dtype=jnp.int32)[None, :]).astype(jnp.int32)
     source_of = jnp.sum(at_place * (ghost_source[:, None] + 1), axis=0) - 1
     select = (jnp.arange(cells, dtype=jnp.int32)[:, None] == source_of[None, :]).astype(jnp.bfloat16)
+    walls = wall_cell.reshape(slots)
+    land = (walls[:, None] == jnp.arange(cells, dtype=jnp.int32)[None, :]).astype(jnp.bfloat16)
+    return select, land
+
+
+def ghost_walls(targets, select, land):
     outgoing = jnp.dot(targets, select, preferred_element_type=jnp.float32).astype(jnp.bfloat16)
     arrived = lax.all_to_all(outgoing, "space", split_axis=1, concat_axis=1, tiled=True)
-    walls = wall_cell.reshape(slots)
-    land = (walls[:, None] == jnp.arange(cells, dtype=jnp.int32)[None, :]).astype(jnp.bfloat16)
     return jnp.dot(arrived, land, preferred_element_type=jnp.float32)
 
 
@@ -337,13 +340,15 @@
         dist, left, right, courant, moment_basis(velocity, quad_weight)
     )
     slab_base = lax.axis_index("space") * cells
+    select, land = ghost_tables(cells, ghost_source, ghost_owner, wall_cell)
+    select, land = lax.optimization_barrier((select, land))
+    recon = recon_basis(velocity)
+    recon3 = lax.optimization_barrier(jnp.concatenate([recon, recon, recon], axis=1))
     moments = sect_sum(partial_moments)
     partial_rows = interface_rows(plenum_moments, iface_cell, cells, slab_base)
     rows = sect_sum(partial_rows.astype(jnp.bfloat16)).astype(jnp.float32)
     targets = inject(es_targets(moments), rows).astype(jnp.bfloat16)
-    wall_moments = ghost_walls(targets, ghost_source, ghost_owner, wall_cell)
-    recon = recon_basis(velocity)
-    recon3 = jnp.concatenate([recon, recon, recon], axis=1)
+    wall_moments = ghost_walls(targets, select, land)
     rate = collision_rate[None, :]
     gain = split_three(rate * targets.astype(jnp.float32) + WALL_SHARE * wall_moments)
     return relax_call(dist, left, right, courant, recon3, gain, 1.0 - rate)

time: 109 us -> 126 us (1.16)
  other arithmetic: 16.2 us -> 24.5 us
  local copies, waits for them, and re-layouts: 18.3 us -> 25.1 us
  matrix products: 2.6 us -> 4.81 us
  waiting for transfers between devices: 17.9 us -> 16.5 us
    convert_element_type x1 -> x3, other arithmetic: 0.01 us -> 2.72 us  [the longest x1 2.31 us: ghost_tables(): (jnp.arange(cells, dtype=jnp.int32)[:, None] == source_of[None, :]).astyp...]
    mul x1, local copies, waits for them, and re-layouts: 0.35 us -> 2.26 us  [hermite(): element = first * second * third]
    mul x1, other arithmetic: 0.03 us -> 1.73 us  [hermite(): element = first * second * third]
    mul x1, local copies, waits for them, and re-layouts: 1.53 us -> 2.97 us  [fold_interface(): pick_hi[:, :, None] * extended[:, None, :]]
    dot_general x1, matrix products: 1 us -> 2.41 us  [fold_interface(): lax.dot_general(spread, pick_lo, (((0,), (0,)), ((), ())), preferred_elem...]
    ppermute x4, waiting for transfers between devices: 11.9 us -> 10.5 us  [sect_sum(): total = total + lax.ppermute(total, 'sect', pairs)]
  transfers between devices with their start and end apart: 8 -> 8, of which waited for: 4 -> 4; matrix products, arithmetic and copies ran while one was open for 28% -> 38% of each run, Pallas kernels for 7% -> 6%
where the time goes in v8:
time: 126 us; the launch traced here: 125 us
  starting transfers between devices  30.4 us (24%)
  local copies, waits for them, and re-layouts  25.1 us (20%)
  other arithmetic  24.5 us (19%)
  Pallas kernels  22.8 us (18%)
  waiting for transfers between devices  16.5 us (13%)
  matrix products  4.81 us (4%)
    pallas_call x1, Pallas kernels, relax_call(): pl.pallas_call(relax_kernel, grid=(steps,), in_specs=[row_spec(cells), ro...  15.5 us
    ppermute x4, waiting for transfers between devices, sect_sum(): total = total + lax.ppermute(total, 'sect', pairs)  10.5 us
    all_to_all x1, starting transfers between devices, interface_rows(): gathered = lax.all_to_all(spread_out, 'space', 0, 0, tiled=True)  9.64 us
    all_to_all x1, starting transfers between devices, ghost_walls(): lax.all_to_all(outgoing, 'space', split_axis=1, concat_axis=1, tiled=True)  9.58 us
    pallas_call x1, Pallas kernels, moments_call(): pl.pallas_call(moments_kernel, grid=(steps,), in_specs=[row_spec(cells),...  7.31 us
    all_to_all x1, waiting for transfers between devices, ghost_walls(): lax.all_to_all(outgoing, 'space', split_axis=1, concat_axis=1, tiled=True)  6.05 us
    ppermute x4, starting transfers between devices, sect_sum(): total = total + lax.ppermute(total, 'sect', pairs)  5.63 us
    reduce_sum x3, local copies, waits for them, and re-layouts, pick(): return jnp.sum(select[:, :, None] * extended[None, :, :], axis=1)  4.96 us
  transfers between devices with their start and end apart: 8, of which 4 were waited for; matrix products, arithmetic and copies ran while one was open for 38% of the time, Pallas kernels for 6%

profile of v8, /device:TPU:1, one launch (start us, length us, event | category | flops | bytes accessed | tf_op | source)
XLA Modules:
  0.0 124.8 jit_solution(5619414817884141598)
XLA Ops:
  0.0 0.7 fusion.61
  0.8 0.8 convert_element_type.230
  1.7 0.7 broadcast_in_dim.15
  2.4 9.6 %all-to-all-start = ((bf16[32,128,22]{1,2,0:T(8,128)(2,1)}), bf16[32,128,22]{1,2,0:T(8,128)(2,1)}, u32[]{:S(2)}, u32[]{:S(2)}) async-start(bf16[32,128,22]{1,2,0:T(8,128)(2,1)} %broadcast_in_dim.15), calls=%async_computation | async-start | bytes 393216 | tf_op jit(solution)/shard_map/all_to_all | solution.py:274
  12.0 2.4 %fusion.65 = (bf16[2000,1]{1,0:T(8,128)(2,1)}, bf16[2000,1]{1,0:T(8,128)(2,1)}) fusion(bf16[2000,2048]{1,0:T(8,128)(2,1)} %dist_ref.3), kind=kLoop, calls=%fused_computation.167 | loop fusion | bytes 16000 | tf_op jit(solution)/shard_map/slice | solution.py:61
  14.4 2.2 %collective-permute-start.1 = (bf16[2000,1]{1,0:T(8,128)(2,1)}, bf16[2000,1]{1,0:T(8,128)(2,1)S(1)}, u32[]{:S(2)}, u32[]{:S(2)}) collective-permute-start(bf16[2000,1]{1,0:T(8,128)(2,1)} %get-tuple-element.34), channel_id=1, source_target_pairs={{1,0},{2,1},{3,2},{4,3},{5,4},{6,5},{7,6},{8,7},{9,8},{10,9},{11,1... | collective-permute-start | bytes 12008 | tf_op jit(solution)/shard_map/ppermute | solution.py:61
  16.6 3.4 %collective-permute-start = (bf16[2000,1]{1,0:T(8,128)(2,1)}, bf16[2000,1]{1,0:T(8,128)(2,1)S(1)}, u32[]{:S(2)}, u32[]{:S(2)}) collective-permute-start(bf16[2000,1]{1,0:T(8,128)(2,1)} %get-tuple-element.35), channel_id=1, source_target_pairs={{0,1},{1,2},{2,3},{3,4},{4,5},{5,6},{6,7},{7,8},{8,9},{9,10},{10,1... | collective-permute-start | bytes 12008 | tf_op jit(solution)/shard_map/ppermute | solution.py:60
  20.2 0.6 reduce-window.6
  21.4 2.3 %fusion.3 = bf16[2048,512]{1,0:T(8,128)(2,1)} fusion(s32[512]{0:T(512)S(1)} %broadcast_add_fusion), kind=kLoop, calls=%fused_computation.5 | loop fusion | flops 2097152 | bytes 2099200 | tf_op jit(solution)/shard_map/convert_element_type | solution.py:313
  24.1 0.6 fusion.57
  24.7 0.5 broadcast.442
  25.3 1.9 %add_reduce_fusion = (f32[2000]{0:T(1024)S(1)}, f32[2000]{0:T(1024)S(1)}, f32[2000]{0:T(1024)}, f32[1,2000]{1,0:T(1,128)}, f32[1,2000]{1,0:T(1,128)}, /*index=5*/f32[2000,1]{0,1:T(1,128)}) fusion(f32[]{:T(128)} %broadcast.442, f32[3,2000]{1,0:T(4,128)S(1)} %copy-done.5), kind=kLoop, calls=%fused_computation.135 | loop fusion | flops 10000 | bytes 56004 | tf_op jit(solution)/shard_map/add | solution.py:201
  27.2 2.2 %multiply_reduce_fusion.2 = (f32[20,2000]{1,0:T(8,128)}, f32[20,2000]{1,0:T(8,128)}, f32[20,2000]{1,0:T(8,128)S(1)}, f32[20,2000]{1,0:T(8,128)S(1)}, f32[20,2000]{1,0:T(8,128)}) fusion(f32[20,5]{0,1:T(8,128)S(1)} %get-tuple-element.65, f32[5,2000]{1,0:T(8,128)S(1)} %pad_maximum_fusion.3, f32[20,5]{0,1:T(8,128)S(1)} %get-tuple-element.64, ...), kind=kLoop, calls=%fused_computation.27 | loop fusion | flops 1800000 | bytes 842000 | tf_op jit(solution)/shard_map/reduce_sum | solution.py:93
  29.4 0.7 mul.530
  30.0 0.7 mul.533
  30.8 0.8 mul.539
  31.6 1.7 %mul.505 = f32[20,2000]{1,0:T(8,128)} multiply(f32[20,2000]{1,0:T(8,128)} %get-tuple-element.15, f32[20,2000]{1,0:T(8,128)} %get-tuple-element.12) | non-fusion elementwise | flops 40000 | bytes 480000 | tf_op jit(solution)/shard_map/mul | solution.py:96
  33.3 2.3 %copy.69 = f32[20,2000]{0,1:T(8,128)} copy(f32[20,2000]{1,0:T(8,128)} %mul.505) | data formatting | bytes 320000 | tf_op jit(solution)/shard_map/mul | solution.py:96
  35.5 2.2 %copy.70 = f32[20,2000]{0,1:T(8,128)} copy(f32[20,2000]{1,0:T(8,128)} %get-tuple-element.11) | data formatting | bytes 320000 | tf_op jit(solution)/shard_map/reduce_sum | solution.py:93
  37.8 1.3 %copy.71 = f32[20,2000]{0,1:T(8,128)} copy(f32[20,2000]{1,0:T(8,128)S(1)} %get-tuple-element.13) | data formatting | bytes 320000 | tf_op jit(solution)/shard_map/reduce_sum | solution.py:93
  39.1 1.4 %copy.72 = f32[20,2000]{0,1:T(8,128)} copy(f32[20,2000]{1,0:T(8,128)S(1)} %get-tuple-element.14) | data formatting | bytes 320000 | tf_op jit(solution)/shard_map/reduce_sum | solution.py:93
  40.5 2.0 %copy.83.courant_ref = f32[2000,1]{1,0:T(8,128)} copy(f32[2000,1]{0,1:T(1,128)} %get-tuple-element.60) | data formatting | bytes 16000 | tf_op jit(solution)/shard_map/mul | solution.py:337
  43.6 4.1 %fusion.17 = (f32[20]{0:T(128)S(1)}, f32[20]{0:T(128)S(1)}, f32[20,2000]{0,1:T(8,128)S(1)}) fusion(f32[2000]{0:T(1024)S(1)} %convert_reduce_fusion, f32[2000]{0:T(1024)S(1)} %bitcast.83, f32[2000]{0:T(1024)S(1)} %broadcast_multiply_fusion.1, f32[2000]{0:T(1024)S(1)} %convert_reduce_fusion.1, f32[2000]{0:T(1024)S(1)} %bitcast.82, f32[20,2000]{0,1:T(8,128)} %copy.72, ...), kind=kLoop, calls=%fused_computation.20 | loop fusion | flops 559960 | bytes 840160 | tf_op jit(solution)/shard_map/reduce_sum | solution.py:207
  47.9 0.4 copy.74
  48.6 1.1 maximum_bitcast_fusion.basis_ref
  49.7 7.3 %shard_map.208 = f32[180,2048]{1,0:T(8,128)} custom-call(bf16[2000,2048]{1,0:T(8,128)(2,1)} %dist_ref.3, bf16[5,180,400]{2,1,0:T(8,128)(2,1)} %maximum_bitcast_fusion.basis_ref), custom_call_target="tpu_custom_call" | custom-call | flops 1474560000 | bytes 9666560 | tf_op jit(solution)/shard_map/pallas_call | solution.py:179
  57.0 1.5 %slice_add_fusion = f32[60,2048]{1,0:T(8,128)S(1)} fusion(f32[180,2048]{1,0:T(8,128)} %shard_map.208), kind=kLoop, calls=%fused_computation.38 | loop fusion | flops 245760 | bytes 1966080 | tf_op jit(solution)/shard_map/add | solution.py:205
  58.7 1.3 %collective-permute-start.2 = (f32[20,2048]{1,0:T(8,128)S(1)}, f32[20,2048]{1,0:T(8,128)S(1)}, u32[]{:S(2)}, u32[]{:S(2)}) collective-permute-start(f32[20,2048]{1,0:T(8,128)S(1)} %fusion.25), channel_id=1, source_target_pairs={{0,32},{32,0},{64,96},{96,64},{1,33},{33,1},{65,97},{97,65},{2,34}... | collective-permute-start | bytes 491528 | tf_op jit(solution)/shard_map/ppermute | solution.py:254
  60.0 0.6 broadcast_subtract_fusion
  60.6 4.4 %collective-permute-done.2 = f32[20,2048]{1,0:T(8,128)S(1)} collective-permute-done((f32[20,2048]{1,0:T(8,128)S(1)}, f32[20,2048]{1,0:T(8,128)S(1)}, u32[]{:S(2)}, u32[]{:S(2)}) %collective-permute-start.2) | collective-permute-done | bytes 163872 | tf_op jit(solution)/shard_map/ppermute | solution.py:254
  65.0 2.8 %collective-permute-start.3 = (f32[20,2048]{1,0:T(8,128)S(1)}, f32[20,2048]{1,0:T(8,128)S(1)}, u32[]{:S(2)}, u32[]{:S(2)}) collective-permute-start(f32[20,2048]{1,0:T(8,128)S(1)} %add.252), channel_id=1, source_target_pairs={{0,64},{32,96},{64,0},{96,32},{1,65},{33,97},{65,1},{97,33},{2,66}... | collective-permute-start | bytes 491528 | tf_op jit(solution)/shard_map/ppermute | solution.py:254
  67.8 1.0 copy.91
  69.2 1.3 %broadcast_multiply_fusion = bf16[4096,8,21]{0,2,1:T(8,128)(2,1)} fusion(bf16[4096,21]{0,1:T(8,128)(2,1)S(1)} %slice_select_fusion, bf16[4096,8]{0,1:T(8,128)(2,1)S(1)} %fusion.26), kind=kLoop, calls=%fused_computation.35 | loop fusion | flops 688128 | bytes 1613824 | tf_op jit(solution)/shard_map/mul | solution.py:288
  70.5 3.0 %mul.595 = bf16[4096,168]{0,1:T(8,128)(2,1)} reshape(bf16[4096,8,21]{0,2,1:T(8,128)(2,1)} %broadcast_multiply_fusion) | data formatting | bytes 2752512 | tf_op jit(solution)/shard_map/mul | solution.py:288
  73.5 2.9 %dot_general.14 = bf16[8,21,4096]{2,1,0:T(8,128)(2,1)} reshape(bf16[168,4096]{1,0:T(8,128)(2,1)} %bitcast.70) | data formatting | bytes 2752512 | tf_op jit(solution)/shard_map/dot_general | solution.py:290
  76.4 2.4 %fusion.10 = bf16[21,8,256]{2,0,1:T(8,128)(2,1)S(1)} fusion(bf16[8,21,4096]{2,1,0:T(8,128)(2,1)} %dot_general.14, s32[4096]{0:T(1024)S(1)} %bitcast.85), kind=kOutput, calls=%fused_computation.14 | convolution fusion | flops 353413120 | bytes 1478656 | tf_op jit(solution)/shard_map/dot_general | solution.py:290
  79.3 0.8 fusion.19
  80.1 2.7 %collective-permute-done.4 = bf16[21,2048]{1,0:T(8,128)(2,1)S(1)} collective-permute-done((bf16[21,2048]{1,0:T(8,128)(2,1)S(1)}, bf16[21,2048]{1,0:T(8,128)(2,1)S(1)}, u32[]{:S(2)}, u32[]{:S(2)}) %collective-permute-start.4) | collective-permute-done | bytes 86048 | tf_op jit(solution)/shard_map/ppermute | solution.py:254
  82.8 1.1 collective-permute-start.5
  84.6 3.4 %collective-permute-done.5 = bf16[21,2048]{1,0:T(8,128)(2,1)S(1)} collective-permute-done((bf16[21,2048]{1,0:T(8,128)(2,1)S(1)}, bf16[21,2048]{1,0:T(8,128)(2,1)S(1)}, u32[]{:S(2)}, u32[]{:S(2)}) %collective-permute-start.5) | collective-permute-done | bytes 86048 | tf_op jit(solution)/shard_map/ppermute | solution.py:254
  88.2 2.0 %convolution_convert_fusion = bf16[20,512]{1,0:T(8,128)(2,1)S(1)} fusion(bf16[20,2048]{1,0:T(8,128)(2,1)S(1)} %fusion.24, bf16[2048,512]{1,0:T(8,128)(2,1)} %fusion.3), kind=kOutput, calls=%fused_computation.15 | convolution fusion | flops 41953280 | bytes 2199552 | tf_op jit(solution)/shard_map/dot_general | solution.py:320
  90.3 0.8 reshape.463
  91.1 9.6 %all-to-all-start.1 = ((bf16[32,2,160]{2,1,0:T(2,128)(2,1)}), bf16[32,2,160]{2,1,0:T(2,128)(2,1)S(1)}, u32[]{:S(2)}, u32[]{:S(2)}) async-start(bf16[32,2,160]{2,1,0:T(2,128)(2,1)} %reshape.463), calls=%async_computation.1 | async-start | bytes 65536 | tf_op jit(solution)/shard_map/all_to_all | solution.py:321
  100.7 1.2 pad_maximum_fusion.1.recon3_ref
  101.9 6.0 %all-to-all-done.1 = bf16[32,2,160]{2,1,0:T(2,128)(2,1)S(1)} async-done(((bf16[32,2,160]{2,1,0:T(2,128)(2,1)}), bf16[32,2,160]{2,1,0:T(2,128)(2,1)S(1)}, u32[]{:S(2)}, u32[]{:S(2)}) %all-to-all-start.1) | async-done | bytes 20512 | tf_op jit(solution)/shard_map/all_to_all | solution.py:321
  108.1 0.4 reduce-precision_convert_fusion.3
  108.5 0.7 pad_maximum_fusion.2.gain_ref
  109.3 15.5 %shard_map.209 = bf16[2000,2048]{1,0:T(8,128)(2,1)} custom-call(bf16[2000,2048]{1,0:T(8,128)(2,1)} %dist_ref.3, bf16[2000,1]{1,0:T(8,128)(2,1)} %copy-done.1, bf16[2000,1]{1,0:T(8,128)(2,1)} %copy-done, f32[2000,1]{1,0:T(8,128)} %copy.83.courant_ref, bf16[2000,60]{1,0:T(8,128)(2,1)} %pad_maximum_fusion.1.recon3_ref, ...), custom_call_target="tpu_custom_call" | custom-call | flops 532480000 | bytes 16384000 | tf_op jit(solution)/shard_map/pallas_call | solution.py:216
  (99 shorter events, 4.9 us)
Async XLA Ops:
  0.0 20.0 %copy-start.19 = (s32[20]{0:T(128)S(1)}, s32[20]{0:T(128)}, u32[]{:S(2)}) copy-start(s32[20]{0:T(128)} %constant.118.clone) | copy-start | bytes 244
  0.0 19.9 %copy-start.12 = (s32[256]{0:T(256)S(1)}, s32[256]{0:T(256)}, u32[]{:S(2)}) copy-start(s32[256]{0:T(256)} %param.26) | copy-start | bytes 3076
  0.0 20.0 %copy-start.11 = (f32[2000]{0:T(1024)S(1)}, f32[2000]{0:T(1024)}, u32[]{:S(2)}) copy-start(f32[2000]{0:T(1024)} %param.24) | copy-start | bytes 24004
  0.0 20.0 %copy-start.10 = (s32[1,32,16]{1,2,0:T(8,128)S(1)}, s32[1,32,16]{1,2,0:T(8,128)}, u32[]{:S(2)}) copy-start(s32[1,32,16]{1,2,0:T(8,128)} %param.28) | copy-start | bytes 6148
  0.0 20.2 %copy-start.9 = (s32[256,1]{0,1:T(1,128)S(1)}, s32[256,1]{0,1:T(1,128)}, u32[]{:S(2)}) copy-start(s32[256,1]{0,1:T(1,128)} %param.27) | copy-start | bytes 3076
  2.4 65.5 %all-to-all-start = ((bf16[32,128,22]{1,2,0:T(8,128)(2,1)}), bf16[32,128,22]{1,2,0:T(8,128)(2,1)}, u32[]{:S(2)}, u32[]{:S(2)}) async-start(bf16[32,128,22]{1,2,0:T(8,128)(2,1)} %broadcast_in_dim.15), calls=%async_computation | async-start | bytes 393216 | tf_op jit(solution)/shard_map/all_to_all | solution.py:274
  14.4 28.2 %collective-permute-start.1 = (bf16[2000,1]{1,0:T(8,128)(2,1)}, bf16[2000,1]{1,0:T(8,128)(2,1)S(1)}, u32[]{:S(2)}, u32[]{:S(2)}) collective-permute-start(bf16[2000,1]{1,0:T(8,128)(2,1)} %get-tuple-element.34), channel_id=1, source_target_pairs={{1,0},{2,1},{3,2},{4,3},{5,4},{6,5},{7,6},{8,7},{9,8},{10,9},{11,1... | collective-permute-start | bytes 12008 | tf_op jit(solution)/shard_map/ppermute | solution.py:61
  16.6 26.2 %collective-permute-start = (bf16[2000,1]{1,0:T(8,128)(2,1)}, bf16[2000,1]{1,0:T(8,128)(2,1)S(1)}, u32[]{:S(2)}, u32[]{:S(2)}) collective-permute-start(bf16[2000,1]{1,0:T(8,128)(2,1)} %get-tuple-element.35), channel_id=1, source_target_pairs={{0,1},{1,2},{2,3},{3,4},{4,5},{5,6},{6,7},{7,8},{8,9},{9,10},{10,1... | collective-permute-start | bytes 12008 | tf_op jit(solution)/shard_map/ppermute | solution.py:60
  21.3 2.8 %copy-start.17 = (s32[20]{0:T(128)S(1)}, s32[20]{0:T(128)}, u32[]{:S(2)}) copy-start(s32[20]{0:T(128)} %constant.115.clone) | copy-start | bytes 244
  21.3 2.8 %copy-start.18 = (s32[20]{0:T(128)S(1)}, s32[20]{0:T(128)}, u32[]{:S(2)}) copy-start(s32[20]{0:T(128)} %constant.114.clone) | copy-start | bytes 244
  21.3 2.8 %copy-start.15 = (s32[20]{0:T(128)S(1)}, s32[20]{0:T(128)}, u32[]{:S(2)}) copy-start(s32[20]{0:T(128)} %constant.117.clone) | copy-start | bytes 244
  21.3 2.8 %copy-start.16 = (s32[20]{0:T(128)S(1)}, s32[20]{0:T(128)}, u32[]{:S(2)}) copy-start(s32[20]{0:T(128)} %constant.116.clone) | copy-start | bytes 244
  21.3 3.9 %copy-start.5 = (f32[3,2000]{1,0:T(4,128)S(1)}, f32[3,2000]{1,0:T(4,128)}, u32[]{:S(2)}) copy-start(f32[3,2000]{1,0:T(4,128)} %param.23) | copy-start | bytes 72004
  39.1 4.5 %copy-start.6 = (f32[1,2000]{1,0:T(1,128)S(1)}, f32[1,2000]{1,0:T(1,128)}, u32[]{:S(2)}) copy-start(f32[1,2000]{1,0:T(1,128)} %get-tuple-element.32) | copy-start | bytes 24004
  39.1 4.5 %copy-start.7 = (f32[1,2000]{1,0:T(1,128)S(1)}, f32[1,2000]{1,0:T(1,128)}, u32[]{:S(2)}) copy-start(f32[1,2000]{1,0:T(1,128)} %get-tuple-element.33) | copy-start | bytes 24004
  42.5 0.8 copy-start
  42.8 0.8 copy-start.1
  43.6 4.7 %copy-start.3 = (f32[5,400]{1,0:T(8,128)S(1)}, f32[5,400]{1,0:T(8,128)}, u32[]{:S(2)}) copy-start(f32[5,400]{1,0:T(8,128)} %mul.530) | copy-start | bytes 24004
  43.6 4.7 %copy-start.4 = (f32[5,400]{1,0:T(8,128)S(1)}, f32[5,400]{1,0:T(8,128)}, u32[]{:S(2)}) copy-start(f32[5,400]{1,0:T(8,128)} %mul.533) | copy-start | bytes 24004
  57.0 3.0 %copy-start.8 = (f32[2048]{0:T(1024)S(1)}, f32[2048]{0:T(1024)}, u32[]{:S(2)}) copy-start(f32[2048]{0:T(1024)} %param.25) | copy-start | bytes 24580
  58.5 10.6 %copy-start.14 = (pred[21]{0:T(512)(128)(4,1)S(1)}, pred[21]{0:T(512)(128)(4,1)}, u32[]{:S(2)}) copy-start(pred[21]{0:T(512)(128)(4,1)} %constant.111.clone.1) | copy-start | bytes 67
  58.7 6.3 %collective-permute-start.2 = (f32[20,2048]{1,0:T(8,128)S(1)}, f32[20,2048]{1,0:T(8,128)S(1)}, u32[]{:S(2)}, u32[]{:S(2)}) collective-permute-start(f32[20,2048]{1,0:T(8,128)S(1)} %fusion.25), channel_id=1, source_target_pairs={{0,32},{32,0},{64,96},{96,64},{1,33},{33,1},{65,97},{97,65},{2,34}... | collective-permute-start | bytes 491528 | tf_op jit(solution)/shard_map/ppermute | solution.py:254
  65.0 19.0 %collective-permute-start.3 = (f32[20,2048]{1,0:T(8,128)S(1)}, f32[20,2048]{1,0:T(8,128)S(1)}, u32[]{:S(2)}, u32[]{:S(2)}) collective-permute-start(f32[20,2048]{1,0:T(8,128)S(1)} %add.252), channel_id=1, source_target_pairs={{0,64},{32,96},{64,0},{96,32},{1,65},{33,97},{65,1},{97,33},{2,66}... | collective-permute-start | bytes 491528 | tf_op jit(solution)/shard_map/ppermute | solution.py:254
  76.4 2.9 %copy-start.13 = (f32[20]{0:T(128)S(1)}, f32[20]{0:T(128)}, u32[]{:S(2)}) copy-start(f32[20]{0:T(128)} %constant.121) | copy-start | bytes 244
  78.9 3.9 %collective-permute-start.4 = (bf16[21,2048]{1,0:T(8,128)(2,1)S(1)}, bf16[21,2048]{1,0:T(8,128)(2,1)S(1)}, u32[]{:S(2)}, u32[]{:S(2)}) collective-permute-start(bf16[21,2048]{1,0:T(8,128)(2,1)S(1)} %bitcast.78), channel_id=1, source_target_pairs={{0,32},{32,0},{64,96},{96,64},{1,33},{33,1},{65,97},{97,65},{2,34}... | collective-permute-start | bytes 258056 | tf_op jit(solution)/shard_map/ppermute | solution.py:254
  82.8 5.2 %collective-permute-start.5 = (bf16[21,2048]{1,0:T(8,128)(2,1)S(1)}, bf16[21,2048]{1,0:T(8,128)(2,1)S(1)}, u32[]{:S(2)}, u32[]{:S(2)}) collective-permute-start(bf16[21,2048]{1,0:T(8,128)(2,1)S(1)} %add.293), channel_id=1, source_target_pairs={{0,64},{32,96},{64,0},{96,32},{1,65},{33,97},{65,1},{97,33},{2,66}... | collective-permute-start | bytes 258056 | tf_op jit(solution)/shard_map/ppermute | solution.py:254
  84.2 16.5 %copy-start.2 = (bf16[2000,20]{1,0:T(8,128)(2,1)S(1)}, bf16[2000,20]{1,0:T(8,128)(2,1)}, u32[]{:S(2)}) copy-start(bf16[2000,20]{1,0:T(8,128)(2,1)} %fusion.19) | copy-start | bytes 240004
  91.1 16.8 %all-to-all-start.1 = ((bf16[32,2,160]{2,1,0:T(2,128)(2,1)}), bf16[32,2,160]{2,1,0:T(2,128)(2,1)S(1)}, u32[]{:S(2)}, u32[]{:S(2)}) async-start(bf16[32,2,160]{2,1,0:T(2,128)(2,1)} %reshape.463), calls=%async_computation.1 | async-start | bytes 65536 | tf_op jit(solution)/shard_map/all_to_all | solution.py:321

commit v9 on v8

--- a/solution.py
+++ b/solution.py
@@ -49,6 +49,7 @@
     1.0,
 )
 ROW_BLOCK = 400
+CHUNK = 16
 CELL_HI = 8
 
 
@@ -156,11 +157,20 @@
 
 
 def relax_kernel(
-    dist_ref, left_ref, right_ref, courant_ref, recon3_ref, gain_ref, keep_ref, out_ref,
+    dist_ref, left_ref, right_ref, courant_ref, recon3_ref, gain_ref, keep_ref, out_ref, gained_ref,
 ):
-    read = transport_block(dist_ref, left_ref, right_ref, courant_ref).astype(jnp.float32)
-    gained = jnp.dot(recon3_ref[...], gain_ref[...], preferred_element_type=jnp.float32)
-    out_ref[...] = (read * keep_ref[...] + gained).astype(out_ref.dtype)
+    gained_ref[...] = jnp.dot(recon3_ref[...], gain_ref[...], preferred_element_type=jnp.float32)
+    keep = keep_ref[...]
+
+    def chunk(step, carry):
+        rows = pl.ds(pl.multiple_of(step * CHUNK, CHUNK), CHUNK)
+        read = transport_block(
+            dist_ref.at[rows], left_ref.at[rows], right_ref.at[rows], courant_ref.at[rows]
+        ).astype(jnp.float32)
+        out_ref[rows, :] = (read * keep + gained_ref[rows, :]).astype(out_ref.dtype)
+        return carry
+
+    lax.fori_loop(0, ROW_BLOCK // CHUNK, chunk, 0, unroll=True)
 
 
 def row_spec(width):
@@ -227,6 +237,7 @@
         ],
         out_specs=row_spec(cells),
         out_shape=jax.ShapeDtypeStruct((rows, cells), jnp.bfloat16),
+        scratch_shapes=[pltpu.VMEM((ROW_BLOCK, cells), jnp.float32)],
         compiler_params=pltpu.CompilerParams(dimension_semantics=("parallel",)),
         cost_estimate=pl.CostEstimate(
             flops=2 * rows * cells * 60 + 10 * rows * cells,

time: 126 us -> 124 us (0.984)
  Pallas kernels: 22.8 us -> 21 us
    pallas_call x1, Pallas kernels: 15.5 us -> 13.7 us  [relax_call(): pl.pallas_call(relax_kernel, grid=(steps,), in_specs=[row_spec(cells), ro...]
where the time goes in v9:
time: 124 us; the launch traced here: 123 us
  starting transfers between devices  30.4 us (25%)
  local copies, waits for them, and re-layouts  25.1 us (20%)
  other arithmetic  24.5 us (20%)
  Pallas kernels  21 us (17%)
  waiting for transfers between devices  16.5 us (13%)
  matrix products  4.81 us (4%)
    pallas_call x1, Pallas kernels, relax_call(): pl.pallas_call(relax_kernel, grid=(steps,), in_specs=[row_spec(cells), ro...  13.7 us
    ppermute x4, waiting for transfers between devices, sect_sum(): total = total + lax.ppermute(total, 'sect', pairs)  10.5 us
    all_to_all x1, starting transfers between devices, interface_rows(): gathered = lax.all_to_all(spread_out, 'space', 0, 0, tiled=True)  9.64 us
    all_to_all x1, starting transfers between devices, ghost_walls(): lax.all_to_all(outgoing, 'space', split_axis=1, concat_axis=1, tiled=True)  9.58 us
    pallas_call x1, Pallas kernels, moments_call(): pl.pallas_call(moments_kernel, grid=(steps,), in_specs=[row_spec(cells),...  7.31 us
    all_to_all x1, waiting for transfers between devices, ghost_walls(): lax.all_to_all(outgoing, 'space', split_axis=1, concat_axis=1, tiled=True)  6.05 us
    ppermute x4, starting transfers between devices, sect_sum(): total = total + lax.ppermute(total, 'sect', pairs)  5.63 us
    reduce_sum x3, local copies, waits for them, and re-layouts, pick(): return jnp.sum(select[:, :, None] * extended[None, :, :], axis=1)  4.96 us
  transfers between devices with their start and end apart: 8, of which 4 were waited for; matrix products, arithmetic and copies ran while one was open for 38% of the time, Pallas kernels for 6%

profile of v9, /device:TPU:1, one launch (start us, length us, event | category | flops | bytes accessed | tf_op | source)
XLA Modules:
  0.0 123.0 jit_solution(5332268098605262595)
XLA Ops:
  0.0 0.7 fusion.61
  0.8 0.8 convert_element_type.230
  1.7 0.7 broadcast_in_dim.15
  2.4 9.6 %all-to-all-start = ((bf16[32,128,22]{1,2,0:T(8,128)(2,1)}), bf16[32,128,22]{1,2,0:T(8,128)(2,1)}, u32[]{:S(2)}, u32[]{:S(2)}) async-start(bf16[32,128,22]{1,2,0:T(8,128)(2,1)} %broadcast_in_dim.15), calls=%async_computation | async-start | bytes 393216 | tf_op jit(solution)/shard_map/all_to_all | solution.py:285
  12.0 2.4 %fusion.65 = (bf16[2000,1]{1,0:T(8,128)(2,1)}, bf16[2000,1]{1,0:T(8,128)(2,1)}) fusion(bf16[2000,2048]{1,0:T(8,128)(2,1)} %dist_ref.3), kind=kLoop, calls=%fused_computation.167 | loop fusion | bytes 16000 | tf_op jit(solution)/shard_map/slice | solution.py:62
  14.4 2.2 %collective-permute-start.1 = (bf16[2000,1]{1,0:T(8,128)(2,1)}, bf16[2000,1]{1,0:T(8,128)(2,1)S(1)}, u32[]{:S(2)}, u32[]{:S(2)}) collective-permute-start(bf16[2000,1]{1,0:T(8,128)(2,1)} %get-tuple-element.34), channel_id=1, source_target_pairs={{1,0},{2,1},{3,2},{4,3},{5,4},{6,5},{7,6},{8,7},{9,8},{10,9},{11,1... | collective-permute-start | bytes 12008 | tf_op jit(solution)/shard_map/ppermute | solution.py:62
  16.6 3.4 %collective-permute-start = (bf16[2000,1]{1,0:T(8,128)(2,1)}, bf16[2000,1]{1,0:T(8,128)(2,1)S(1)}, u32[]{:S(2)}, u32[]{:S(2)}) collective-permute-start(bf16[2000,1]{1,0:T(8,128)(2,1)} %get-tuple-element.35), channel_id=1, source_target_pairs={{0,1},{1,2},{2,3},{3,4},{4,5},{5,6},{6,7},{7,8},{8,9},{9,10},{10,1... | collective-permute-start | bytes 12008 | tf_op jit(solution)/shard_map/ppermute | solution.py:61
  20.2 0.6 reduce-window.6
  21.4 2.3 %fusion.3 = bf16[2048,512]{1,0:T(8,128)(2,1)} fusion(s32[512]{0:T(512)S(1)} %broadcast_add_fusion), kind=kLoop, calls=%fused_computation.5 | loop fusion | flops 2097152 | bytes 2099200 | tf_op jit(solution)/shard_map/convert_element_type | solution.py:324
  24.1 0.6 fusion.57
  24.7 0.5 broadcast.442
  25.3 1.9 %add_reduce_fusion = (f32[2000]{0:T(1024)S(1)}, f32[2000]{0:T(1024)S(1)}, f32[2000]{0:T(1024)}, f32[1,2000]{1,0:T(1,128)}, f32[1,2000]{1,0:T(1,128)}, /*index=5*/f32[2000,1]{0,1:T(1,128)}) fusion(f32[]{:T(128)} %broadcast.442, f32[3,2000]{1,0:T(4,128)S(1)} %copy-done.5), kind=kLoop, calls=%fused_computation.135 | loop fusion | flops 10000 | bytes 56004 | tf_op jit(solution)/shard_map/add | solution.py:211
  27.2 2.2 %multiply_reduce_fusion.2 = (f32[20,2000]{1,0:T(8,128)}, f32[20,2000]{1,0:T(8,128)}, f32[20,2000]{1,0:T(8,128)S(1)}, f32[20,2000]{1,0:T(8,128)S(1)}, f32[20,2000]{1,0:T(8,128)}) fusion(f32[20,5]{0,1:T(8,128)S(1)} %get-tuple-element.65, f32[5,2000]{1,0:T(8,128)S(1)} %pad_maximum_fusion.3, f32[20,5]{0,1:T(8,128)S(1)} %get-tuple-element.64, ...), kind=kLoop, calls=%fused_computation.27 | loop fusion | flops 1800000 | bytes 842000 | tf_op jit(solution)/shard_map/reduce_sum | solution.py:94
  29.4 0.7 mul.530
  30.0 0.7 mul.533
  30.8 0.8 mul.539
  31.6 1.7 %mul.505 = f32[20,2000]{1,0:T(8,128)} multiply(f32[20,2000]{1,0:T(8,128)} %get-tuple-element.15, f32[20,2000]{1,0:T(8,128)} %get-tuple-element.12) | non-fusion elementwise | flops 40000 | bytes 480000 | tf_op jit(solution)/shard_map/mul | solution.py:97
  33.3 2.3 %copy.69 = f32[20,2000]{0,1:T(8,128)} copy(f32[20,2000]{1,0:T(8,128)} %mul.505) | data formatting | bytes 320000 | tf_op jit(solution)/shard_map/mul | solution.py:97
  35.5 2.2 %copy.70 = f32[20,2000]{0,1:T(8,128)} copy(f32[20,2000]{1,0:T(8,128)} %get-tuple-element.11) | data formatting | bytes 320000 | tf_op jit(solution)/shard_map/reduce_sum | solution.py:94
  37.8 1.3 %copy.71 = f32[20,2000]{0,1:T(8,128)} copy(f32[20,2000]{1,0:T(8,128)S(1)} %get-tuple-element.13) | data formatting | bytes 320000 | tf_op jit(solution)/shard_map/reduce_sum | solution.py:94
  39.1 1.4 %copy.72 = f32[20,2000]{0,1:T(8,128)} copy(f32[20,2000]{1,0:T(8,128)S(1)} %get-tuple-element.14) | data formatting | bytes 320000 | tf_op jit(solution)/shard_map/reduce_sum | solution.py:94
  40.5 2.0 %copy.83.courant_ref = f32[2000,1]{1,0:T(8,128)} copy(f32[2000,1]{0,1:T(1,128)} %get-tuple-element.60) | data formatting | bytes 16000 | tf_op jit(solution)/shard_map/mul | solution.py:348
  43.6 4.1 %fusion.17 = (f32[20]{0:T(128)S(1)}, f32[20]{0:T(128)S(1)}, f32[20,2000]{0,1:T(8,128)S(1)}) fusion(f32[2000]{0:T(1024)S(1)} %convert_reduce_fusion, f32[2000]{0:T(1024)S(1)} %bitcast.83, f32[2000]{0:T(1024)S(1)} %broadcast_multiply_fusion.1, f32[2000]{0:T(1024)S(1)} %convert_reduce_fusion.1, f32[2000]{0:T(1024)S(1)} %bitcast.82, f32[20,2000]{0,1:T(8,128)} %copy.72, ...), kind=kLoop, calls=%fused_computation.20 | loop fusion | flops 559960 | bytes 840160 | tf_op jit(solution)/shard_map/reduce_sum | solution.py:217
  47.9 0.4 copy.74
  48.6 1.1 maximum_bitcast_fusion.basis_ref
  49.7 7.3 %shard_map.208 = f32[180,2048]{1,0:T(8,128)} custom-call(bf16[2000,2048]{1,0:T(8,128)(2,1)} %dist_ref.3, bf16[5,180,400]{2,1,0:T(8,128)(2,1)} %maximum_bitcast_fusion.basis_ref), custom_call_target="tpu_custom_call" | custom-call | flops 1474560000 | bytes 9666560 | tf_op jit(solution)/shard_map/pallas_call | solution.py:189
  57.0 1.5 %slice_add_fusion = f32[60,2048]{1,0:T(8,128)S(1)} fusion(f32[180,2048]{1,0:T(8,128)} %shard_map.208), kind=kLoop, calls=%fused_computation.38 | loop fusion | flops 245760 | bytes 1966080 | tf_op jit(solution)/shard_map/add | solution.py:215
  58.7 1.3 %collective-permute-start.2 = (f32[20,2048]{1,0:T(8,128)S(1)}, f32[20,2048]{1,0:T(8,128)S(1)}, u32[]{:S(2)}, u32[]{:S(2)}) collective-permute-start(f32[20,2048]{1,0:T(8,128)S(1)} %fusion.25), channel_id=1, source_target_pairs={{0,32},{32,0},{64,96},{96,64},{1,33},{33,1},{65,97},{97,65},{2,34}... | collective-permute-start | bytes 491528 | tf_op jit(solution)/shard_map/ppermute | solution.py:265
  60.0 0.6 broadcast_subtract_fusion
  60.6 4.4 %collective-permute-done.2 = f32[20,2048]{1,0:T(8,128)S(1)} collective-permute-done((f32[20,2048]{1,0:T(8,128)S(1)}, f32[20,2048]{1,0:T(8,128)S(1)}, u32[]{:S(2)}, u32[]{:S(2)}) %collective-permute-start.2) | collective-permute-done | bytes 163872 | tf_op jit(solution)/shard_map/ppermute | solution.py:265
  65.0 2.8 %collective-permute-start.3 = (f32[20,2048]{1,0:T(8,128)S(1)}, f32[20,2048]{1,0:T(8,128)S(1)}, u32[]{:S(2)}, u32[]{:S(2)}) collective-permute-start(f32[20,2048]{1,0:T(8,128)S(1)} %add.252), channel_id=1, source_target_pairs={{0,64},{32,96},{64,0},{96,32},{1,65},{33,97},{65,1},{97,33},{2,66}... | collective-permute-start | bytes 491528 | tf_op jit(solution)/shard_map/ppermute | solution.py:265
  67.8 1.0 copy.91
  69.2 1.3 %broadcast_multiply_fusion = bf16[4096,8,21]{0,2,1:T(8,128)(2,1)} fusion(bf16[4096,21]{0,1:T(8,128)(2,1)S(1)} %slice_select_fusion, bf16[4096,8]{0,1:T(8,128)(2,1)S(1)} %fusion.26), kind=kLoop, calls=%fused_computation.35 | loop fusion | flops 688128 | bytes 1613824 | tf_op jit(solution)/shard_map/mul | solution.py:299
  70.5 3.0 %mul.595 = bf16[4096,168]{0,1:T(8,128)(2,1)} reshape(bf16[4096,8,21]{0,2,1:T(8,128)(2,1)} %broadcast_multiply_fusion) | data formatting | bytes 2752512 | tf_op jit(solution)/shard_map/mul | solution.py:299
  73.5 2.9 %dot_general.14 = bf16[8,21,4096]{2,1,0:T(8,128)(2,1)} reshape(bf16[168,4096]{1,0:T(8,128)(2,1)} %bitcast.70) | data formatting | bytes 2752512 | tf_op jit(solution)/shard_map/dot_general | solution.py:301
  76.4 2.4 %fusion.10 = bf16[21,8,256]{2,0,1:T(8,128)(2,1)S(1)} fusion(bf16[8,21,4096]{2,1,0:T(8,128)(2,1)} %dot_general.14, s32[4096]{0:T(1024)S(1)} %bitcast.85), kind=kOutput, calls=%fused_computation.14 | convolution fusion | flops 353413120 | bytes 1478656 | tf_op jit(solution)/shard_map/dot_general | solution.py:301
  79.3 0.8 fusion.19
  80.1 2.7 %collective-permute-done.4 = bf16[21,2048]{1,0:T(8,128)(2,1)S(1)} collective-permute-done((bf16[21,2048]{1,0:T(8,128)(2,1)S(1)}, bf16[21,2048]{1,0:T(8,128)(2,1)S(1)}, u32[]{:S(2)}, u32[]{:S(2)}) %collective-permute-start.4) | collective-permute-done | bytes 86048 | tf_op jit(solution)/shard_map/ppermute | solution.py:265
  82.8 1.1 collective-permute-start.5
  84.6 3.4 %collective-permute-done.5 = bf16[21,2048]{1,0:T(8,128)(2,1)S(1)} collective-permute-done((bf16[21,2048]{1,0:T(8,128)(2,1)S(1)}, bf16[21,2048]{1,0:T(8,128)(2,1)S(1)}, u32[]{:S(2)}, u32[]{:S(2)}) %collective-permute-start.5) | collective-permute-done | bytes 86048 | tf_op jit(solution)/shard_map/ppermute | solution.py:265
  88.2 2.0 %convolution_convert_fusion = bf16[20,512]{1,0:T(8,128)(2,1)S(1)} fusion(bf16[20,2048]{1,0:T(8,128)(2,1)S(1)} %fusion.24, bf16[2048,512]{1,0:T(8,128)(2,1)} %fusion.3), kind=kOutput, calls=%fused_computation.15 | convolution fusion | flops 41953280 | bytes 2199552 | tf_op jit(solution)/shard_map/dot_general | solution.py:331
  90.3 0.8 reshape.463
  91.1 9.6 %all-to-all-start.1 = ((bf16[32,2,160]{2,1,0:T(2,128)(2,1)}), bf16[32,2,160]{2,1,0:T(2,128)(2,1)S(1)}, u32[]{:S(2)}, u32[]{:S(2)}) async-start(bf16[32,2,160]{2,1,0:T(2,128)(2,1)} %reshape.463), calls=%async_computation.1 | async-start | bytes 65536 | tf_op jit(solution)/shard_map/all_to_all | solution.py:332
  100.7 1.2 pad_maximum_fusion.1.recon3_ref
  101.9 6.0 %all-to-all-done.1 = bf16[32,2,160]{2,1,0:T(2,128)(2,1)S(1)} async-done(((bf16[32,2,160]{2,1,0:T(2,128)(2,1)}), bf16[32,2,160]{2,1,0:T(2,128)(2,1)S(1)}, u32[]{:S(2)}, u32[]{:S(2)}) %all-to-all-start.1) | async-done | bytes 20512 | tf_op jit(solution)/shard_map/all_to_all | solution.py:332
  108.1 0.4 reduce-precision_convert_fusion.3
  108.5 0.7 pad_maximum_fusion.2.gain_ref
  109.3 13.7 %shard_map.209 = bf16[2000,2048]{1,0:T(8,128)(2,1)} custom-call(bf16[2000,2048]{1,0:T(8,128)(2,1)} %dist_ref.3, bf16[2000,1]{1,0:T(8,128)(2,1)} %copy-done.1, bf16[2000,1]{1,0:T(8,128)(2,1)} %copy-done, f32[2000,1]{1,0:T(8,128)} %copy.83.courant_ref, bf16[2000,60]{1,0:T(8,128)(2,1)} %pad_maximum_fusion.1.recon3_ref, ...), custom_call_target="tpu_custom_call" | custom-call | flops 532480000 | bytes 16384000 | tf_op jit(solution)/shard_map/pallas_call | solution.py:226
  (99 shorter events, 4.9 us)
Async XLA Ops:
  0.0 20.0 %copy-start.19 = (s32[20]{0:T(128)S(1)}, s32[20]{0:T(128)}, u32[]{:S(2)}) copy-start(s32[20]{0:T(128)} %constant.118.clone) | copy-start | bytes 244
  0.0 19.9 %copy-start.12 = (s32[256]{0:T(256)S(1)}, s32[256]{0:T(256)}, u32[]{:S(2)}) copy-start(s32[256]{0:T(256)} %param.26) | copy-start | bytes 3076
  0.0 20.0 %copy-start.11 = (f32[2000]{0:T(1024)S(1)}, f32[2000]{0:T(1024)}, u32[]{:S(2)}) copy-start(f32[2000]{0:T(1024)} %param.24) | copy-start | bytes 24004
  0.0 20.0 %copy-start.10 = (s32[1,32,16]{1,2,0:T(8,128)S(1)}, s32[1,32,16]{1,2,0:T(8,128)}, u32[]{:S(2)}) copy-start(s32[1,32,16]{1,2,0:T(8,128)} %param.28) | copy-start | bytes 6148
  0.0 20.2 %copy-start.9 = (s32[256,1]{0,1:T(1,128)S(1)}, s32[256,1]{0,1:T(1,128)}, u32[]{:S(2)}) copy-start(s32[256,1]{0,1:T(1,128)} %param.27) | copy-start | bytes 3076
  2.4 65.5 %all-to-all-start = ((bf16[32,128,22]{1,2,0:T(8,128)(2,1)}), bf16[32,128,22]{1,2,0:T(8,128)(2,1)}, u32[]{:S(2)}, u32[]{:S(2)}) async-start(bf16[32,128,22]{1,2,0:T(8,128)(2,1)} %broadcast_in_dim.15), calls=%async_computation | async-start | bytes 393216 | tf_op jit(solution)/shard_map/all_to_all | solution.py:285
  14.4 28.2 %collective-permute-start.1 = (bf16[2000,1]{1,0:T(8,128)(2,1)}, bf16[2000,1]{1,0:T(8,128)(2,1)S(1)}, u32[]{:S(2)}, u32[]{:S(2)}) collective-permute-start(bf16[2000,1]{1,0:T(8,128)(2,1)} %get-tuple-element.34), channel_id=1, source_target_pairs={{1,0},{2,1},{3,2},{4,3},{5,4},{6,5},{7,6},{8,7},{9,8},{10,9},{11,1... | collective-permute-start | bytes 12008 | tf_op jit(solution)/shard_map/ppermute | solution.py:62
  16.6 26.2 %collective-permute-start = (bf16[2000,1]{1,0:T(8,128)(2,1)}, bf16[2000,1]{1,0:T(8,128)(2,1)S(1)}, u32[]{:S(2)}, u32[]{:S(2)}) collective-permute-start(bf16[2000,1]{1,0:T(8,128)(2,1)} %get-tuple-element.35), channel_id=1, source_target_pairs={{0,1},{1,2},{2,3},{3,4},{4,5},{5,6},{6,7},{7,8},{8,9},{9,10},{10,1... | collective-permute-start | bytes 12008 | tf_op jit(solution)/shard_map/ppermute | solution.py:61
  21.3 2.8 %copy-start.17 = (s32[20]{0:T(128)S(1)}, s32[20]{0:T(128)}, u32[]{:S(2)}) copy-start(s32[20]{0:T(128)} %constant.115.clone) | copy-start | bytes 244
  21.3 2.8 %copy-start.18 = (s32[20]{0:T(128)S(1)}, s32[20]{0:T(128)}, u32[]{:S(2)}) copy-start(s32[20]{0:T(128)} %constant.114.clone) | copy-start | bytes 244
  21.3 2.8 %copy-start.15 = (s32[20]{0:T(128)S(1)}, s32[20]{0:T(128)}, u32[]{:S(2)}) copy-start(s32[20]{0:T(128)} %constant.117.clone) | copy-start | bytes 244
  21.3 2.8 %copy-start.16 = (s32[20]{0:T(128)S(1)}, s32[20]{0:T(128)}, u32[]{:S(2)}) copy-start(s32[20]{0:T(128)} %constant.116.clone) | copy-start | bytes 244
  21.3 3.9 %copy-start.5 = (f32[3,2000]{1,0:T(4,128)S(1)}, f32[3,2000]{1,0:T(4,128)}, u32[]{:S(2)}) copy-start(f32[3,2000]{1,0:T(4,128)} %param.23) | copy-start | bytes 72004
  39.1 4.5 %copy-start.6 = (f32[1,2000]{1,0:T(1,128)S(1)}, f32[1,2000]{1,0:T(1,128)}, u32[]{:S(2)}) copy-start(f32[1,2000]{1,0:T(1,128)} %get-tuple-element.32) | copy-start | bytes 24004
  39.1 4.5 %copy-start.7 = (f32[1,2000]{1,0:T(1,128)S(1)}, f32[1,2000]{1,0:T(1,128)}, u32[]{:S(2)}) copy-start(f32[1,2000]{1,0:T(1,128)} %get-tuple-element.33) | copy-start | bytes 24004
  42.5 0.8 copy-start
  42.8 0.8 copy-start.1
  43.6 4.7 %copy-start.3 = (f32[5,400]{1,0:T(8,128)S(1)}, f32[5,400]{1,0:T(8,128)}, u32[]{:S(2)}) copy-start(f32[5,400]{1,0:T(8,128)} %mul.530) | copy-start | bytes 24004
  43.6 4.7 %copy-start.4 = (f32[5,400]{1,0:T(8,128)S(1)}, f32[5,400]{1,0:T(8,128)}, u32[]{:S(2)}) copy-start(f32[5,400]{1,0:T(8,128)} %mul.533) | copy-start | bytes 24004
  57.0 3.0 %copy-start.8 = (f32[2048]{0:T(1024)S(1)}, f32[2048]{0:T(1024)}, u32[]{:S(2)}) copy-start(f32[2048]{0:T(1024)} %param.25) | copy-start | bytes 24580
  58.5 10.6 %copy-start.14 = (pred[21]{0:T(512)(128)(4,1)S(1)}, pred[21]{0:T(512)(128)(4,1)}, u32[]{:S(2)}) copy-start(pred[21]{0:T(512)(128)(4,1)} %constant.111.clone.1) | copy-start | bytes 67
  58.7 6.3 %collective-permute-start.2 = (f32[20,2048]{1,0:T(8,128)S(1)}, f32[20,2048]{1,0:T(8,128)S(1)}, u32[]{:S(2)}, u32[]{:S(2)}) collective-permute-start(f32[20,2048]{1,0:T(8,128)S(1)} %fusion.25), channel_id=1, source_target_pairs={{0,32},{32,0},{64,96},{96,64},{1,33},{33,1},{65,97},{97,65},{2,34}... | collective-permute-start | bytes 491528 | tf_op jit(solution)/shard_map/ppermute | solution.py:265
  65.0 19.0 %collective-permute-start.3 = (f32[20,2048]{1,0:T(8,128)S(1)}, f32[20,2048]{1,0:T(8,128)S(1)}, u32[]{:S(2)}, u32[]{:S(2)}) collective-permute-start(f32[20,2048]{1,0:T(8,128)S(1)} %add.252), channel_id=1, source_target_pairs={{0,64},{32,96},{64,0},{96,32},{1,65},{33,97},{65,1},{97,33},{2,66}... | collective-permute-start | bytes 491528 | tf_op jit(solution)/shard_map/ppermute | solution.py:265
  76.4 2.9 %copy-start.13 = (f32[20]{0:T(128)S(1)}, f32[20]{0:T(128)}, u32[]{:S(2)}) copy-start(f32[20]{0:T(128)} %constant.121) | copy-start | bytes 244
  78.9 3.9 %collective-permute-start.4 = (bf16[21,2048]{1,0:T(8,128)(2,1)S(1)}, bf16[21,2048]{1,0:T(8,128)(2,1)S(1)}, u32[]{:S(2)}, u32[]{:S(2)}) collective-permute-start(bf16[21,2048]{1,0:T(8,128)(2,1)S(1)} %bitcast.78), channel_id=1, source_target_pairs={{0,32},{32,0},{64,96},{96,64},{1,33},{33,1},{65,97},{97,65},{2,34}... | collective-permute-start | bytes 258056 | tf_op jit(solution)/shard_map/ppermute | solution.py:265
  82.8 5.2 %collective-permute-start.5 = (bf16[21,2048]{1,0:T(8,128)(2,1)S(1)}, bf16[21,2048]{1,0:T(8,128)(2,1)S(1)}, u32[]{:S(2)}, u32[]{:S(2)}) collective-permute-start(bf16[21,2048]{1,0:T(8,128)(2,1)S(1)} %add.293), channel_id=1, source_target_pairs={{0,64},{32,96},{64,0},{96,32},{1,65},{33,97},{65,1},{97,33},{2,66}... | collective-permute-start | bytes 258056 | tf_op jit(solution)/shard_map/ppermute | solution.py:265
  84.2 16.5 %copy-start.2 = (bf16[2000,20]{1,0:T(8,128)(2,1)S(1)}, bf16[2000,20]{1,0:T(8,128)(2,1)}, u32[]{:S(2)}) copy-start(bf16[2000,20]{1,0:T(8,128)(2,1)} %fusion.19) | copy-start | bytes 240004
  91.1 16.8 %all-to-all-start.1 = ((bf16[32,2,160]{2,1,0:T(2,128)(2,1)}), bf16[32,2,160]{2,1,0:T(2,128)(2,1)S(1)}, u32[]{:S(2)}, u32[]{:S(2)}) async-start(bf16[32,2,160]{2,1,0:T(2,128)(2,1)} %reshape.463), calls=%async_computation.1 | async-start | bytes 65536 | tf_op jit(solution)/shard_map/all_to_all | solution.py:332

commit v10 on v9

--- a/solution.py
+++ b/solution.py
@@ -355,10 +355,9 @@
     select, land = lax.optimization_barrier((select, land))
     recon = recon_basis(velocity)
     recon3 = lax.optimization_barrier(jnp.concatenate([recon, recon, recon], axis=1))
-    moments = sect_sum(partial_moments)
     partial_rows = interface_rows(plenum_moments, iface_cell, cells, slab_base)
-    rows = sect_sum(partial_rows.astype(jnp.bfloat16)).astype(jnp.float32)
-    targets = inject(es_targets(moments), rows).astype(jnp.bfloat16)
+    summed = sect_sum(jnp.concatenate([partial_moments, partial_rows], axis=0))
+    targets = inject(es_targets(summed[:MOMENTS]), summed[MOMENTS:]).astype(jnp.bfloat16)
     wall_moments = ghost_walls(targets, select, land)
     rate = collision_rate[None, :]
     gain = split_three(rate * targets.astype(jnp.float32) + WALL_SHARE * wall_moments)

time: 124 us -> 113 us (0.911)
  local copies, waits for them, and re-layouts: 25.1 us -> 17.8 us
  waiting for transfers between devices: 16.5 us -> 21.5 us
  other arithmetic: 24.5 us -> 20.9 us
  starting transfers between devices: 30.4 us -> 27.5 us
  matrix products: 4.81 us -> 3.4 us
    ppermute x4 -> x2, waiting for transfers between devices: 10.5 us -> 15.4 us  [sect_sum(): total = total + lax.ppermute(total, 'sect', pairs)]
    mul x1, local copies, waits for them, and re-layouts: 2.26 us -> 0.35 us  [hermite(): element = first * second * third]
    mul x1, other arithmetic: 1.73 us -> 0.03 us  [hermite(): element = first * second * third]
    ppermute x4 -> x2, starting transfers between devices: 5.63 us -> 4.04 us  [sect_sum(): total = total + lax.ppermute(total, 'sect', pairs)]
    mul x1, local copies, waits for them, and re-layouts: 2.97 us -> 1.54 us  [fold_interface(): pick_hi[:, :, None] * extended[:, None, :]]
    all_to_all x1, starting transfers between devices: 9.58 us -> 8.16 us  [ghost_walls(): lax.all_to_all(outgoing, 'space', split_axis=1, concat_axis=1, tiled=True)]
    dot_general x1, matrix products: 2.41 us -> 1 us  [fold_interface(): lax.dot_general(spread, pick_lo, (((0,), (0,)), ((), ())), preferred_elem...]
  transfers between devices with their start and end apart: 8 -> 6, of which waited for: 4 -> 3; matrix products, arithmetic and copies ran while one was open for 38% -> 23% of each run, Pallas kernels for 6% -> 6%
where the time goes in v10:
time: 113 us
  starting transfers between devices  27.5 us (24%)
  waiting for transfers between devices  21.5 us (19%)
  Pallas kernels  21 us (19%)
  other arithmetic  20.9 us (18%)
  local copies, waits for them, and re-layouts  17.8 us (16%)
  matrix products  3.4 us (3%)
    ppermute x2, waiting for transfers between devices, sect_sum(): total = total + lax.ppermute(total, 'sect', pairs)  15.4 us
    pallas_call x1, Pallas kernels, relax_call(): pl.pallas_call(relax_kernel, grid=(steps,), in_specs=[row_spec(cells), ro...  13.7 us
    all_to_all x1, starting transfers between devices, interface_rows(): gathered = lax.all_to_all(spread_out, 'space', 0, 0, tiled=True)  9.64 us
    all_to_all x1, starting transfers between devices, ghost_walls(): lax.all_to_all(outgoing, 'space', split_axis=1, concat_axis=1, tiled=True)  8.16 us
    pallas_call x1, Pallas kernels, moments_call(): pl.pallas_call(moments_kernel, grid=(steps,), in_specs=[row_spec(cells),...  7.3 us
    all_to_all x1, waiting for transfers between devices, ghost_walls(): lax.all_to_all(outgoing, 'space', split_axis=1, concat_axis=1, tiled=True)  6.04 us
    ppermute x2, starting transfers between devices, sect_sum(): total = total + lax.ppermute(total, 'sect', pairs)  4.04 us
    reduce_sum x3, local copies, waits for them, and re-layouts, pick(): return jnp.sum(select[:, :, None] * extended[None, :, :], axis=1)  3.95 us
  transfers between devices with their start and end apart: 6, of which 3 were waited for; matrix products, arithmetic and copies ran while one was open for 23% of the time, Pallas kernels for 6%

profile of v10, /device:TPU:1, one launch (start us, length us, event | category | flops | bytes accessed | tf_op | source)
XLA Modules:
  0.0 112.6 jit_solution(7960772624887300664)
XLA Ops:
  0.0 0.7 fusion.58
  0.8 0.8 convert_element_type.218
  1.7 0.7 broadcast_in_dim.15
  2.4 9.6 %all-to-all-start = ((bf16[32,128,22]{1,2,0:T(8,128)(2,1)}), bf16[32,128,22]{1,2,0:T(8,128)(2,1)}, u32[]{:S(2)}, u32[]{:S(2)}) async-start(bf16[32,128,22]{1,2,0:T(8,128)(2,1)} %broadcast_in_dim.15), calls=%async_computation | async-start | bytes 393216 | tf_op jit(solution)/shard_map/all_to_all | solution.py:285
  12.1 2.4 %fusion.63 = (bf16[2000,1]{1,0:T(8,128)(2,1)}, bf16[2000,1]{1,0:T(8,128)(2,1)}) fusion(bf16[2000,2048]{1,0:T(8,128)(2,1)} %dist_ref.3), kind=kLoop, calls=%fused_computation.167 | loop fusion | bytes 16000 | tf_op jit(solution)/shard_map/slice | solution.py:62
  14.5 2.3 %collective-permute-start.1 = (bf16[2000,1]{1,0:T(8,128)(2,1)}, bf16[2000,1]{1,0:T(8,128)(2,1)S(1)}, u32[]{:S(2)}, u32[]{:S(2)}) collective-permute-start(bf16[2000,1]{1,0:T(8,128)(2,1)} %get-tuple-element.34), channel_id=1, source_target_pairs={{1,0},{2,1},{3,2},{4,3},{5,4},{6,5},{7,6},{8,7},{9,8},{10,9},{11,1... | collective-permute-start | bytes 12008 | tf_op jit(solution)/shard_map/ppermute | solution.py:62
  16.8 3.4 %collective-permute-start = (bf16[2000,1]{1,0:T(8,128)(2,1)}, bf16[2000,1]{1,0:T(8,128)(2,1)S(1)}, u32[]{:S(2)}, u32[]{:S(2)}) collective-permute-start(bf16[2000,1]{1,0:T(8,128)(2,1)} %get-tuple-element.35), channel_id=1, source_target_pairs={{0,1},{1,2},{2,3},{3,4},{4,5},{5,6},{6,7},{7,8},{8,9},{9,10},{10,1... | collective-permute-start | bytes 12008 | tf_op jit(solution)/shard_map/ppermute | solution.py:61
  20.2 0.6 reduce-window.6
  21.3 2.3 %fusion.3 = bf16[2048,512]{1,0:T(8,128)(2,1)} fusion(s32[512]{0:T(512)S(1)} %broadcast_add_fusion), kind=kLoop, calls=%fused_computation.5 | loop fusion | flops 2097152 | bytes 2099200 | tf_op jit(solution)/shard_map/convert_element_type | solution.py:324
  23.7 0.5 broadcast.442
  24.2 1.2 %add_reduce_fusion = (f32[2000]{0:T(1024)S(1)}, f32[2000]{0:T(1024)S(1)}, f32[2000]{0:T(1024)S(1)}, f32[1,2000]{1,0:T(1,128)S(1)}, f32[1,2000]{1,0:T(1,128)}, /*index=5*/f32[2000,1]{0,1:T(1,128)S(1)}) fusion(f32[]{:T(128)} %broadcast.442, f32[3,2000]{1,0:T(4,128)S(1)} %copy-done.3), kind=kLoop, calls=%fused_computation.134 | loop fusion | flops 10000 | bytes 56004 | tf_op jit(solution)/shard_map/add | solution.py:211
  25.5 1.2 %multiply_reduce_fusion.2 = (f32[20,2000]{1,0:T(8,128)}, f32[20,2000]{1,0:T(8,128)S(1)}, f32[20,2000]{1,0:T(8,128)S(1)}, f32[20,2000]{1,0:T(8,128)S(1)}, f32[20,2000]{1,0:T(8,128)S(1)}) fusion(f32[20,5]{0,1:T(8,128)S(1)} %get-tuple-element.64, f32[5,2000]{1,0:T(8,128)S(1)} %pad_maximum_fusion.4, f32[20,5]{0,1:T(8,128)S(1)} %get-tuple-element.63, ...), kind=kLoop, calls=%fused_computation.26 | loop fusion | flops 1800000 | bytes 842000 | tf_op jit(solution)/shard_map/reduce_sum | solution.py:94
  26.9 0.7 eq.366
  27.8 0.4 copy.69
  28.2 1.3 %copy.70 = f32[20,2000]{0,1:T(8,128)S(1)} copy(f32[20,2000]{1,0:T(8,128)} %get-tuple-element.11) | data formatting | bytes 320000 | tf_op jit(solution)/shard_map/reduce_sum | solution.py:94
  29.4 1.3 %copy.71 = f32[20,2000]{0,1:T(8,128)} copy(f32[20,2000]{1,0:T(8,128)S(1)} %get-tuple-element.13) | data formatting | bytes 320000 | tf_op jit(solution)/shard_map/reduce_sum | solution.py:94
  30.8 1.3 %copy.72 = f32[20,2000]{0,1:T(8,128)} copy(f32[20,2000]{1,0:T(8,128)S(1)} %get-tuple-element.14) | data formatting | bytes 320000 | tf_op jit(solution)/shard_map/reduce_sum | solution.py:94
  32.4 0.2 convert_reduce_fusion.1
  32.6 0.3 copy-done
  32.9 0.3 copy-done.1
  33.2 3.5 %fusion.14 = (f32[20]{0:T(128)S(1)}, f32[20]{0:T(128)S(1)}, f32[20,2000]{0,1:T(8,128)S(1)}) fusion(f32[2000]{0:T(1024)S(1)} %convert_reduce_fusion, f32[2000]{0:T(1024)S(1)} %bitcast.81, f32[2000]{0:T(1024)S(1)} %broadcast_multiply_fusion.1, f32[2000]{0:T(1024)S(1)} %convert_reduce_fusion.1, f32[2000]{0:T(1024)S(1)} %bitcast.80, f32[20,2000]{0,1:T(8,128)} %copy.72, ...), kind=kLoop, calls=%fused_computation.19 | loop fusion | flops 559960 | bytes 840160 | tf_op jit(solution)/shard_map/reduce_sum | solution.py:217
  36.9 0.4 copy.74
  37.6 1.1 maximum_bitcast_fusion.basis_ref
  38.7 7.3 %shard_map.208 = f32[180,2048]{1,0:T(8,128)} custom-call(bf16[2000,2048]{1,0:T(8,128)(2,1)} %dist_ref.3, bf16[5,180,400]{2,1,0:T(8,128)(2,1)} %maximum_bitcast_fusion.basis_ref), custom_call_target="tpu_custom_call" | custom-call | flops 1474560000 | bytes 9666560 | tf_op jit(solution)/shard_map/pallas_call | solution.py:189
  46.0 1.5 %slice_add_fusion = f32[60,2048]{1,0:T(8,128)S(1)} fusion(f32[180,2048]{1,0:T(8,128)} %shard_map.208), kind=kLoop, calls=%fused_computation.37 | loop fusion | flops 245760 | bytes 1966080 | tf_op jit(solution)/shard_map/add | solution.py:215
  47.8 1.0 copy.91
  49.3 1.5 %mul.561 = bf16[4096,168]{0,1:T(8,128)(2,1)} reshape(bf16[4096,8,21]{0,2,1:T(8,128)(2,1)S(1)} %broadcast_multiply_fusion) | data formatting | bytes 2752512 | tf_op jit(solution)/shard_map/mul | solution.py:299
  50.9 1.8 %dot_general.14 = bf16[8,21,4096]{2,1,0:T(8,128)(2,1)S(1)} reshape(bf16[168,4096]{1,0:T(8,128)(2,1)} %bitcast.68) | data formatting | bytes 2752512 | tf_op jit(solution)/shard_map/dot_general | solution.py:301
  52.7 1.0 fusion.7
  53.8 0.8 pad_maximum_fusion.2
  54.6 1.2 %collective-permute-start.2 = (f32[41,2048]{1,0:T(8,128)}, f32[41,2048]{1,0:T(8,128)}, u32[]{:S(2)}, u32[]{:S(2)}) collective-permute-start(f32[41,2048]{1,0:T(8,128)} %pad_maximum_fusion.2), channel_id=1, source_target_pairs={{0,32},{32,0},{64,96},{96,64},{1,33},{33,1},{65,97},{97,65},{2,34}... | collective-permute-start | bytes 1007624 | tf_op jit(solution)/shard_map/ppermute | solution.py:265
  55.9 0.4 fusion.4
  56.3 1.4 %copy.83.courant_ref = f32[2000,1]{1,0:T(8,128)} copy(f32[2000,1]{0,1:T(1,128)S(1)} %get-tuple-element.59) | data formatting | bytes 16000 | tf_op jit(solution)/shard_map/mul | solution.py:348
  57.7 0.6 broadcast_subtract_fusion
  58.3 7.1 %collective-permute-done.2 = f32[41,2048]{1,0:T(8,128)} collective-permute-done((f32[41,2048]{1,0:T(8,128)}, f32[41,2048]{1,0:T(8,128)}, u32[]{:S(2)}, u32[]{:S(2)}) %collective-permute-start.2) | collective-permute-done | bytes 335904 | tf_op jit(solution)/shard_map/ppermute | solution.py:265
  65.4 1.1 fusion.61
  66.4 2.8 %collective-permute-start.3 = (f32[41,2048]{1,0:T(8,128)S(1)}, f32[41,2048]{1,0:T(8,128)S(1)}, u32[]{:S(2)}, u32[]{:S(2)}) collective-permute-start(f32[41,2048]{1,0:T(8,128)S(1)} %fusion.61), channel_id=1, source_target_pairs={{0,64},{32,96},{64,0},{96,32},{1,65},{33,97},{65,1},{97,33},{2,66}... | collective-permute-start | bytes 1007624 | tf_op jit(solution)/shard_map/ppermute | solution.py:265
  69.2 0.8 fusion.16
  70.1 8.3 %collective-permute-done.3 = f32[41,2048]{1,0:T(8,128)S(1)} collective-permute-done((f32[41,2048]{1,0:T(8,128)S(1)}, f32[41,2048]{1,0:T(8,128)S(1)}, u32[]{:S(2)}, u32[]{:S(2)}) %collective-permute-start.3) | collective-permute-done | bytes 335904 | tf_op jit(solution)/shard_map/ppermute | solution.py:265
  78.9 0.2 stack.3
  79.2 2.0 %convolution_convert_fusion = bf16[20,512]{1,0:T(8,128)(2,1)S(1)} fusion(bf16[20,2048]{1,0:T(8,128)(2,1)S(1)} %fusion.21, bf16[2048,512]{1,0:T(8,128)(2,1)} %fusion.3), kind=kOutput, calls=%fused_computation.14 | convolution fusion | flops 41953280 | bytes 2199552 | tf_op jit(solution)/shard_map/dot_general | solution.py:331
  81.3 0.8 reshape.465
  82.1 8.2 %all-to-all-start.1 = ((bf16[32,2,160]{2,1,0:T(2,128)(2,1)}), bf16[32,2,160]{2,1,0:T(2,128)(2,1)S(1)}, u32[]{:S(2)}, u32[]{:S(2)}) async-start(bf16[32,2,160]{2,1,0:T(2,128)(2,1)} %reshape.465), calls=%async_computation.1 | async-start | bytes 65536 | tf_op jit(solution)/shard_map/all_to_all | solution.py:332
  90.3 1.2 %pad_maximum_fusion.1.recon3_ref = bf16[2000,60]{1,0:T(8,128)(2,1)} fusion(bf16[2000,20]{1,0:T(8,128)(2,1)S(1)} %copy-done.2), kind=kLoop, calls=%fused_computation.42 | loop fusion | flops 720000 | bytes 320000 | tf_op jit(solution)/shard_map/concatenate | solution.py:357
  91.5 6.0 %all-to-all-done.1 = bf16[32,2,160]{2,1,0:T(2,128)(2,1)S(1)} async-done(((bf16[32,2,160]{2,1,0:T(2,128)(2,1)}), bf16[32,2,160]{2,1,0:T(2,128)(2,1)S(1)}, u32[]{:S(2)}, u32[]{:S(2)}) %all-to-all-start.1) | async-done | bytes 20512 | tf_op jit(solution)/shard_map/all_to_all | solution.py:332
  97.7 0.4 reduce-precision_convert_fusion.3
  98.1 0.8 pad_maximum_fusion.3.gain_ref
  98.9 13.7 %shard_map.209 = bf16[2000,2048]{1,0:T(8,128)(2,1)} custom-call(bf16[2000,2048]{1,0:T(8,128)(2,1)} %dist_ref.3, bf16[2000,1]{1,0:T(8,128)(2,1)} %copy-done.1, bf16[2000,1]{1,0:T(8,128)(2,1)} %copy-done, f32[2000,1]{1,0:T(8,128)} %copy.83.courant_ref, bf16[2000,60]{1,0:T(8,128)(2,1)} %pad_maximum_fusion.1.recon3_ref, ...), custom_call_target="tpu_custom_call" | custom-call | flops 532480000 | bytes 16384000 | tf_op jit(solution)/shard_map/pallas_call | solution.py:226
  (90 shorter events, 3.5 us)
Async XLA Ops:
  0.0 20.2 %copy-start.17 = (s32[20]{0:T(128)S(1)}, s32[20]{0:T(128)}, u32[]{:S(2)}) copy-start(s32[20]{0:T(128)} %constant.118.clone) | copy-start | bytes 244
  0.0 20.2 %copy-start.10 = (s32[256]{0:T(256)S(1)}, s32[256]{0:T(256)}, u32[]{:S(2)}) copy-start(s32[256]{0:T(256)} %param.26) | copy-start | bytes 3076
  0.0 20.2 %copy-start.9 = (f32[2000]{0:T(1024)S(1)}, f32[2000]{0:T(1024)}, u32[]{:S(2)}) copy-start(f32[2000]{0:T(1024)} %param.24) | copy-start | bytes 24004
  0.0 20.2 %copy-start.6 = (s32[256,1]{0,1:T(1,128)S(1)}, s32[256,1]{0,1:T(1,128)}, u32[]{:S(2)}) copy-start(s32[256,1]{0,1:T(1,128)} %param.27) | copy-start | bytes 3076
  2.4 45.4 %all-to-all-start = ((bf16[32,128,22]{1,2,0:T(8,128)(2,1)}), bf16[32,128,22]{1,2,0:T(8,128)(2,1)}, u32[]{:S(2)}, u32[]{:S(2)}) async-start(bf16[32,128,22]{1,2,0:T(8,128)(2,1)} %broadcast_in_dim.15), calls=%async_computation | async-start | bytes 393216 | tf_op jit(solution)/shard_map/all_to_all | solution.py:285
  12.0 11.7 %copy-start.15 = (s32[20]{0:T(128)S(1)}, s32[20]{0:T(128)}, u32[]{:S(2)}) copy-start(s32[20]{0:T(128)} %constant.115.clone) | copy-start | bytes 244
  12.0 11.6 %copy-start.16 = (s32[20]{0:T(128)S(1)}, s32[20]{0:T(128)}, u32[]{:S(2)}) copy-start(s32[20]{0:T(128)} %constant.114.clone) | copy-start | bytes 244
  12.0 11.6 %copy-start.13 = (s32[20]{0:T(128)S(1)}, s32[20]{0:T(128)}, u32[]{:S(2)}) copy-start(s32[20]{0:T(128)} %constant.117.clone) | copy-start | bytes 244
  12.0 11.6 %copy-start.14 = (s32[20]{0:T(128)S(1)}, s32[20]{0:T(128)}, u32[]{:S(2)}) copy-start(s32[20]{0:T(128)} %constant.116.clone) | copy-start | bytes 244
  12.0 12.2 %copy-start.3 = (f32[3,2000]{1,0:T(4,128)S(1)}, f32[3,2000]{1,0:T(4,128)}, u32[]{:S(2)}) copy-start(f32[3,2000]{1,0:T(4,128)} %param.23) | copy-start | bytes 72004
  14.5 12.4 %copy-start.8 = (s32[1,32,16]{1,2,0:T(8,128)S(1)}, s32[1,32,16]{1,2,0:T(8,128)}, u32[]{:S(2)}) copy-start(s32[1,32,16]{1,2,0:T(8,128)} %param.28) | copy-start | bytes 6148
  14.5 17.7 %collective-permute-start.1 = (bf16[2000,1]{1,0:T(8,128)(2,1)}, bf16[2000,1]{1,0:T(8,128)(2,1)S(1)}, u32[]{:S(2)}, u32[]{:S(2)}) collective-permute-start(bf16[2000,1]{1,0:T(8,128)(2,1)} %get-tuple-element.34), channel_id=1, source_target_pairs={{1,0},{2,1},{3,2},{4,3},{5,4},{6,5},{7,6},{8,7},{9,8},{10,9},{11,1... | collective-permute-start | bytes 12008 | tf_op jit(solution)/shard_map/ppermute | solution.py:62
  16.8 15.6 %collective-permute-start = (bf16[2000,1]{1,0:T(8,128)(2,1)}, bf16[2000,1]{1,0:T(8,128)(2,1)S(1)}, u32[]{:S(2)}, u32[]{:S(2)}) collective-permute-start(bf16[2000,1]{1,0:T(8,128)(2,1)} %get-tuple-element.35), channel_id=1, source_target_pairs={{0,1},{1,2},{2,3},{3,4},{4,5},{5,6},{6,7},{7,8},{8,9},{9,10},{10,1... | collective-permute-start | bytes 12008 | tf_op jit(solution)/shard_map/ppermute | solution.py:61
  30.8 2.4 %copy-start.4 = (f32[1,2000]{1,0:T(1,128)S(1)}, f32[1,2000]{1,0:T(1,128)}, u32[]{:S(2)}) copy-start(f32[1,2000]{1,0:T(1,128)} %get-tuple-element.30) | copy-start | bytes 24004
  32.1 0.8 copy-start
  32.4 0.8 copy-start.1
  46.0 2.9 %copy-start.12 = (pred[21]{0:T(512)(128)(4,1)S(1)}, pred[21]{0:T(512)(128)(4,1)}, u32[]{:S(2)}) copy-start(pred[21]{0:T(512)(128)(4,1)} %constant.108.clone.1) | copy-start | bytes 67
  52.6 3.2 %copy-start.7 = (s32[512]{0:T(512)S(1)}, s32[512]{0:T(512)}, u32[]{:S(2)}) copy-start(s32[512]{0:T(512)} %eq.366) | copy-start | bytes 6148
  53.8 3.9 %copy-start.5 = (f32[2048]{0:T(1024)S(1)}, f32[2048]{0:T(1024)}, u32[]{:S(2)}) copy-start(f32[2048]{0:T(1024)} %param.25) | copy-start | bytes 24580
  54.6 14.6 %copy-start.11 = (f32[20]{0:T(128)S(1)}, f32[20]{0:T(128)}, u32[]{:S(2)}) copy-start(f32[20]{0:T(128)} %constant.121) | copy-start | bytes 244
  54.6 10.7 %collective-permute-start.2 = (f32[41,2048]{1,0:T(8,128)}, f32[41,2048]{1,0:T(8,128)}, u32[]{:S(2)}, u32[]{:S(2)}) collective-permute-start(f32[41,2048]{1,0:T(8,128)} %pad_maximum_fusion.2), channel_id=1, source_target_pairs={{0,32},{32,0},{64,96},{96,64},{1,33},{33,1},{65,97},{97,65},{2,34}... | collective-permute-start | bytes 1007624 | tf_op jit(solution)/shard_map/ppermute | solution.py:265
  66.4 12.0 %collective-permute-start.3 = (f32[41,2048]{1,0:T(8,128)S(1)}, f32[41,2048]{1,0:T(8,128)S(1)}, u32[]{:S(2)}, u32[]{:S(2)}) collective-permute-start(f32[41,2048]{1,0:T(8,128)S(1)} %fusion.61), channel_id=1, source_target_pairs={{0,64},{32,96},{64,0},{96,32},{1,65},{33,97},{65,1},{97,33},{2,66}... | collective-permute-start | bytes 1007624 | tf_op jit(solution)/shard_map/ppermute | solution.py:265
  78.5 11.8 %copy-start.2 = (bf16[2000,20]{1,0:T(8,128)(2,1)S(1)}, bf16[2000,20]{1,0:T(8,128)(2,1)}, u32[]{:S(2)}) copy-start(bf16[2000,20]{1,0:T(8,128)(2,1)} %fusion.16) | copy-start | bytes 240004
  82.1 15.4 %all-to-all-start.1 = ((bf16[32,2,160]{2,1,0:T(2,128)(2,1)}), bf16[32,2,160]{2,1,0:T(2,128)(2,1)S(1)}, u32[]{:S(2)}, u32[]{:S(2)}) async-start(bf16[32,2,160]{2,1,0:T(2,128)(2,1)} %reshape.465), calls=%async_computation.1 | async-start | bytes 65536 | tf_op jit(solution)/shard_map/all_to_all | solution.py:332

commit v11 on v9

--- a/solution.py
+++ b/solution.py
@@ -86,12 +86,14 @@
     extended = jnp.concatenate(
         [jnp.ones((1, width), jnp.float32), velocity, jnp.zeros((1, width), jnp.float32)], axis=0
     )
-    rows = jnp.arange(5, dtype=jnp.int32)
 
     def pick(column):
         chosen = jnp.array(column, dtype=jnp.int32)
-        select = (chosen[:, None] == rows[None, :]).astype(jnp.float32)
-        return jnp.sum(select[:, :, None] * extended[None, :, :], axis=1)
+        total = None
+        for m in range(5):
+            term = (chosen == m).astype(jnp.float32)[:, None] * extended[m][None, :]
+            total = term if total is None else total + term
+        return total
 
     first, second, third = [pick([f[n] for f in factors]) for n in range(3)]
     element = first * second * third

time: 124 us -> 106 us (0.85)
  local copies, waits for them, and re-layouts: 25.1 us -> 12.6 us
  waiting for transfers between devices: 16.5 us -> 12.3 us
    reduce_sum x3 -> x0, local copies, waits for them, and re-layouts: 4.96 us -> none  [pick(): return jnp.sum(select[:, :, None] * extended[None, :, :], axis=1)]
    reduce_sum x1, other arithmetic: 4.06 us -> 0.45 us  [stencil_moments(): jnp.sum(stencil[2] * right[:, 0].astype(jnp.float32)[None, :], axis=1)]
    ppermute x4, waiting for transfers between devices: 10.5 us -> 6.96 us  [sect_sum(): total = total + lax.ppermute(total, 'sect', pairs)]
    convert_element_type x1, other arithmetic: 0.84 us -> 3.16 us  [recon_basis(): return (hermite(velocity) / norms[:, None]).T.astype(jnp.bfloat16)]
    reduce_sum x1 -> x0, other arithmetic: 2.19 us -> none  [pick(): return jnp.sum(select[:, :, None] * extended[None, :, :], axis=1)]
    mul x1 -> x3, local copies, waits for them, and re-layouts: 2.26 us -> 0.23 us  [pick(): term = (chosen == m).astype(jnp.float32)[:, None] * extended[m][None, :]]
    add x3, other arithmetic: 0.07 us -> 1.79 us  [sect_sum(): total = total + lax.ppermute(total, 'sect', pairs)]
    dot_general x1, local copies, waits for them, and re-layouts: 2.93 us -> 1.61 us  [fold_interface(): lax.dot_general(spread, pick_lo, (((0,), (0,)), ((), ())), preferred_elem...]
  transfers between devices with their start and end apart: 8 -> 8, of which waited for: 4 -> 4; matrix products, arithmetic and copies ran while one was open for 38% -> 33% of each run, Pallas kernels for 6% -> 7%
where the time goes in v11:
time: 106 us; the launch traced here: 105 us
  starting transfers between devices  29.8 us (28%)
  other arithmetic  23.8 us (22%)
  Pallas kernels  21 us (20%)
  local copies, waits for them, and re-layouts  12.6 us (12%)
  waiting for transfers between devices  12.3 us (12%)
  matrix products  4.85 us (5%)
    pallas_call x1, Pallas kernels, relax_call(): pl.pallas_call(relax_kernel, grid=(steps,), in_specs=[row_spec(cells), ro...  13.7 us
    all_to_all x1, starting transfers between devices, interface_rows(): gathered = lax.all_to_all(spread_out, 'space', 0, 0, tiled=True)  9.59 us
    all_to_all x1, starting transfers between devices, ghost_walls(): lax.all_to_all(outgoing, 'space', split_axis=1, concat_axis=1, tiled=True)  9.42 us
    pallas_call x1, Pallas kernels, moments_call(): pl.pallas_call(moments_kernel, grid=(steps,), in_specs=[row_spec(cells),...  7.3 us
    ppermute x4, waiting for transfers between devices, sect_sum(): total = total + lax.ppermute(total, 'sect', pairs)  6.96 us
    all_to_all x1, waiting for transfers between devices, ghost_walls(): lax.all_to_all(outgoing, 'space', split_axis=1, concat_axis=1, tiled=True)  5.31 us
    ppermute x4, starting transfers between devices, sect_sum(): total = total + lax.ppermute(total, 'sect', pairs)  5.28 us
    ppermute x1, starting transfers between devices, halo_columns(): before = lax.ppermute(shard[:, length - 1:], 'space', up)  3.42 us
  transfers between devices with their start and end apart: 8, of which 4 were waited for; matrix products, arithmetic and copies ran while one was open for 33% of the time, Pallas kernels for 7%

profile of v11, /device:TPU:1, one launch (start us, length us, event | category | flops | bytes accessed | tf_op | source)
XLA Modules:
  0.0 105.1 jit_solution(17745247772917294238)
XLA Ops:
  0.2 0.8 fusion.73
  1.1 0.8 convert_element_type.338
  1.9 0.7 broadcast_in_dim.15
  2.7 9.6 %all-to-all-start = ((bf16[32,128,22]{1,2,0:T(8,128)(2,1)}), bf16[32,128,22]{1,2,0:T(8,128)(2,1)S(1)}, u32[]{:S(2)}, u32[]{:S(2)}) async-start(bf16[32,128,22]{1,2,0:T(8,128)(2,1)} %broadcast_in_dim.15), calls=%async_computation | async-start | bytes 393216 | tf_op jit(solution)/shard_map/all_to_all | solution.py:287
  12.3 2.4 %fusion.79 = (bf16[2000,1]{1,0:T(8,128)(2,1)}, bf16[2000,1]{1,0:T(8,128)(2,1)}) fusion(bf16[2000,2048]{1,0:T(8,128)(2,1)} %dist_ref.3), kind=kLoop, calls=%fused_computation.184 | loop fusion | bytes 16000 | tf_op jit(solution)/shard_map/slice | solution.py:62
  14.6 2.1 %collective-permute-start.1 = (bf16[2000,1]{1,0:T(8,128)(2,1)}, bf16[2000,1]{1,0:T(8,128)(2,1)S(1)}, u32[]{:S(2)}, u32[]{:S(2)}) collective-permute-start(bf16[2000,1]{1,0:T(8,128)(2,1)} %get-tuple-element.27), channel_id=1, source_target_pairs={{1,0},{2,1},{3,2},{4,3},{5,4},{6,5},{7,6},{8,7},{9,8},{10,9},{11,1... | collective-permute-start | bytes 12008 | tf_op jit(solution)/shard_map/ppermute | solution.py:62
  16.8 3.4 %collective-permute-start = (bf16[2000,1]{1,0:T(8,128)(2,1)}, bf16[2000,1]{1,0:T(8,128)(2,1)}, u32[]{:S(2)}, u32[]{:S(2)}) collective-permute-start(bf16[2000,1]{1,0:T(8,128)(2,1)} %get-tuple-element.28), channel_id=1, source_target_pairs={{0,1},{1,2},{2,3},{3,4},{4,5},{5,6},{6,7},{7,8},{8,9},{9,10},{10,1... | collective-permute-start | bytes 12008 | tf_op jit(solution)/shard_map/ppermute | solution.py:61
  20.5 0.6 reduce-window.6
  21.6 0.6 add_reduce_fusion
  22.9 0.6 fusion.25
  23.5 0.6 convert_multiply_fusion
  24.1 0.6 convert_multiply_fusion.1
  24.9 1.1 %maximum_bitcast_fusion.basis_ref = bf16[5,180,400]{2,1,0:T(8,128)(2,1)} fusion(bf16[60,5,400]{2,0,1:T(8,128)(2,1)S(1)} %get-tuple-element.31, bf16[60,5,400]{2,0,1:T(8,128)(2,1)S(1)} %get-tuple-element.30, bf16[60,5,400]{2,0,1:T(8,128)(2,1)S(1)} %get-tuple-element.29), kind=kLoop, calls=%fused_computation.30 | loop fusion | flops 2160000 | bytes 1440000 | tf_op jit(solution)/shard_map/transpose | solution.py:190
  26.0 7.3 %shard_map.208 = f32[180,2048]{1,0:T(8,128)} custom-call(bf16[2000,2048]{1,0:T(8,128)(2,1)} %dist_ref.3, bf16[5,180,400]{2,1,0:T(8,128)(2,1)} %maximum_bitcast_fusion.basis_ref), custom_call_target="tpu_custom_call" | custom-call | flops 1474560000 | bytes 9666560 | tf_op jit(solution)/shard_map/pallas_call | solution.py:191
  33.3 1.5 %slice_add_fusion = f32[60,2048]{1,0:T(8,128)S(1)} fusion(f32[180,2048]{1,0:T(8,128)} %shard_map.208), kind=kLoop, calls=%fused_computation.34 | loop fusion | flops 245760 | bytes 1966080 | tf_op jit(solution)/shard_map/add | solution.py:217
  34.8 2.3 %fusion.3 = bf16[2048,512]{1,0:T(8,128)(2,1)} fusion(s32[512]{0:T(512)S(1)} %broadcast_add_fusion), kind=kLoop, calls=%fused_computation.5 | loop fusion | flops 2097152 | bytes 2099200 | tf_op jit(solution)/shard_map/convert_element_type | solution.py:326
  37.1 0.4 fusion.4
  37.5 0.8 fusion.80
  38.6 1.3 %convert_reduce_fusion.1 = f32[2000]{0:T(1024)S(1)} fusion(bf16[2000,1]{1,0:T(8,128)(2,1)} %collective-permute-done.left_ref), kind=kLoop, calls=%fused_computation.24 | loop fusion | flops 2000 | bytes 12000 | tf_op jit(solution)/shard_map/convert_element_type | solution.py:218
  39.8 0.5 fusion.31
  40.3 0.7 copy.59
  41.0 0.7 copy.60
  41.7 1.2 %fusion.41 = f32[20,2048]{1,0:T(8,128)S(1)} fusion(f32[60,2048]{1,0:T(8,128)S(1)} %slice_add_fusion, f32[20,2047]{1,0:T(8,128)} %get-tuple-element.33, f32[20,1]{1,0:T(8,128)} %copy.59, f32[20,1]{1,0:T(8,128)} %copy.60, f32[20,2047]{1,0:T(8,128)} %get-tuple-element.32), kind=kLoop, calls=%fused_computation.83 | loop fusion | flops 163840 | bytes 655360 | tf_op jit(solution)/shard_map/add | solution.py:222
  42.8 1.3 %collective-permute-start.2 = (f32[20,2048]{1,0:T(8,128)S(1)}, f32[20,2048]{1,0:T(8,128)S(1)}, u32[]{:S(2)}, u32[]{:S(2)}) collective-permute-start(f32[20,2048]{1,0:T(8,128)S(1)} %fusion.41), channel_id=1, source_target_pairs={{0,32},{32,0},{64,96},{96,64},{1,33},{33,1},{65,97},{97,65},{2,34}... | collective-permute-start | bytes 491528 | tf_op jit(solution)/shard_map/ppermute | solution.py:267
  44.1 3.2 %fusion.18 = bf16[2000,20]{1,0:T(8,128)(2,1)} fusion(f32[20]{0:T(128)} %constant.141, f32[20]{0:T(128)} %constant.139, f32[20]{0:T(128)S(1)} %copy-done.5, f32[20]{0:T(128)} %constant.177, f32[20]{0:T(128)} %constant.175, f32[20]{0:T(128)} %constant.171, f32[20]{0:T(128)} %constant.165, f32[20]{0:T(128)} %constant.163, f32[20]{0:T(128)} %constant.161, ...), kind=kLoop, calls=%fused_computation.25 | loop fusion | flops 1360000 | bytes 105440 | tf_op jit(solution)/shard_map/convert_element_type | solution.py:111
  47.3 2.3 %collective-permute-done.2 = f32[20,2048]{1,0:T(8,128)S(1)} collective-permute-done((f32[20,2048]{1,0:T(8,128)S(1)}, f32[20,2048]{1,0:T(8,128)S(1)}, u32[]{:S(2)}, u32[]{:S(2)}) %collective-permute-start.2) | collective-permute-done | bytes 163872 | tf_op jit(solution)/shard_map/ppermute | solution.py:267
  49.6 0.7 add.540
  50.3 2.7 %collective-permute-start.3 = (f32[20,2048]{1,0:T(8,128)}, f32[20,2048]{1,0:T(8,128)}, u32[]{:S(2)}, u32[]{:S(2)}) collective-permute-start(f32[20,2048]{1,0:T(8,128)} %add.540), channel_id=1, source_target_pairs={{0,64},{32,96},{64,0},{96,32},{1,65},{33,97},{65,1},{97,33},{2,66}... | collective-permute-start | bytes 491528 | tf_op jit(solution)/shard_map/ppermute | solution.py:267
  53.4 0.7 slice_select_fusion
  54.2 1.3 %broadcast_multiply_fusion = bf16[4096,8,21]{0,2,1:T(8,128)(2,1)} fusion(bf16[4096,21]{0,1:T(8,128)(2,1)S(1)} %slice_select_fusion, bf16[4096,8]{0,1:T(8,128)(2,1)S(1)} %fusion.43), kind=kLoop, calls=%fused_computation.31 | loop fusion | flops 688128 | bytes 1613824 | tf_op jit(solution)/shard_map/mul | solution.py:301
  55.5 1.9 %mul.1281 = bf16[4096,168]{0,1:T(8,128)(2,1)S(1)} reshape(bf16[4096,8,21]{0,2,1:T(8,128)(2,1)} %broadcast_multiply_fusion) | data formatting | bytes 2752512 | tf_op jit(solution)/shard_map/mul | solution.py:301
  57.4 1.6 %dot_general.14 = bf16[8,21,4096]{2,1,0:T(8,128)(2,1)} reshape(bf16[168,4096]{1,0:T(8,128)(2,1)S(1)} %bitcast.69) | data formatting | bytes 2752512 | tf_op jit(solution)/shard_map/dot_general | solution.py:303
  59.0 2.5 %fusion.10 = bf16[21,8,256]{2,0,1:T(8,128)(2,1)S(1)} fusion(bf16[8,21,4096]{2,1,0:T(8,128)(2,1)} %dot_general.14, s32[4096]{0:T(1024)S(1)} %bitcast.90), kind=kOutput, calls=%fused_computation.16 | convolution fusion | flops 353413120 | bytes 1478656 | tf_op jit(solution)/shard_map/dot_general | solution.py:303
  61.5 0.4 collective-permute-start.4
  62.0 1.2 %pad_maximum_fusion.1.recon3_ref = bf16[2000,60]{1,0:T(8,128)(2,1)} fusion(bf16[2000,20]{1,0:T(8,128)(2,1)S(1)} %copy-done.1), kind=kLoop, calls=%fused_computation.38 | loop fusion | flops 720000 | bytes 320000 | tf_op jit(solution)/shard_map/concatenate | solution.py:359
  63.2 1.9 %collective-permute-done.4 = bf16[21,2048]{1,0:T(8,128)(2,1)S(1)} collective-permute-done((bf16[21,2048]{1,0:T(8,128)(2,1)S(1)}, bf16[21,2048]{1,0:T(8,128)(2,1)S(1)}, u32[]{:S(2)}, u32[]{:S(2)}) %collective-permute-start.4) | collective-permute-done | bytes 86048 | tf_op jit(solution)/shard_map/ppermute | solution.py:267
  65.1 0.8 collective-permute-start.5
  66.0 1.0 add.541
  67.7 2.7 %collective-permute-done.5 = bf16[21,2048]{1,0:T(8,128)(2,1)S(1)} collective-permute-done((bf16[21,2048]{1,0:T(8,128)(2,1)S(1)}, bf16[21,2048]{1,0:T(8,128)(2,1)S(1)}, u32[]{:S(2)}, u32[]{:S(2)}) %collective-permute-start.5) | collective-permute-done | bytes 86048 | tf_op jit(solution)/shard_map/ppermute | solution.py:267
  70.4 2.0 %convolution_convert_fusion = bf16[20,512]{1,0:T(8,128)(2,1)S(1)} fusion(bf16[20,2048]{1,0:T(8,128)(2,1)S(1)} %fusion.40, bf16[2048,512]{1,0:T(8,128)(2,1)} %fusion.3), kind=kOutput, calls=%fused_computation.17 | convolution fusion | flops 41953280 | bytes 2199552 | tf_op jit(solution)/shard_map/dot_general | solution.py:333
  72.6 0.8 reshape.804
  73.4 9.4 %all-to-all-start.1 = ((bf16[32,2,160]{2,1,0:T(2,128)(2,1)}), bf16[32,2,160]{2,1,0:T(2,128)(2,1)S(1)}, u32[]{:S(2)}, u32[]{:S(2)}) async-start(bf16[32,2,160]{2,1,0:T(2,128)(2,1)} %reshape.804), calls=%async_computation.1 | async-start | bytes 65536 | tf_op jit(solution)/shard_map/all_to_all | solution.py:334
  82.8 0.6 broadcast_subtract_fusion
  83.4 1.3 %copy.67.courant_ref = f32[2000,1]{1,0:T(8,128)} copy(f32[2000,1]{0,1:T(1,128)S(1)} %copy-done.3) | data formatting | bytes 16000 | tf_op jit(solution)/shard_map/mul | solution.py:350
  84.7 5.3 %all-to-all-done.1 = bf16[32,2,160]{2,1,0:T(2,128)(2,1)S(1)} async-done(((bf16[32,2,160]{2,1,0:T(2,128)(2,1)}), bf16[32,2,160]{2,1,0:T(2,128)(2,1)S(1)}, u32[]{:S(2)}, u32[]{:S(2)}) %all-to-all-start.1) | async-done | bytes 20512 | tf_op jit(solution)/shard_map/all_to_all | solution.py:334
  90.2 0.4 reduce-precision_convert_fusion.3
  90.6 0.7 pad_maximum_fusion.2.gain_ref
  91.4 13.7 %shard_map.209 = bf16[2000,2048]{1,0:T(8,128)(2,1)} custom-call(bf16[2000,2048]{1,0:T(8,128)(2,1)} %dist_ref.3, bf16[2000,1]{1,0:T(8,128)(2,1)} %collective-permute-done.left_ref, bf16[2000,1]{1,0:T(8,128)(2,1)} %copy-done, f32[2000,1]{1,0:T(8,128)} %copy.67.courant_ref, bf16[2000,60]{1,0:T(8,128)(2,1)} %pad_maximum_fusion.1.recon3_ref, ...), custom_call_target="tpu_custom_call" | custom-call | flops 532480000 | bytes 16384000 | tf_op jit(solution)/shard_map/pallas_call | solution.py:228
  (101 shorter events, 3.2 us)
Async XLA Ops:
  0.0 22.7 %copy-start.5 = (f32[20]{0:T(128)S(1)}, f32[20]{0:T(128)}, u32[]{:S(2)}) copy-start(f32[20]{0:T(128)} %constant.179) | copy-start | bytes 244
  0.0 22.7 %copy-start.6 = (f32[20]{0:T(128)S(1)}, f32[20]{0:T(128)}, u32[]{:S(2)}) copy-start(f32[20]{0:T(128)} %constant.177) | copy-start | bytes 244
  0.0 22.7 %copy-start.7 = (f32[20]{0:T(128)S(1)}, f32[20]{0:T(128)}, u32[]{:S(2)}) copy-start(f32[20]{0:T(128)} %constant.175) | copy-start | bytes 244
  0.0 22.7 %copy-start.8 = (f32[20]{0:T(128)S(1)}, f32[20]{0:T(128)}, u32[]{:S(2)}) copy-start(f32[20]{0:T(128)} %constant.171) | copy-start | bytes 244
  0.0 22.7 %copy-start.9 = (f32[20]{0:T(128)S(1)}, f32[20]{0:T(128)}, u32[]{:S(2)}) copy-start(f32[20]{0:T(128)} %constant.165) | copy-start | bytes 244
  0.0 22.7 %copy-start.10 = (f32[20]{0:T(128)S(1)}, f32[20]{0:T(128)}, u32[]{:S(2)}) copy-start(f32[20]{0:T(128)} %constant.163) | copy-start | bytes 244
  0.0 22.7 %copy-start.11 = (f32[20]{0:T(128)S(1)}, f32[20]{0:T(128)}, u32[]{:S(2)}) copy-start(f32[20]{0:T(128)} %constant.161) | copy-start | bytes 244
  0.1 22.7 %copy-start.12 = (f32[20]{0:T(128)S(1)}, f32[20]{0:T(128)}, u32[]{:S(2)}) copy-start(f32[20]{0:T(128)} %constant.159) | copy-start | bytes 244
  0.1 22.7 %copy-start.13 = (f32[20]{0:T(128)S(1)}, f32[20]{0:T(128)}, u32[]{:S(2)}) copy-start(f32[20]{0:T(128)} %constant.157) | copy-start | bytes 244
  0.1 22.7 %copy-start.14 = (f32[20]{0:T(128)S(1)}, f32[20]{0:T(128)}, u32[]{:S(2)}) copy-start(f32[20]{0:T(128)} %constant.155) | copy-start | bytes 244
  0.1 22.7 %copy-start.15 = (f32[20]{0:T(128)S(1)}, f32[20]{0:T(128)}, u32[]{:S(2)}) copy-start(f32[20]{0:T(128)} %constant.153) | copy-start | bytes 244
  0.1 22.7 %copy-start.16 = (f32[20]{0:T(128)S(1)}, f32[20]{0:T(128)}, u32[]{:S(2)}) copy-start(f32[20]{0:T(128)} %constant.151) | copy-start | bytes 244
  0.1 22.7 %copy-start.17 = (f32[20]{0:T(128)S(1)}, f32[20]{0:T(128)}, u32[]{:S(2)}) copy-start(f32[20]{0:T(128)} %constant.149) | copy-start | bytes 244
  0.1 22.7 %copy-start.18 = (f32[20]{0:T(128)S(1)}, f32[20]{0:T(128)}, u32[]{:S(2)}) copy-start(f32[20]{0:T(128)} %constant.147) | copy-start | bytes 244
  0.1 22.7 %copy-start.19 = (f32[20]{0:T(128)S(1)}, f32[20]{0:T(128)}, u32[]{:S(2)}) copy-start(f32[20]{0:T(128)} %constant.145) | copy-start | bytes 244
  0.2 22.7 %copy-start.20 = (f32[20]{0:T(128)S(1)}, f32[20]{0:T(128)}, u32[]{:S(2)}) copy-start(f32[20]{0:T(128)} %constant.143) | copy-start | bytes 244
  0.2 22.7 %copy-start.21 = (f32[20]{0:T(128)S(1)}, f32[20]{0:T(128)}, u32[]{:S(2)}) copy-start(f32[20]{0:T(128)} %constant.141) | copy-start | bytes 244
  0.2 20.0 %copy-start.25 = (s32[256]{0:T(256)S(1)}, s32[256]{0:T(256)}, u32[]{:S(2)}) copy-start(s32[256]{0:T(256)} %param.26) | copy-start | bytes 3076
  0.2 20.0 %copy-start.24 = (f32[2000]{0:T(1024)S(1)}, f32[2000]{0:T(1024)}, u32[]{:S(2)}) copy-start(f32[2000]{0:T(1024)} %param.24) | copy-start | bytes 24004
  0.2 20.1 %copy-start.23 = (s32[1,32,16]{1,2,0:T(8,128)S(1)}, s32[1,32,16]{1,2,0:T(8,128)}, u32[]{:S(2)}) copy-start(s32[1,32,16]{1,2,0:T(8,128)} %param.28) | copy-start | bytes 6148
  0.2 20.3 %copy-start.22 = (s32[256,1]{0,1:T(1,128)S(1)}, s32[256,1]{0,1:T(1,128)}, u32[]{:S(2)}) copy-start(s32[256,1]{0,1:T(1,128)} %param.27) | copy-start | bytes 3076
  0.2 21.4 %copy-start.4 = (f32[3,2000]{1,0:T(4,128)S(1)}, f32[3,2000]{1,0:T(4,128)}, u32[]{:S(2)}) copy-start(f32[3,2000]{1,0:T(4,128)} %param.23) | copy-start | bytes 72004
  2.7 50.4 %all-to-all-start = ((bf16[32,128,22]{1,2,0:T(8,128)(2,1)}), bf16[32,128,22]{1,2,0:T(8,128)(2,1)S(1)}, u32[]{:S(2)}, u32[]{:S(2)}) async-start(bf16[32,128,22]{1,2,0:T(8,128)(2,1)} %broadcast_in_dim.15), calls=%async_computation | async-start | bytes 393216 | tf_op jit(solution)/shard_map/all_to_all | solution.py:287
  14.6 23.7 %collective-permute-start.1 = (bf16[2000,1]{1,0:T(8,128)(2,1)}, bf16[2000,1]{1,0:T(8,128)(2,1)S(1)}, u32[]{:S(2)}, u32[]{:S(2)}) collective-permute-start(bf16[2000,1]{1,0:T(8,128)(2,1)} %get-tuple-element.27), channel_id=1, source_target_pairs={{1,0},{2,1},{3,2},{4,3},{5,4},{6,5},{7,6},{8,7},{9,8},{10,9},{11,1... | collective-permute-start | bytes 12008 | tf_op jit(solution)/shard_map/ppermute | solution.py:62
  16.8 21.8 %collective-permute-start = (bf16[2000,1]{1,0:T(8,128)(2,1)}, bf16[2000,1]{1,0:T(8,128)(2,1)}, u32[]{:S(2)}, u32[]{:S(2)}) collective-permute-start(bf16[2000,1]{1,0:T(8,128)(2,1)} %get-tuple-element.28), channel_id=1, source_target_pairs={{0,1},{1,2},{2,3},{3,4},{4,5},{5,6},{6,7},{7,8},{8,9},{9,10},{10,1... | collective-permute-start | bytes 12008 | tf_op jit(solution)/shard_map/ppermute | solution.py:61
  38.3 14.9 %copy-start = (bf16[2000,1]{1,0:T(8,128)(2,1)}, bf16[2000,1]{1,0:T(8,128)(2,1)S(1)}, u32[]{:S(2)}) copy-start(bf16[2000,1]{1,0:T(8,128)(2,1)S(1)} %collective-permute-done.1.right_ref) | copy-start | bytes 12004
  42.8 6.8 %collective-permute-start.2 = (f32[20,2048]{1,0:T(8,128)S(1)}, f32[20,2048]{1,0:T(8,128)S(1)}, u32[]{:S(2)}, u32[]{:S(2)}) collective-permute-start(f32[20,2048]{1,0:T(8,128)S(1)} %fusion.41), channel_id=1, source_target_pairs={{0,32},{32,0},{64,96},{96,64},{1,33},{33,1},{65,97},{97,65},{2,34}... | collective-permute-start | bytes 491528 | tf_op jit(solution)/shard_map/ppermute | solution.py:267
  50.3 15.6 %collective-permute-start.3 = (f32[20,2048]{1,0:T(8,128)}, f32[20,2048]{1,0:T(8,128)}, u32[]{:S(2)}, u32[]{:S(2)}) collective-permute-start(f32[20,2048]{1,0:T(8,128)} %add.540), channel_id=1, source_target_pairs={{0,64},{32,96},{64,0},{96,32},{1,65},{33,97},{65,1},{97,33},{2,66}... | collective-permute-start | bytes 491528 | tf_op jit(solution)/shard_map/ppermute | solution.py:267
  59.0 2.9 %copy-start.1 = (bf16[2000,20]{1,0:T(8,128)(2,1)S(1)}, bf16[2000,20]{1,0:T(8,128)(2,1)}, u32[]{:S(2)}) copy-start(bf16[2000,20]{1,0:T(8,128)(2,1)} %fusion.18) | copy-start | bytes 240004
  61.5 3.5 %collective-permute-start.4 = (bf16[21,2048]{1,0:T(8,128)(2,1)S(1)}, bf16[21,2048]{1,0:T(8,128)(2,1)S(1)}, u32[]{:S(2)}, u32[]{:S(2)}) collective-permute-start(bf16[21,2048]{1,0:T(8,128)(2,1)S(1)} %bitcast.77), channel_id=1, source_target_pairs={{0,32},{32,0},{64,96},{96,64},{1,33},{33,1},{65,97},{97,65},{2,34}... | collective-permute-start | bytes 258056 | tf_op jit(solution)/shard_map/ppermute | solution.py:267
  65.1 5.2 %collective-permute-start.5 = (bf16[21,2048]{1,0:T(8,128)(2,1)S(1)}, bf16[21,2048]{1,0:T(8,128)(2,1)S(1)}, u32[]{:S(2)}, u32[]{:S(2)}) collective-permute-start(bf16[21,2048]{1,0:T(8,128)(2,1)S(1)} %add.581), channel_id=1, source_target_pairs={{0,64},{32,96},{64,0},{96,32},{1,65},{33,97},{65,1},{97,33},{2,66}... | collective-permute-start | bytes 258056 | tf_op jit(solution)/shard_map/ppermute | solution.py:267
  67.2 15.6 %copy-start.2 = (f32[2048]{0:T(1024)S(1)}, f32[2048]{0:T(1024)}, u32[]{:S(2)}) copy-start(f32[2048]{0:T(1024)} %param.25) | copy-start | bytes 24580
  67.2 16.2 %copy-start.3 = (f32[2000,1]{0,1:T(1,128)S(1)}, f32[2000,1]{0,1:T(1,128)}, u32[]{:S(2)}) copy-start(f32[2000,1]{0,1:T(1,128)} %get-tuple-element.53) | copy-start | bytes 24004
  73.4 16.7 %all-to-all-start.1 = ((bf16[32,2,160]{2,1,0:T(2,128)(2,1)}), bf16[32,2,160]{2,1,0:T(2,128)(2,1)S(1)}, u32[]{:S(2)}, u32[]{:S(2)}) async-start(bf16[32,2,160]{2,1,0:T(2,128)(2,1)} %reshape.804), calls=%async_computation.1 | async-start | bytes 65536 | tf_op jit(solution)/shard_map/all_to_all | solution.py:334

commit v12 on v11

--- a/solution.py
+++ b/solution.py
@@ -58,9 +58,9 @@
     length = shard.shape[1]
     up = [(i, i + 1) for i in range(count - 1)]
     down = [(j, i) for i, j in up]
-    before = lax.ppermute(shard[:, length - 1 :], "space", up)
-    after = lax.ppermute(shard[:, :1], "space", down)
-    return before, after
+    before = lax.ppermute(shard[:, length - 1], "space", up)
+    after = lax.ppermute(shard[:, 0], "space", down)
+    return before[:, None], after[:, None]
 
 
 def hermite_tables():

time: 106 us -> 107 us (level)
  waiting for transfers between devices: 12.3 us -> 9.74 us
  starting transfers between devices: 29.8 us -> 32.3 us
    all_to_all x1, waiting for transfers between devices: 5.31 us -> 3.05 us  [ghost_walls(): lax.all_to_all(outgoing, 'space', split_axis=1, concat_axis=1, tiled=True)]
    broadcast_in_dim x0 -> x2, local copies, waits for them, and re-layouts: none -> 2.26 us  [halo_columns(): return (before[:, None], after[:, None])]
    convert_element_type x1, other arithmetic: 1.25 us -> 0.01 us  [stencil_moments(): left[:, 0].astype(jnp.float32)[None, :]]
    all_to_all x1, starting transfers between devices: 9.42 us -> 10.7 us  [ghost_walls(): lax.all_to_all(outgoing, 'space', split_axis=1, concat_axis=1, tiled=True)]
  transfers between devices with their start and end apart: 8 -> 8, of which waited for: 4 -> 4; matrix products, arithmetic and copies ran while one was open for 33% -> 34% of each run, Pallas kernels for 7% -> 7%
where the time goes in v12:
time: 107 us; the launch traced here: 106 us
  starting transfers between devices  32.3 us (30%)
  other arithmetic  24.8 us (23%)
  Pallas kernels  21 us (20%)
  local copies, waits for them, and re-layouts  13.1 us (12%)
  waiting for transfers between devices  9.74 us (9%)
  matrix products  4.85 us (5%)
    pallas_call x1, Pallas kernels, relax_call(): pl.pallas_call(relax_kernel, grid=(steps,), in_specs=[row_spec(cells), ro...  13.7 us
    all_to_all x1, starting transfers between devices, ghost_walls(): lax.all_to_all(outgoing, 'space', split_axis=1, concat_axis=1, tiled=True)  10.7 us
    all_to_all x1, starting transfers between devices, interface_rows(): gathered = lax.all_to_all(spread_out, 'space', 0, 0, tiled=True)  9.86 us
    pallas_call x1, Pallas kernels, moments_call(): pl.pallas_call(moments_kernel, grid=(steps,), in_specs=[row_spec(cells),...  7.3 us
    ppermute x4, waiting for transfers between devices, sect_sum(): total = total + lax.ppermute(total, 'sect', pairs)  6.68 us
    ppermute x4, starting transfers between devices, sect_sum(): total = total + lax.ppermute(total, 'sect', pairs)  5.25 us
    ppermute x1, starting transfers between devices, halo_columns(): after = lax.ppermute(shard[:, 0], 'space', down)  3.29 us
    ppermute x1, starting transfers between devices, halo_columns(): before = lax.ppermute(shard[:, length - 1], 'space', up)  3.21 us
  transfers between devices with their start and end apart: 8, of which 4 were waited for; matrix products, arithmetic and copies ran while one was open for 34% of the time, Pallas kernels for 7%

profile of v12, /device:TPU:1, one launch (start us, length us, event | category | flops | bytes accessed | tf_op | source)
XLA Modules:
  0.0 106.4 jit_solution(1034199886862584276)
XLA Ops:
  0.2 1.8 %slice_reduce_fusion = (bf16[2000]{0:T(1024)(128)(2,1)S(1)}, bf16[2000]{0:T(1024)(128)(2,1)S(1)}) fusion(bf16[2000,2048]{1,0:T(8,128)(2,1)} %dist_ref.3), kind=kLoop, calls=%fused_computation.37 | loop fusion | bytes 16000 | tf_op jit(solution)/shard_map/slice | solution.py:62
  2.0 3.3 %collective-permute-start.1 = (bf16[2000]{0:T(1024)(128)(2,1)S(1)}, bf16[2000]{0:T(1024)(128)(2,1)S(1)}, u32[]{:S(2)}, u32[]{:S(2)}) collective-permute-start(bf16[2000]{0:T(1024)(128)(2,1)S(1)} %get-tuple-element.9), channel_id=1, source_target_pairs={{1,0},{2,1},{3,2},{4,3},{5,4},{6,5},{7,6},{8,7},{9,8},{10,9},{11,1... | collective-permute-start | bytes 12008 | tf_op jit(solution)/shard_map/ppermute | solution.py:62
  5.3 3.2 %collective-permute-start = (bf16[2000]{0:T(1024)(128)(2,1)S(1)}, bf16[2000]{0:T(1024)(128)(2,1)S(1)}, u32[]{:S(2)}, u32[]{:S(2)}) collective-permute-start(bf16[2000]{0:T(1024)(128)(2,1)S(1)} %get-tuple-element.10), channel_id=1, source_target_pairs={{0,1},{1,2},{2,3},{3,4},{4,5},{5,6},{6,7},{7,8},{8,9},{9,10},{10,1... | collective-permute-start | bytes 12008 | tf_op jit(solution)/shard_map/ppermute | solution.py:61
  8.5 0.7 fusion.73
  9.2 0.8 convert_element_type.322
  10.1 0.7 broadcast_in_dim.21
  10.8 9.9 %all-to-all-start = ((bf16[32,128,22]{1,2,0:T(8,128)(2,1)}), bf16[32,128,22]{1,2,0:T(8,128)(2,1)S(1)}, u32[]{:S(2)}, u32[]{:S(2)}) async-start(bf16[32,128,22]{1,2,0:T(8,128)(2,1)} %broadcast_in_dim.21), calls=%async_computation | async-start | bytes 393216 | tf_op jit(solution)/shard_map/all_to_all | solution.py:287
  20.7 0.7 broadcast_add_fusion.1
  21.4 0.7 broadcast_multiply_fusion.1
  22.2 0.8 copy.72
  23.0 0.7 fusion.47
  23.7 0.6 reduce-window.6
  24.5 0.8 fusion.46
  25.3 0.7 multiply_add_fusion.21
  26.1 1.0 add_reduce_fusion
  27.8 0.6 fusion.25
  28.4 0.6 convert_multiply_fusion
  29.0 0.6 convert_multiply_fusion.1
  29.9 1.1 %maximum_bitcast_fusion.basis_ref = bf16[5,180,400]{2,1,0:T(8,128)(2,1)} fusion(bf16[60,5,400]{2,0,1:T(8,128)(2,1)S(1)} %get-tuple-element.31, bf16[60,5,400]{2,0,1:T(8,128)(2,1)S(1)} %get-tuple-element.30, bf16[60,5,400]{2,0,1:T(8,128)(2,1)S(1)} %get-tuple-element.29), kind=kLoop, calls=%fused_computation.28 | loop fusion | flops 2160000 | bytes 1440000 | tf_op jit(solution)/shard_map/transpose | solution.py:190
  31.0 7.3 %shard_map.208 = f32[180,2048]{1,0:T(8,128)} custom-call(bf16[2000,2048]{1,0:T(8,128)(2,1)} %dist_ref.3, bf16[5,180,400]{2,1,0:T(8,128)(2,1)} %maximum_bitcast_fusion.basis_ref), custom_call_target="tpu_custom_call" | custom-call | flops 1474560000 | bytes 9666560 | tf_op jit(solution)/shard_map/pallas_call | solution.py:191
  38.3 1.5 %slice_add_fusion = f32[60,2048]{1,0:T(8,128)S(1)} fusion(f32[180,2048]{1,0:T(8,128)} %shard_map.208), kind=kLoop, calls=%fused_computation.32 | loop fusion | flops 245760 | bytes 1966080 | tf_op jit(solution)/shard_map/add | solution.py:217
  39.7 2.3 %fusion.3 = bf16[2048,512]{1,0:T(8,128)(2,1)} fusion(s32[512]{0:T(512)S(1)} %broadcast_add_fusion), kind=kLoop, calls=%fused_computation.5 | loop fusion | flops 2097152 | bytes 2099200 | tf_op jit(solution)/shard_map/convert_element_type | solution.py:326
  42.6 0.4 fusion.31
  43.4 1.3 %collective-permute-start.2 = (f32[20,2048]{1,0:T(8,128)S(1)}, f32[20,2048]{1,0:T(8,128)S(1)}, u32[]{:S(2)}, u32[]{:S(2)}) collective-permute-start(f32[20,2048]{1,0:T(8,128)S(1)} %fusion.41), channel_id=1, source_target_pairs={{0,32},{32,0},{64,96},{96,64},{1,33},{33,1},{65,97},{97,65},{2,34}... | collective-permute-start | bytes 491528 | tf_op jit(solution)/shard_map/ppermute | solution.py:267
  44.7 3.0 %fusion.18 = bf16[2000,20]{1,0:T(8,128)(2,1)} fusion(f32[20]{0:T(128)S(1)} %copy-done.19, f32[20]{0:T(128)} %constant.139, f32[20]{0:T(128)S(1)} %copy-done.2, f32[20]{0:T(128)S(1)} %copy-done.3, f32[20]{0:T(128)S(1)} %copy-done.4, f32[20]{0:T(128)S(1)} %copy-done.5, f32[20]{0:T(128)S(1)} %copy-done.6, f32[20]{0:T(128)S(1)} %copy-done.7, ...), kind=kLoop, calls=%fused_computation.23 | loop fusion | flops 1360000 | bytes 105440 | tf_op jit(solution)/shard_map/convert_element_type | solution.py:111
  47.7 2.0 %collective-permute-done.2 = f32[20,2048]{1,0:T(8,128)S(1)} collective-permute-done((f32[20,2048]{1,0:T(8,128)S(1)}, f32[20,2048]{1,0:T(8,128)S(1)}, u32[]{:S(2)}, u32[]{:S(2)}) %collective-permute-start.2) | collective-permute-done | bytes 163872 | tf_op jit(solution)/shard_map/ppermute | solution.py:267
  49.7 0.7 add.540
  50.4 2.7 %collective-permute-start.3 = (f32[20,2048]{1,0:T(8,128)}, f32[20,2048]{1,0:T(8,128)}, u32[]{:S(2)}, u32[]{:S(2)}) collective-permute-start(f32[20,2048]{1,0:T(8,128)} %add.540), channel_id=1, source_target_pairs={{0,64},{32,96},{64,0},{96,32},{1,65},{33,97},{65,1},{97,33},{2,66}... | collective-permute-start | bytes 491528 | tf_op jit(solution)/shard_map/ppermute | solution.py:267
  53.4 0.7 slice_select_fusion
  54.3 1.3 %broadcast_multiply_fusion = bf16[4096,8,21]{0,2,1:T(8,128)(2,1)} fusion(bf16[4096,21]{0,1:T(8,128)(2,1)S(1)} %slice_select_fusion, bf16[4096,8]{0,1:T(8,128)(2,1)S(1)} %fusion.43), kind=kLoop, calls=%fused_computation.29 | loop fusion | flops 688128 | bytes 1613824 | tf_op jit(solution)/shard_map/mul | solution.py:301
  55.6 1.9 %mul.1281 = bf16[4096,168]{0,1:T(8,128)(2,1)S(1)} reshape(bf16[4096,8,21]{0,2,1:T(8,128)(2,1)} %broadcast_multiply_fusion) | data formatting | bytes 2752512 | tf_op jit(solution)/shard_map/mul | solution.py:301
  57.4 1.6 %dot_general.14 = bf16[8,21,4096]{2,1,0:T(8,128)(2,1)} reshape(bf16[168,4096]{1,0:T(8,128)(2,1)S(1)} %bitcast.69) | data formatting | bytes 2752512 | tf_op jit(solution)/shard_map/dot_general | solution.py:303
  59.0 2.5 %fusion.10 = bf16[21,8,256]{2,0,1:T(8,128)(2,1)S(1)} fusion(bf16[8,21,4096]{2,1,0:T(8,128)(2,1)} %dot_general.14, s32[4096]{0:T(1024)S(1)} %bitcast.90), kind=kOutput, calls=%fused_computation.16 | convolution fusion | flops 353413120 | bytes 1478656 | tf_op jit(solution)/shard_map/dot_general | solution.py:303
  61.9 1.2 %pad_maximum_fusion.1.recon3_ref = bf16[2000,60]{1,0:T(8,128)(2,1)} fusion(bf16[2000,20]{1,0:T(8,128)(2,1)S(1)} %copy-done), kind=kLoop, calls=%fused_computation.36 | loop fusion | flops 720000 | bytes 320000 | tf_op jit(solution)/shard_map/concatenate | solution.py:359
  63.2 1.9 %collective-permute-done.4 = bf16[21,2048]{1,0:T(8,128)(2,1)S(1)} collective-permute-done((bf16[21,2048]{1,0:T(8,128)(2,1)S(1)}, bf16[21,2048]{1,0:T(8,128)(2,1)S(1)}, u32[]{:S(2)}, u32[]{:S(2)}) %collective-permute-start.4) | collective-permute-done | bytes 86048 | tf_op jit(solution)/shard_map/ppermute | solution.py:267
  65.1 0.8 collective-permute-start.5
  66.0 1.0 add.541
  67.7 2.7 %collective-permute-done.5 = bf16[21,2048]{1,0:T(8,128)(2,1)S(1)} collective-permute-done((bf16[21,2048]{1,0:T(8,128)(2,1)S(1)}, bf16[21,2048]{1,0:T(8,128)(2,1)S(1)}, u32[]{:S(2)}, u32[]{:S(2)}) %collective-permute-start.5) | collective-permute-done | bytes 86048 | tf_op jit(solution)/shard_map/ppermute | solution.py:267
  70.4 2.0 %convolution_convert_fusion = bf16[20,512]{1,0:T(8,128)(2,1)S(1)} fusion(bf16[20,2048]{1,0:T(8,128)(2,1)S(1)} %fusion.40, bf16[2048,512]{1,0:T(8,128)(2,1)} %fusion.3), kind=kOutput, calls=%fused_computation.17 | convolution fusion | flops 41953280 | bytes 2199552 | tf_op jit(solution)/shard_map/dot_general | solution.py:333
  72.6 0.8 reshape.790
  73.4 10.7 %all-to-all-start.1 = ((bf16[32,2,160]{2,1,0:T(2,128)(2,1)}), bf16[32,2,160]{2,1,0:T(2,128)(2,1)S(1)}, u32[]{:S(2)}, u32[]{:S(2)}) async-start(bf16[32,2,160]{2,1,0:T(2,128)(2,1)} %reshape.790), calls=%async_computation.1 | async-start | bytes 65536 | tf_op jit(solution)/shard_map/all_to_all | solution.py:334
  84.1 0.6 broadcast_subtract_fusion
  84.7 1.3 %copy.77.courant_ref = f32[2000,1]{1,0:T(8,128)} copy(f32[2000,1]{0,1:T(1,128)S(1)} %get-tuple-element.53) | data formatting | bytes 16000 | tf_op jit(solution)/shard_map/mul | solution.py:350
  86.0 1.1 %broadcast_in_dim.22.left_ref = bf16[2000,1]{1,0:T(8,128)(2,1)} reshape(bf16[2000]{0:T(1024)(128)(2,1)S(1)} %collective-permute-done) | data formatting | bytes 8000 | tf_op jit(solution)/shard_map/broadcast_in_dim | solution.py:63
  87.1 1.1 %broadcast_in_dim.23.right_ref = bf16[2000,1]{1,0:T(8,128)(2,1)} reshape(bf16[2000]{0:T(1024)(128)(2,1)S(1)} %collective-permute-done.1) | data formatting | bytes 8000 | tf_op jit(solution)/shard_map/broadcast_in_dim | solution.py:63
  88.3 3.0 %all-to-all-done.1 = bf16[32,2,160]{2,1,0:T(2,128)(2,1)S(1)} async-done(((bf16[32,2,160]{2,1,0:T(2,128)(2,1)}), bf16[32,2,160]{2,1,0:T(2,128)(2,1)S(1)}, u32[]{:S(2)}, u32[]{:S(2)}) %all-to-all-start.1) | async-done | bytes 20512 | tf_op jit(solution)/shard_map/all_to_all | solution.py:334
  91.9 0.8 pad_maximum_fusion.2.gain_ref
  92.6 13.7 %shard_map.209 = bf16[2000,2048]{1,0:T(8,128)(2,1)} custom-call(bf16[2000,2048]{1,0:T(8,128)(2,1)} %dist_ref.3, bf16[2000,1]{1,0:T(8,128)(2,1)} %broadcast_in_dim.22.left_ref, bf16[2000,1]{1,0:T(8,128)(2,1)} %broadcast_in_dim.23.right_ref, f32[2000,1]{1,0:T(8,128)} %copy.77.courant_ref, bf16[2000,60]{1,0:T(8,128)(2,1)} %pad_maximum_fusion.1.recon3_ref, ...), custom_call_target="tpu_custom_call" | custom-call | flops 532480000 | bytes 16384000 | tf_op jit(solution)/shard_map/pallas_call | solution.py:228
  (91 shorter events, 4.4 us)
Async XLA Ops:
  0.0 27.6 %copy-start.2 = (f32[20]{0:T(128)S(1)}, f32[20]{0:T(128)}, u32[]{:S(2)}) copy-start(f32[20]{0:T(128)} %constant.179) | copy-start | bytes 244
  0.0 27.6 %copy-start.3 = (f32[20]{0:T(128)S(1)}, f32[20]{0:T(128)}, u32[]{:S(2)}) copy-start(f32[20]{0:T(128)} %constant.177) | copy-start | bytes 244
  0.0 27.6 %copy-start.4 = (f32[20]{0:T(128)S(1)}, f32[20]{0:T(128)}, u32[]{:S(2)}) copy-start(f32[20]{0:T(128)} %constant.175) | copy-start | bytes 244
  0.0 27.6 %copy-start.5 = (f32[20]{0:T(128)S(1)}, f32[20]{0:T(128)}, u32[]{:S(2)}) copy-start(f32[20]{0:T(128)} %constant.171) | copy-start | bytes 244
  0.0 27.6 %copy-start.6 = (f32[20]{0:T(128)S(1)}, f32[20]{0:T(128)}, u32[]{:S(2)}) copy-start(f32[20]{0:T(128)} %constant.165) | copy-start | bytes 244
  0.0 27.6 %copy-start.7 = (f32[20]{0:T(128)S(1)}, f32[20]{0:T(128)}, u32[]{:S(2)}) copy-start(f32[20]{0:T(128)} %constant.163) | copy-start | bytes 244
  0.0 27.6 %copy-start.8 = (f32[20]{0:T(128)S(1)}, f32[20]{0:T(128)}, u32[]{:S(2)}) copy-start(f32[20]{0:T(128)} %constant.161) | copy-start | bytes 244
  0.1 27.6 %copy-start.9 = (f32[20]{0:T(128)S(1)}, f32[20]{0:T(128)}, u32[]{:S(2)}) copy-start(f32[20]{0:T(128)} %constant.159) | copy-start | bytes 244
  0.1 27.6 %copy-start.10 = (f32[20]{0:T(128)S(1)}, f32[20]{0:T(128)}, u32[]{:S(2)}) copy-start(f32[20]{0:T(128)} %constant.157) | copy-start | bytes 244
  0.1 27.6 %copy-start.11 = (f32[20]{0:T(128)S(1)}, f32[20]{0:T(128)}, u32[]{:S(2)}) copy-start(f32[20]{0:T(128)} %constant.155) | copy-start | bytes 244
  0.1 27.6 %copy-start.12 = (f32[20]{0:T(128)S(1)}, f32[20]{0:T(128)}, u32[]{:S(2)}) copy-start(f32[20]{0:T(128)} %constant.153) | copy-start | bytes 244
  0.1 27.6 %copy-start.13 = (f32[20]{0:T(128)S(1)}, f32[20]{0:T(128)}, u32[]{:S(2)}) copy-start(f32[20]{0:T(128)} %constant.151) | copy-start | bytes 244
  0.1 27.6 %copy-start.14 = (f32[20]{0:T(128)S(1)}, f32[20]{0:T(128)}, u32[]{:S(2)}) copy-start(f32[20]{0:T(128)} %constant.149) | copy-start | bytes 244
  0.1 27.6 %copy-start.15 = (f32[20]{0:T(128)S(1)}, f32[20]{0:T(128)}, u32[]{:S(2)}) copy-start(f32[20]{0:T(128)} %constant.147) | copy-start | bytes 244
  0.1 27.6 %copy-start.16 = (f32[20]{0:T(128)S(1)}, f32[20]{0:T(128)}, u32[]{:S(2)}) copy-start(f32[20]{0:T(128)} %constant.145) | copy-start | bytes 244
  0.2 27.6 %copy-start.17 = (f32[20]{0:T(128)S(1)}, f32[20]{0:T(128)}, u32[]{:S(2)}) copy-start(f32[20]{0:T(128)} %constant.143) | copy-start | bytes 244
  0.2 27.6 %copy-start.18 = (f32[20]{0:T(128)S(1)}, f32[20]{0:T(128)}, u32[]{:S(2)}) copy-start(f32[20]{0:T(128)} %constant.141) | copy-start | bytes 244
  2.0 40.6 %collective-permute-start.1 = (bf16[2000]{0:T(1024)(128)(2,1)S(1)}, bf16[2000]{0:T(1024)(128)(2,1)S(1)}, u32[]{:S(2)}, u32[]{:S(2)}) collective-permute-start(bf16[2000]{0:T(1024)(128)(2,1)S(1)} %get-tuple-element.9), channel_id=1, source_target_pairs={{1,0},{2,1},{3,2},{4,3},{5,4},{6,5},{7,6},{8,7},{9,8},{10,9},{11,1... | collective-permute-start | bytes 12008 | tf_op jit(solution)/shard_map/ppermute | solution.py:62
  5.3 37.3 %collective-permute-start = (bf16[2000]{0:T(1024)(128)(2,1)S(1)}, bf16[2000]{0:T(1024)(128)(2,1)S(1)}, u32[]{:S(2)}, u32[]{:S(2)}) collective-permute-start(bf16[2000]{0:T(1024)(128)(2,1)S(1)} %get-tuple-element.10), channel_id=1, source_target_pairs={{0,1},{1,2},{2,3},{3,4},{4,5},{5,6},{6,7},{7,8},{8,9},{9,10},{10,1... | collective-permute-start | bytes 12008 | tf_op jit(solution)/shard_map/ppermute | solution.py:61
  10.8 42.3 %all-to-all-start = ((bf16[32,128,22]{1,2,0:T(8,128)(2,1)}), bf16[32,128,22]{1,2,0:T(8,128)(2,1)S(1)}, u32[]{:S(2)}, u32[]{:S(2)}) async-start(bf16[32,128,22]{1,2,0:T(8,128)(2,1)} %broadcast_in_dim.21), calls=%async_computation | async-start | bytes 393216 | tf_op jit(solution)/shard_map/all_to_all | solution.py:287
  42.0 2.6 %copy-start.19 = (f32[20]{0:T(128)S(1)}, f32[20]{0:T(128)}, u32[]{:S(2)}) copy-start(f32[20]{0:T(128)} %constant.141) | copy-start | bytes 244
  43.4 6.3 %collective-permute-start.2 = (f32[20,2048]{1,0:T(8,128)S(1)}, f32[20,2048]{1,0:T(8,128)S(1)}, u32[]{:S(2)}, u32[]{:S(2)}) collective-permute-start(f32[20,2048]{1,0:T(8,128)S(1)} %fusion.41), channel_id=1, source_target_pairs={{0,32},{32,0},{64,96},{96,64},{1,33},{33,1},{65,97},{97,65},{2,34}... | collective-permute-start | bytes 491528 | tf_op jit(solution)/shard_map/ppermute | solution.py:267
  50.4 15.6 %collective-permute-start.3 = (f32[20,2048]{1,0:T(8,128)}, f32[20,2048]{1,0:T(8,128)}, u32[]{:S(2)}, u32[]{:S(2)}) collective-permute-start(f32[20,2048]{1,0:T(8,128)} %add.540), channel_id=1, source_target_pairs={{0,64},{32,96},{64,0},{96,32},{1,65},{33,97},{65,1},{97,33},{2,66}... | collective-permute-start | bytes 491528 | tf_op jit(solution)/shard_map/ppermute | solution.py:267
  59.0 2.9 %copy-start = (bf16[2000,20]{1,0:T(8,128)(2,1)S(1)}, bf16[2000,20]{1,0:T(8,128)(2,1)}, u32[]{:S(2)}) copy-start(bf16[2000,20]{1,0:T(8,128)(2,1)} %fusion.18) | copy-start | bytes 240004
  61.6 3.5 %collective-permute-start.4 = (bf16[21,2048]{1,0:T(8,128)(2,1)S(1)}, bf16[21,2048]{1,0:T(8,128)(2,1)S(1)}, u32[]{:S(2)}, u32[]{:S(2)}) collective-permute-start(bf16[21,2048]{1,0:T(8,128)(2,1)S(1)} %bitcast.77), channel_id=1, source_target_pairs={{0,32},{32,0},{64,96},{96,64},{1,33},{33,1},{65,97},{97,65},{2,34}... | collective-permute-start | bytes 258056 | tf_op jit(solution)/shard_map/ppermute | solution.py:267
  65.1 5.2 %collective-permute-start.5 = (bf16[21,2048]{1,0:T(8,128)(2,1)S(1)}, bf16[21,2048]{1,0:T(8,128)(2,1)S(1)}, u32[]{:S(2)}, u32[]{:S(2)}) collective-permute-start(bf16[21,2048]{1,0:T(8,128)(2,1)S(1)} %add.581), channel_id=1, source_target_pairs={{0,64},{32,96},{64,0},{96,32},{1,65},{33,97},{65,1},{97,33},{2,66}... | collective-permute-start | bytes 258056 | tf_op jit(solution)/shard_map/ppermute | solution.py:267
  67.2 16.9 %copy-start.1 = (f32[2048]{0:T(1024)S(1)}, f32[2048]{0:T(1024)}, u32[]{:S(2)}) copy-start(f32[2048]{0:T(1024)} %param.25) | copy-start | bytes 24580
  73.4 17.9 %all-to-all-start.1 = ((bf16[32,2,160]{2,1,0:T(2,128)(2,1)}), bf16[32,2,160]{2,1,0:T(2,128)(2,1)S(1)}, u32[]{:S(2)}, u32[]{:S(2)}) async-start(bf16[32,2,160]{2,1,0:T(2,128)(2,1)} %reshape.790), calls=%async_computation.1 | async-start | bytes 65536 | tf_op jit(solution)/shard_map/all_to_all | solution.py:334
